TPU v7x, 512 devices: a whole 4x8x8 slice. The times are simulated.
512 devices in a mesh: rows: 128 (over z, y, core), blk: 4 (over x).
Axes of the slice: x: 4, y: 8, z: 8, core: 2. Of those that a mesh axis runs over, the one named last changes fastest.
Arguments:
- vectors: bfloat16 [64, 131072], P('blk', 'rows'), may hold values from -40 to 40
- hamiltonian: bfloat16 [2048, 64, 8704], P('rows', None, 'blk'), may hold values from -0.078125 to 0.078125
- column_index: int32 [2048, 136], P('rows', 'blk'), may hold values from 0 to 2047, as said below
- counts: int32 [2048], P('rows'), may hold values from 1 to 129, as said below
Outputs:
- basis: float32 [64, 131072], P('blk', 'rows')
- factor: float32 [64, 64], replicated
Inputs may be any that keep to these rules, and one draw needn't show every extreme that they name: `column_index`: entry I, s for s < counts[I] is (I + d) mod 2048 for offsets -64 <= d <= 64 that are distinct within a row and listed in rising order; slots past the count hold I. Every row counts its own block; some row uses all 129 offsets.
All inputs are finite; a program needn't handle non-finite values.
Results may differ from a plain program's by a relative error of at most 0.018.
Values may be sent and summed in bfloat16 or wider, within the bound.
No kernel may reach another device: no remote copies, remote signals or barrier semaphores. Data moves between devices by JAX's collectives and lax.ppermute only.
A program may use at most 64 MiB of HBM per device.

v0:
```python
import jax
import jax.numpy as jnp
from jax import lax
from jax.sharding import PartitionSpec as P

HW = 64


def from_behind(value, axis, by):
    devices = lax.axis_size(axis)
    return lax.ppermute(value, axis, [(i, (i + by) % devices) for i in range(devices)])


def body(vectors, hamiltonian, column_index, counts):
    block_rows = counts.shape[0]
    block_width = hamiltonian.shape[1]
    slots_here = column_index.shape[1]
    panel_rows = vectors.shape[0]
    total_blocks = block_rows * lax.axis_size("rows")
    spread_devs = HW // block_rows
    first_block = lax.axis_index("rows") * block_rows
    slot_base = lax.axis_index("blk") * slots_here
    window_slot = (column_index - first_block + HW) % total_blocks
    slot_ids = slot_base + jnp.arange(slots_here, dtype=jnp.int32)
    live_slot = (slot_ids[None, :] < counts[:, None]).astype(jnp.bfloat16)
    ham_tiles = hamiltonian.reshape(block_rows, block_width, slots_here, block_width)

    def window(panel_in):
        lower_parts = [
            from_behind(panel_in, "rows", distance) for distance in range(spread_devs, 0, -1)
        ]
        upper_parts = [
            from_behind(panel_in, "rows", -distance) for distance in range(1, spread_devs + 1)
        ]
        return jnp.concatenate(lower_parts + [panel_in] + upper_parts, axis=1)

    def widened(panel_in):
        return window(lax.all_gather(panel_in, "blk", axis=0, tiled=True))

    def products(extended):
        blocks = extended.reshape(extended.shape[0], block_rows + 2 * HW, block_width)
        picked = jnp.take(blocks, window_slot, axis=1) * live_slot[None, :, :, None]
        result = jnp.einsum("vrsk,risk->vri", picked, ham_tiles, preferred_element_type=jnp.float32)
        return result.reshape(extended.shape[0], block_rows * block_width)

    start_window = widened(vectors)
    whole_vectors = start_window[:, HW * block_width : (HW + block_rows) * block_width]
    partial_one = products(start_window)
    first_panel = lax.psum_scatter(
        partial_one.astype(jnp.bfloat16), "blk", scatter_dimension=0, tiled=True
    )
    next_window = widened(first_panel)
    partial_two = products(next_window)
    summed_two = lax.psum(partial_two.astype(jnp.bfloat16), "blk").astype(jnp.float32)
    filtered = (2.0 * summed_two - whole_vectors.astype(jnp.float32)).astype(jnp.bfloat16)
    local_gram = jnp.einsum("vi,wi->vw", filtered, filtered, preferred_element_type=jnp.float32)
    gram_matrix = lax.psum(local_gram, "rows") / float(total_blocks * block_width)
    lower_factor = jnp.linalg.cholesky(gram_matrix)
    solved = lax.linalg.triangular_solve(
        lower_factor, filtered.astype(jnp.float32), left_side=True, lower=True
    )
    basis = lax.dynamic_slice_in_dim(solved, lax.axis_index("blk") * panel_rows, panel_rows, 0)
    return (basis, lower_factor.T)


def solution(mesh):
    in_specs = (P("blk", "rows"), P("rows", None, "blk"), P("rows", "blk"), P("rows"))
    out_specs = (P("blk", "rows"), P())
    return jax.shard_map(body, mesh=mesh, in_specs=in_specs, out_specs=out_specs, check_vma=False)
```

profile of v0, /device:TPU:1, one launch (start us, length us, event | category | flops | bytes accessed | tf_op | source)
XLA Modules:
  0.0 769.6 jit_solution(3885378505090221152)
XLA Ops:
  7.2 10.5 %all_gather.6 = bf16[64,1024]{1,0:T(8,128)(2,1)S(1)} all-gather(bf16[16,1024]{1,0:T(8,128)(2,1)} %param.6), channel_id=1, replica_groups=mesh['rows'=128,'blk'=4] {'blk'}, dimensions={0}, use_global_device_ids=true | all-gather | bytes 163840 | tf_op jit(solution)/shard_map/all_gather | solution.py:38
  17.7 14.4 %collective-permute-start.7 = (bf16[64,1024]{1,0:T(8,128)(2,1)S(1)}, bf16[64,1024]{1,0:T(8,128)(2,1)S(1)}, u32[]{:S(2)}, u32[]{:S(2)}) collective-permute-start(bf16[64,1024]{1,0:T(8,128)(2,1)S(1)} %all_gather.6), channel_id=1, source_target_pairs={{0,496},{4,500},{8,504},{12,508},{16,0},{20,4},{24,8},{28,12},{32,... | collective-permute-start | bytes 393224 | tf_op jit(solution)/shard_map/ppermute | solution.py:11
  32.1 6.7 collective-permute-start.6
  38.8 3.0 collective-permute-start.5
  41.7 1.9 collective-permute-start.1
  43.7 2.4 collective-permute-start
  46.1 0.8 compare_and_fusion
  46.9 0.1 reshape.89
  47.0 13.9 %reshape.67 = bf16[16,64,34,64]{3,2,1,0:T(8,128)(2,1)} reshape(bf16[16,64,2176]{2,1,0:T(8,128)(2,1)} %param.7) | data formatting | bytes 8912896 | tf_op jit(solution)/shard_map/reshape | solution.py:26
  61.0 2.3 collective-permute-start.2
  63.3 2.8 collective-permute-start.3
  66.1 3.9 collective-permute-done.2
  70.0 4.1 collective-permute-start.4
  74.2 2.1 collective-permute-done.4
  76.3 2.6 reshape.66
  78.9 2.3 copy.12
  81.2 18.1 %gather_fusion = bf16[544,64,64]{2,1,0:T(8,128)(2,1)} fusion(bf16[64,144,64]{2,0,1:T(8,128)(2,1)S(1)} %copy.12, s32[1024]{0:T(1024)S(1)} %pad_clamp_fusion), kind=kCustom, calls=%fused_computation.clone | custom fusion | bytes 8915072 | tf_op jit(solution)/shard_map/jit(_take)/gather | solution.py:42
  99.3 8.1 %fusion.24 = bf16[64,16,64]{2,0,1:T(8,128)(2,1)S(1)} fusion(bf16[16,64,34,64]{3,2,1,0:T(8,128)(2,1)} %reshape.67, bf16[16,34,64,64]{3,2,1,0:T(8,128)(2,1)} %bitcast.50, pred[16,34]{1,0:T(8,128)(4,1)S(1)} %get-tuple-element.7, bf16[16,34]{1,0:T(8,128)(2,1)S(1)} %get-tuple-element.11), kind=kOutput, calls=%fused_computation.20 | convolution fusion | flops 289734656 | bytes 9045600 | tf_op jit(solution)/shard_map/vrsk,risk->vri/dot_general | solution.py:43
  107.4 0.2 copy.14
  107.6 0.9 convert_element_type.38
  108.5 18.5 %reduce-scatter.2.cloned.1.call-done = bf16[16,1024]{1,0:T(8,128)(2,1)} async-done(((bf16[64,1024]{1,0:T(8,128)(2,1)}), bf16[16,1024]{1,0:T(8,128)(2,1)}) %reduce-scatter.2.cloned.1.call-update) | async-done | bytes 32784 | tf_op jit(solution)/shard_map/reduce_scatter | solution.py:49
  127.0 9.3 %all_gather.7 = bf16[64,1024]{1,0:T(8,128)(2,1)S(1)} all-gather(bf16[16,1024]{1,0:T(8,128)(2,1)} %reduce-scatter.2.cloned.1.call-done), channel_id=1, replica_groups=mesh['rows'=128,'blk'=4] {'blk'}, dimensions={0}, use_global_device_ids=true | all-gather | bytes 163840 | tf_op jit(solution)/shard_map/all_gather | solution.py:38
  136.3 4.0 collective-permute-start.8
  140.3 11.3 %collective-permute-start.9 = (bf16[64,1024]{1,0:T(8,128)(2,1)S(1)}, bf16[64,1024]{1,0:T(8,128)(2,1)S(1)}, u32[]{:S(2)}, u32[]{:S(2)}) collective-permute-start(bf16[64,1024]{1,0:T(8,128)(2,1)S(1)} %all_gather.7), channel_id=1, source_target_pairs={{0,12},{4,16},{8,20},{12,24},{16,28},{20,32},{24,36},{28,40},{32,4... | collective-permute-start | bytes 393224 | tf_op jit(solution)/shard_map/ppermute | solution.py:11
  151.6 4.2 collective-permute-start.15
  155.8 2.7 collective-permute-start.14
  158.5 3.1 collective-permute-start.13
  161.6 2.2 collective-permute-start.10
  163.9 3.4 collective-permute-start.11
  167.3 3.4 collective-permute-done.10
  170.7 6.0 collective-permute-start.12
  176.7 0.7 collective-permute-done.12
  177.6 2.6 reshape.68
  180.1 2.3 copy.15
  182.4 18.1 %gather_fusion.1 = bf16[544,64,64]{2,1,0:T(8,128)(2,1)} fusion(bf16[64,144,64]{2,0,1:T(8,128)(2,1)S(1)} %copy.15, s32[1024]{0:T(1024)S(1)} %pad_clamp_fusion), kind=kCustom, calls=%fused_computation.1.clone | custom fusion | bytes 8915072 | tf_op jit(solution)/shard_map/jit(_take)/gather | solution.py:42
  200.5 8.1 %fusion.27 = bf16[64,16,64]{2,0,1:T(8,128)(2,1)S(1)} fusion(bf16[16,64,34,64]{3,2,1,0:T(8,128)(2,1)} %reshape.67, bf16[16,34,64,64]{3,2,1,0:T(8,128)(2,1)} %bitcast.49, pred[16,34]{1,0:T(8,128)(4,1)S(1)} %get-tuple-element.7, bf16[16,34]{1,0:T(8,128)(2,1)S(1)} %get-tuple-element.11), kind=kOutput, calls=%fused_computation.21 | convolution fusion | flops 289734656 | bytes 9045600 | tf_op jit(solution)/shard_map/vrsk,risk->vri/dot_general | solution.py:43
  208.6 0.2 copy.17
  208.8 0.9 convert_element_type.41
  209.7 45.7 %all-reduce.2.cloned.1.call-done = bf16[64,1024]{1,0:T(8,128)(2,1)} async-done(((bf16[64,1024]{1,0:T(8,128)(2,1)}), bf16[64,1024]{1,0:T(8,128)(2,1)}) %all-reduce.2.cloned.1.call-update) | async-done | bytes 131088 | tf_op jit(solution)/shard_map/psum | solution.py:54
  255.3 1.2 fusion.31
  256.5 491.5 %psum.15 = f32[64,64]{0,1:T(8,128)S(1)} all-reduce(f32[64,64]{0,1:T(8,128)S(1)} %fusion.31), channel_id=1, replica_groups=mesh['rows'=128,'blk'=4] {'rows'}, use_global_device_ids=true, to_apply=%region_2.4 | all-reduce | flops 4096 | bytes 32768 | tf_op jit(solution)/shard_map/psum | solution.py:57
  748.1 5.8 cholesky.16
  754.0 0.6 compare_reduce_fusion
  754.7 0.7 fusion.34
  755.3 0.7 copy.20
  756.0 4.9 custom-call.6
  760.9 1.2 fusion.30
  762.1 0.6 constant_dynamic-slice_fusion
  (40 shorter events, 0.5 us)
Async XLA Ops:
  7.2 119.8 %reduce-scatter.2.cloned.1.call-start = ((), (), s32[]{:S(2)}) async-start(), calls=%async_computation.1 | async-start | bytes 163840 | tf_op jit(solution)/shard_map/reduce_scatter | solution.py:49
  17.7 58.6 %collective-permute-start.7 = (bf16[64,1024]{1,0:T(8,128)(2,1)S(1)}, bf16[64,1024]{1,0:T(8,128)(2,1)S(1)}, u32[]{:S(2)}, u32[]{:S(2)}) collective-permute-start(bf16[64,1024]{1,0:T(8,128)(2,1)S(1)} %all_gather.6), channel_id=1, source_target_pairs={{0,496},{4,500},{8,504},{12,508},{16,0},{20,4},{24,8},{28,12},{32,... | collective-permute-start | bytes 393224 | tf_op jit(solution)/shard_map/ppermute | solution.py:11
  32.1 44.2 %collective-permute-start.6 = (bf16[64,1024]{1,0:T(8,128)(2,1)S(1)}, bf16[64,1024]{1,0:T(8,128)(2,1)S(1)}, u32[]{:S(2)}, u32[]{:S(2)}) collective-permute-start(bf16[64,1024]{1,0:T(8,128)(2,1)S(1)} %all_gather.6), channel_id=1, source_target_pairs={{0,500},{4,504},{8,508},{12,0},{16,4},{20,8},{24,12},{28,16},{32,2... | collective-permute-start | bytes 393224 | tf_op jit(solution)/shard_map/ppermute | solution.py:11
  38.8 37.5 %collective-permute-start.5 = (bf16[64,1024]{1,0:T(8,128)(2,1)S(1)}, bf16[64,1024]{1,0:T(8,128)(2,1)S(1)}, u32[]{:S(2)}, u32[]{:S(2)}) collective-permute-start(bf16[64,1024]{1,0:T(8,128)(2,1)S(1)} %all_gather.6), channel_id=1, source_target_pairs={{0,504},{4,508},{8,0},{12,4},{16,8},{20,12},{24,16},{28,20},{32,24... | collective-permute-start | bytes 393224 | tf_op jit(solution)/shard_map/ppermute | solution.py:11
  41.7 21.5 %collective-permute-start.1 = (bf16[64,1024]{1,0:T(8,128)(2,1)S(1)}, bf16[64,1024]{1,0:T(8,128)(2,1)S(1)}, u32[]{:S(2)}, u32[]{:S(2)}) collective-permute-start(bf16[64,1024]{1,0:T(8,128)(2,1)S(1)} %all_gather.6), channel_id=1, source_target_pairs={{0,12},{4,16},{8,20},{12,24},{16,28},{20,32},{24,36},{28,40},{32,4... | collective-permute-start | bytes 393224 | tf_op jit(solution)/shard_map/ppermute | solution.py:11
  43.7 17.3 %collective-permute-start = (bf16[64,1024]{1,0:T(8,128)(2,1)S(1)}, bf16[64,1024]{1,0:T(8,128)(2,1)S(1)}, u32[]{:S(2)}, u32[]{:S(2)}) collective-permute-start(bf16[64,1024]{1,0:T(8,128)(2,1)S(1)} %all_gather.6), channel_id=1, source_target_pairs={{0,16},{4,20},{8,24},{12,28},{16,32},{20,36},{24,40},{28,44},{32,4... | collective-permute-start | bytes 393224 | tf_op jit(solution)/shard_map/ppermute | solution.py:11
  61.0 9.0 %collective-permute-start.2 = (bf16[64,1024]{1,0:T(8,128)(2,1)S(1)}, bf16[64,1024]{1,0:T(8,128)(2,1)S(1)}, u32[]{:S(2)}, u32[]{:S(2)}) collective-permute-start(bf16[64,1024]{1,0:T(8,128)(2,1)S(1)} %all_gather.6), channel_id=1, source_target_pairs={{0,8},{4,12},{8,16},{12,20},{16,24},{20,28},{24,32},{28,36},{32,40... | collective-permute-start | bytes 393224 | tf_op jit(solution)/shard_map/ppermute | solution.py:11
  63.3 10.8 %collective-permute-start.3 = (bf16[64,1024]{1,0:T(8,128)(2,1)S(1)}, bf16[64,1024]{1,0:T(8,128)(2,1)S(1)}, u32[]{:S(2)}, u32[]{:S(2)}) collective-permute-start(bf16[64,1024]{1,0:T(8,128)(2,1)S(1)} %all_gather.6), channel_id=1, source_target_pairs={{0,4},{4,8},{8,12},{12,16},{16,20},{20,24},{24,28},{28,32},{32,36}... | collective-permute-start | bytes 393224 | tf_op jit(solution)/shard_map/ppermute | solution.py:11
  70.0 6.3 collective-permute-start.4
  108.5 146.9 %all-reduce.2.cloned.1.call-start = ((), (), s32[]{:S(2)}) async-start(), calls=%async_computation.2 | async-start | bytes 262144 | tf_op jit(solution)/shard_map/psum | solution.py:54
  136.3 25.3 %collective-permute-start.8 = (bf16[64,1024]{1,0:T(8,128)(2,1)S(1)}, bf16[64,1024]{1,0:T(8,128)(2,1)S(1)}, u32[]{:S(2)}, u32[]{:S(2)}) collective-permute-start(bf16[64,1024]{1,0:T(8,128)(2,1)S(1)} %all_gather.7), channel_id=1, source_target_pairs={{0,16},{4,20},{8,24},{12,28},{16,32},{20,36},{24,40},{28,44},{32,4... | collective-permute-start | bytes 393224 | tf_op jit(solution)/shard_map/ppermute | solution.py:11
  140.3 23.5 %collective-permute-start.9 = (bf16[64,1024]{1,0:T(8,128)(2,1)S(1)}, bf16[64,1024]{1,0:T(8,128)(2,1)S(1)}, u32[]{:S(2)}, u32[]{:S(2)}) collective-permute-start(bf16[64,1024]{1,0:T(8,128)(2,1)S(1)} %all_gather.7), channel_id=1, source_target_pairs={{0,12},{4,16},{8,20},{12,24},{16,28},{20,32},{24,36},{28,40},{32,4... | collective-permute-start | bytes 393224 | tf_op jit(solution)/shard_map/ppermute | solution.py:11
  151.6 26.0 %collective-permute-start.15 = (bf16[64,1024]{1,0:T(8,128)(2,1)S(1)}, bf16[64,1024]{1,0:T(8,128)(2,1)S(1)}, u32[]{:S(2)}, u32[]{:S(2)}) collective-permute-start(bf16[64,1024]{1,0:T(8,128)(2,1)S(1)} %all_gather.7), channel_id=1, source_target_pairs={{0,496},{4,500},{8,504},{12,508},{16,0},{20,4},{24,8},{28,12},{32,... | collective-permute-start | bytes 393224 | tf_op jit(solution)/shard_map/ppermute | solution.py:11
  155.8 21.7 %collective-permute-start.14 = (bf16[64,1024]{1,0:T(8,128)(2,1)S(1)}, bf16[64,1024]{1,0:T(8,128)(2,1)S(1)}, u32[]{:S(2)}, u32[]{:S(2)}) collective-permute-start(bf16[64,1024]{1,0:T(8,128)(2,1)S(1)} %all_gather.7), channel_id=1, source_target_pairs={{0,500},{4,504},{8,508},{12,0},{16,4},{20,8},{24,12},{28,16},{32,2... | collective-permute-start | bytes 393224 | tf_op jit(solution)/shard_map/ppermute | solution.py:11
  158.5 19.0 %collective-permute-start.13 = (bf16[64,1024]{1,0:T(8,128)(2,1)S(1)}, bf16[64,1024]{1,0:T(8,128)(2,1)S(1)}, u32[]{:S(2)}, u32[]{:S(2)}) collective-permute-start(bf16[64,1024]{1,0:T(8,128)(2,1)S(1)} %all_gather.7), channel_id=1, source_target_pairs={{0,504},{4,508},{8,0},{12,4},{16,8},{20,12},{24,16},{28,20},{32,24... | collective-permute-start | bytes 393224 | tf_op jit(solution)/shard_map/ppermute | solution.py:11
  161.6 9.0 %collective-permute-start.10 = (bf16[64,1024]{1,0:T(8,128)(2,1)S(1)}, bf16[64,1024]{1,0:T(8,128)(2,1)S(1)}, u32[]{:S(2)}, u32[]{:S(2)}) collective-permute-start(bf16[64,1024]{1,0:T(8,128)(2,1)S(1)} %all_gather.7), channel_id=1, source_target_pairs={{0,8},{4,12},{8,16},{12,20},{16,24},{20,28},{24,32},{28,36},{32,40... | collective-permute-start | bytes 393224 | tf_op jit(solution)/shard_map/ppermute | solution.py:11
  163.9 12.9 %collective-permute-start.11 = (bf16[64,1024]{1,0:T(8,128)(2,1)S(1)}, bf16[64,1024]{1,0:T(8,128)(2,1)S(1)}, u32[]{:S(2)}, u32[]{:S(2)}) collective-permute-start(bf16[64,1024]{1,0:T(8,128)(2,1)S(1)} %all_gather.7), channel_id=1, source_target_pairs={{0,4},{4,8},{8,12},{12,16},{16,20},{20,24},{24,28},{28,32},{32,36}... | collective-permute-start | bytes 393224 | tf_op jit(solution)/shard_map/ppermute | solution.py:11
  170.7 6.8 collective-permute-start.12
Sparse Core Ops, SparseCore 0:
  108.6 18.3 reduce-scatter.1
  209.8 45.4 all-reduce.1
where the time goes:
time: 774 us; the launch traced here: 770 us
  blocking collectives  511 us (66%)
  starting transfers between devices  74.5 us (10%)
  waiting for transfers between devices  74.2 us (10%)
  local copies, waits for them, and re-layouts  63.5 us (8%)
  matrix products  18.6 us (2%)
  between operations  14.5 us (2%)
  other arithmetic  12.9 us (2%)
    psum x1, blocking collectives, body(): lax.psum(local_gram, 'rows') / float(total_blocks * block_width)  492 us
    ppermute x16, starting transfers between devices, from_behind(): lax.ppermute(value, axis, [(i, (i + by) % devices) for i in range(devices)])  74.5 us
    psum x1, waiting for transfers between devices, body(): lax.psum(partial_two.astype(jnp.bfloat16), 'blk').astype(jnp.float32)  45.7 us
    gather x2, local copies, waits for them, and re-layouts, products(): picked = jnp.take(blocks, window_slot, axis=1) * live_slot[None, :, :, None]  36.1 us
    all_gather x2, blocking collectives, widened(): return window(lax.all_gather(panel_in, 'blk', axis=0, tiled=True))  19.8 us
    reduce_scatter x1, waiting for transfers between devices, body(): lax.psum_scatter(partial_one.astype(jnp.bfloat16), 'blk', scatter_dimensi...  18.5 us
    dot_general x2, matrix products, products(): jnp.einsum('vrsk,risk->vri', picked, ham_tiles, preferred_element_type=jn...  16.2 us
  transfers between devices with their start and end apart: 18, of which 6 were waited for; matrix products, arithmetic and copies ran while one was open for 2% of the time, Pallas kernels for 0%

commit v1 on v0

v1 whole, which is shorter than its diff:
```python
import functools

import jax
import jax.numpy as jnp
from jax import lax
from jax.experimental import pallas as pl
from jax.experimental.pallas import tpu as pltpu
from jax.sharding import Mesh, PartitionSpec as P

HW = 64
ROWS = ("z", "y", "core")
F32 = jnp.float32
BF16 = jnp.bfloat16
VMEM_SPEC = pl.BlockSpec(memory_space=pltpu.VMEM)
SMEM_SPEC = pl.BlockSpec(memory_space=pltpu.SMEM)


def call(kernel, out_shape, in_specs, scratch=()):
    outs = jax.tree.map(lambda _: VMEM_SPEC, out_shape)
    return pl.pallas_call(
        kernel, out_shape=out_shape, in_specs=in_specs, out_specs=outs, scratch_shapes=scratch
    )


def shape(dims, dtype):
    return jax.ShapeDtypeStruct(dims, dtype)


def product_kernel(copies, index, *refs):
    pieces, (ham, out, tiles) = refs[:5], refs[5:]
    vecs = ham.shape[1]
    half = lax.broadcasted_iota(jnp.int32, (vecs, 128), 1) < 64
    for p, piece in enumerate(pieces):
        for u in range(2):
            base = 32 * p + 16 * u
            loaded = [piece[u, :, 128 * t : 128 * (t + 1)] for t in range(8)]
            for t in range(8):
                tiles[base + 2 * t] = loaded[t]
                tiles[base + 2 * t + 1] = jnp.concatenate(
                    [loaded[t][:, 64:], loaded[(t + 1) % 8][:, :64]], axis=1
                )
    tiles[160] = jnp.zeros((vecs, 128), BF16)
    pairs = ham.shape[2] // 128

    def two_rows(m, carry):
        sums = []
        for k in range(2):
            row = 2 * m + k
            picked = jnp.concatenate(
                [
                    jnp.where(half, tiles[index[row, 2 * s]], tiles[index[row, 2 * s + 1]])
                    for s in range(pairs)
                ],
                axis=1,
            )
            sums.append(
                lax.dot_general(
                    picked, ham[row], (((1,), (1,)), ((), ())), preferred_element_type=F32
                )
            )
        both = jnp.concatenate(sums, axis=1).astype(BF16)
        lanes = pl.ds(pl.multiple_of(m * 128, 128), 128)
        for c in range(copies):
            out[c, :, lanes] = both
        return carry

    lax.fori_loop(0, ham.shape[0] // 2, two_rows, 0)


def gram_kernel(core, parts, own, filtered, gram):
    total = parts[0].astype(F32)
    for b in range(1, 4):
        total += parts[b].astype(F32)
    value = (2.0 * total - own[core[0]].astype(F32)).astype(BF16)
    filtered[...] = value
    g = lax.dot_general(value, value, (((1,), (1,)), ((), ())), preferred_element_type=F32)
    packed = jnp.concatenate([g[:32], g[32:]], axis=1)
    for c in range(8):
        gram[c] = packed


def sum_kernel(parts, out):
    total = parts[0]
    for c in range(1, 8):
        total += parts[c]
    for c in range(out.shape[0]):
        out[c] = total


def factor_kernel(scale, blk, one, two, filtered, basis, factor, scratch):
    packed = (one[0] + two[0]) * scale
    lane = lax.broadcasted_iota(jnp.int32, (8, 128), 1)
    sub = lax.broadcasted_iota(jnp.int32, (8, 128), 0)
    chunks = []
    for c in range(8):
        rows = packed[8 * (c % 4) : 8 * (c % 4) + 8]
        if c >= 4:
            rows = jnp.concatenate([rows[:, 64:], rows[:, :64]], axis=1)
        eye = jnp.where(lane - 64 == sub + 8 * c, F32(1.0), F32(0.0))
        chunks.append(jnp.where(lane < 64, rows, eye))
    for k in range(64):
        ck, r = divmod(k, 8)
        row = chunks[ck][r : r + 1]
        inv = 1.0 / jnp.sqrt(row[:, k : k + 1])
        unit = row * inv
        for c in range(ck, 8):
            col = chunks[c][:, k : k + 1] * inv
            if c == ck:
                moved = jnp.where(sub > r, chunks[c] - col * unit, chunks[c])
                chunks[c] = jnp.where(sub == r, jnp.broadcast_to(unit, (8, 128)), moved)
            else:
                chunks[c] = chunks[c] - col * unit
    for c in range(8):
        keep = jnp.where(lane >= sub + 8 * c, chunks[c], F32(0.0))
        factor[8 * c : 8 * c + 8, :] = keep[:, :64]
        scratch[8 * c : 8 * c + 8, :] = chunks[c][:, 64:]
    mine = scratch[pl.ds(pl.multiple_of(blk[0] * 16, 16), 16), :]
    total = jnp.zeros(basis.shape, F32)
    rest = mine
    parts = []
    for _ in range(3):
        top = rest.astype(BF16)
        parts.append(top)
        rest = rest - top.astype(F32)
    for top in reversed(parts):
        total += jnp.dot(top, filtered[...], preferred_element_type=F32)
    basis[...] = total


def from_chip(value, distance):
    chips = lax.axis_size("z") * lax.axis_size("y")
    pairs = []
    for c in range(chips):
        pairs.append((2 * ((c - distance) % chips), 2 * c))
        pairs.append((2 * ((c + distance) % chips) + 1, 2 * c + 1))
    return lax.ppermute(value, ROWS, pairs)


def flip(value):
    return lax.ppermute(value, "core", [(0, 1), (1, 0)])


def window(pair):
    far = from_chip(pair, 2)
    near = from_chip(pair, 1)
    far_other = flip(far)
    near_other = flip(near)
    return far, near, pair, near_other, far_other


def to_all(value, axes, count):
    return lax.all_to_all(
        jnp.broadcast_to(value[None], (count,) + value.shape), axes, 0, 0, tiled=True
    )


def body(vectors, hamiltonian, column_index, counts):
    block_rows = counts.shape[0]
    width = hamiltonian.shape[1]
    slots_here = column_index.shape[1]
    vecs = width
    core = lax.axis_index("core")
    blk = lax.axis_index("blk")
    chip = lax.axis_index("z") * lax.axis_size("y") + lax.axis_index("y")
    total_blocks = block_rows * lax.axis_size(ROWS)

    offset = (column_index - (chip - 2) * 2 * block_rows) % total_blocks
    slot_ids = lax.broadcasted_iota(jnp.int32, column_index.shape, 1)
    live = slot_ids + blk * slots_here < counts[:, None]
    away, within = offset // 32, offset % 32
    place = jnp.where(core == 0, away, 4 - away) * 32 + (within // 16) * 16
    block = within % 16
    tile = place + jnp.where(slot_ids % 2 == 0, block, (block + 15) % 16)
    index = jnp.where(live, tile, 160)

    core_id = core.reshape(1).astype(jnp.int32)
    blk_id = blk.reshape(1).astype(jnp.int32)

    def products(pieces, copies):
        return call(
            functools.partial(product_kernel, copies),
            shape((copies, vecs, block_rows * width), BF16),
            [SMEM_SPEC] + [VMEM_SPEC] * 6,
            [pltpu.VMEM((161, vecs, 128), BF16)],
        )(index, *pieces, hamiltonian)

    pair = to_all(vectors, ("core", "blk"), 8).reshape(2, vecs, block_rows * width)
    parts = products(window(pair), 4)
    parts = lax.all_to_all(parts, "blk", 0, 0, tiled=True)
    first = jnp.sum(parts.astype(F32), axis=0).astype(BF16)
    other = flip(first)
    pair_two = jnp.where(core == 0, jnp.stack([first, other]), jnp.stack([other, first]))
    parts = products(window(pair_two), 4)
    parts = lax.all_to_all(parts, "blk", 0, 0, tiled=True)
    filtered, gram = call(
        gram_kernel,
        (shape((vecs, block_rows * width), BF16), shape((8, 32, 128), F32)),
        [SMEM_SPEC, VMEM_SPEC, VMEM_SPEC],
    )(core_id, parts, pair)
    gram = lax.all_to_all(gram, "y", 0, 0, tiled=True)
    gram = call(sum_kernel, shape((8, 32, 128), F32), [VMEM_SPEC])(gram)
    gram = lax.all_to_all(gram, "z", 0, 0, tiled=True)
    gram = call(sum_kernel, shape((1, 32, 128), F32), [VMEM_SPEC])(gram)
    basis, factor = call(
        functools.partial(factor_kernel, 1.0 / (total_blocks * width)),
        (shape(vectors.shape, F32), shape((vecs, vecs), F32)),
        [SMEM_SPEC] + [VMEM_SPEC] * 3,
        [pltpu.VMEM((vecs, vecs), F32)],
    )(blk_id, gram, flip(gram), filtered)
    return basis, factor


def solution(mesh):
    chips = mesh.shape["rows"] // 2
    y = 8
    fine = Mesh(
        mesh.devices.reshape(chips // y, y, 2, mesh.shape["blk"]), ("z", "y", "core", "blk")
    )
    in_specs = (P("blk", ROWS), P(ROWS, None, "blk"), P(ROWS, "blk"), P(ROWS))
    out_specs = (P("blk", ROWS), P())
    return jax.shard_map(body, mesh=fine, in_specs=in_specs, out_specs=out_specs, check_vma=False)
```

time: 774 us -> 155 us (0.20)
  blocking collectives: 511 us -> 66.1 us
  waiting for transfers between devices: 74.2 us -> 6.58 us
  local copies, waits for them, and re-layouts: 63.5 us -> 3.47 us
  Pallas kernels: 0 us -> 27.6 us
  starting transfers between devices: 74.5 us -> 48 us
  matrix products: 18.6 us -> 0 us
  between operations: 14.5 us -> 0.85 us
  other arithmetic: 12.9 us -> 1.5 us
    psum x1 -> x0, blocking collectives: 492 us -> none  [body(): lax.psum(local_gram, 'rows') / float(total_blocks * block_width)]
    all_to_all x0 -> x5, blocking collectives: none -> 66.1 us  [the longest x2 26.1 us: body(): parts = lax.all_to_all(parts, 'blk', 0, 0, tiled=True)]
    psum x1 -> x0, waiting for transfers between devices: 45.7 us -> none  [body(): lax.psum(partial_two.astype(jnp.bfloat16), 'blk').astype(jnp.float32)]
    gather x2 -> x0, local copies, waits for them, and re-layouts: 36.1 us -> none  [products(): picked = jnp.take(blocks, window_slot, axis=1) * live_slot[None, :, :, None]]
    pallas_call x0 -> x6, Pallas kernels: none -> 27.6 us  [the longest x2 14.3 us: products(): call(functools.partial(product_kernel, copies), shape((copies, vecs, bloc...]
    ppermute x16 -> x10, starting transfers between devices: 74.5 us -> 48 us  [the longest x6 24.5 us: flip(): return lax.ppermute(value, 'core', [(0, 1), (1, 0)])]
    reshape x5 -> x0, local copies, waits for them, and re-layouts: 23.6 us -> none  [the longest x1 13.9 us: body(): hamiltonian.reshape(block_rows, block_width, slots_here, block_width)]
    all_gather x2 -> x0, blocking collectives: 19.8 us -> none  [widened(): return window(lax.all_gather(panel_in, 'blk', axis=0, tiled=True))]
  transfers between devices with their start and end apart: 18 -> 10, of which waited for: 6 -> 6; matrix products, arithmetic and copies ran while one was open for 2% -> 1% of each run, Pallas kernels for 0% -> 0%
where the time goes in v1:
time: 155 us; the launch traced here: 154 us
  blocking collectives  66.1 us (43%)
  starting transfers between devices  48 us (31%)
  Pallas kernels  27.6 us (18%)
  waiting for transfers between devices  6.58 us (4%)
  local copies, waits for them, and re-layouts  3.47 us (2%)
    all_to_all x2, blocking collectives, body(): parts = lax.all_to_all(parts, 'blk', 0, 0, tiled=True)  26.1 us
    ppermute x6, starting transfers between devices, flip(): return lax.ppermute(value, 'core', [(0, 1), (1, 0)])  24.5 us
    ppermute x4, starting transfers between devices, from_chip(): return lax.ppermute(value, ROWS, pairs)  23.5 us
    all_to_all x1, blocking collectives, to_all(): lax.all_to_all(jnp.broadcast_to(value[None], (count,) + value.shape), axe...  15.8 us
    pallas_call x2, Pallas kernels, products(): call(functools.partial(product_kernel, copies), shape((copies, vecs, bloc...  14.3 us
    all_to_all x1, blocking collectives, body(): gram = lax.all_to_all(gram, 'z', 0, 0, tiled=True)  12.3 us
    all_to_all x1, blocking collectives, body(): gram = lax.all_to_all(gram, 'y', 0, 0, tiled=True)  11.9 us
    pallas_call x1, Pallas kernels, body(): call(functools.partial(factor_kernel, 1.0 / (total_blocks * width)), (sha...  8.01 us
  transfers between devices with their start and end apart: 10, of which 6 were waited for; matrix products, arithmetic and copies ran while one was open for 1% of the time, Pallas kernels for 0%

profile of v1, /device:TPU:1, one launch (start us, length us, event | category | flops | bytes accessed | tf_op | source)
XLA Modules:
  0.0 154.1 jit_solution(17244117569801898112)
XLA Ops:
  0.6 0.8 broadcast_in_dim.12
  1.4 15.8 %all_to_all.25 = bf16[8,16,1024]{2,1,0:T(8,128)(2,1)S(1)} all-to-all(bf16[8,16,1024]{2,1,0:T(8,128)(2,1)S(1)} %broadcast_in_dim.12), channel_id=1, replica_groups=mesh['z'=8,'y'=8,'core'=2,'blk'=4] {'core','blk'}, dimensions={0} | all-to-all | bytes 524288 | tf_op jit(solution)/shard_map/all_to_all | solution.py:152
  17.2 9.9 %collective-permute-start.1 = (bf16[2,64,1024]{2,1,0:T(8,128)(2,1)S(1)}, bf16[2,64,1024]{2,1,0:T(8,128)(2,1)S(1)}, u32[]{:S(2)}, u32[]{:S(2)}) collective-permute-start(bf16[2,64,1024]{2,1,0:T(8,128)(2,1)S(1)} %bitcast.5), channel_id=1, source_target_pairs={{504,0},{12,4},{0,8},{20,12},{8,16},{28,20},{16,24},{36,28},{24,32... | collective-permute-start | bytes 786440 | tf_op jit(solution)/shard_map/ppermute | solution.py:136
  27.1 3.8 %collective-permute-start = (bf16[2,64,1024]{2,1,0:T(8,128)(2,1)S(1)}, bf16[2,64,1024]{2,1,0:T(8,128)(2,1)S(1)}, u32[]{:S(2)}, u32[]{:S(2)}) collective-permute-start(bf16[2,64,1024]{2,1,0:T(8,128)(2,1)S(1)} %bitcast.6), channel_id=1, source_target_pairs={{496,0},{20,4},{504,8},{28,12},{0,16},{36,20},{8,24},{44,28},{16,3... | collective-permute-start | bytes 786440 | tf_op jit(solution)/shard_map/ppermute | solution.py:136
  30.9 0.0 collective-permute-done.1.refs_1_
  30.9 0.0 copy-start.2
  30.9 3.0 %collective-permute-start.2 = (bf16[2,64,1024]{2,1,0:T(8,128)(2,1)S(1)}, bf16[2,64,1024]{2,1,0:T(8,128)(2,1)S(1)}, u32[]{:S(2)}, u32[]{:S(2)}) collective-permute-start(bf16[2,64,1024]{2,1,0:T(8,128)(2,1)S(1)} %collective-permute-done.1.refs_1_), channel_id=1, source_target_pairs={{0,4},{4,0},{1,5},{5,1},{2,6},{6,2},{3,7},{7,3},{8,12},{12,8},{9,1... | collective-permute-start | bytes 786440 | tf_op jit(solution)/shard_map/ppermute | solution.py:140
  34.0 1.5 collective-permute-done.refs_0_
  35.5 3.6 %collective-permute-start.3 = (bf16[2,64,1024]{2,1,0:T(8,128)(2,1)S(1)}, bf16[2,64,1024]{2,1,0:T(8,128)(2,1)S(1)}, u32[]{:S(2)}, u32[]{:S(2)}) collective-permute-start(bf16[2,64,1024]{2,1,0:T(8,128)(2,1)S(1)} %collective-permute-done.refs_0_), channel_id=1, source_target_pairs={{0,4},{4,0},{1,5},{5,1},{2,6},{6,2},{3,7},{7,3},{8,12},{12,8},{9,1... | collective-permute-start | bytes 786440 | tf_op jit(solution)/shard_map/ppermute | solution.py:140
  39.1 1.4 fusion.4.index
  40.5 0.0 collective-permute-done.2.refs_3_
  40.5 0.0 collective-permute-done.3.refs_4_
  40.5 0.0 copy-done
  40.5 0.0 copy-done.2
  40.5 0.0 copy-done.3
  40.6 0.7 copy-done.4
  41.2 0.7 copy-done.5
  41.9 7.2 %shard_map.59 = bf16[4,64,1024]{2,1,0:T(8,128)(2,1)} custom-call(s32[16,34]{1,0:T(8,128)} %fusion.4.index, bf16[2,64,1024]{2,1,0:T(8,128)(2,1)} %copy-done.3, bf16[2,64,1024]{2,1,0:T(8,128)(2,1)} %copy-done.2, bf16[2,64,1024]{2,1,0:T(8,128)(2,1)} %bitcast.7, bf16[2,64,1024]{2,1,0:T(8,128)(2,1)} %copy-done.4, bf16[2,64,1024]{2,1,0:T(8,128)(2,1)} %copy-done.5, ...), custom_call_target="tpu_custom_call" | custom-call | tf_op jit(solution)/shard_map/pallas_call | solution.py:180
  49.1 12.7 %all_to_all.26 = bf16[4,64,1024]{2,1,0:T(8,128)(2,1)S(1)} all-to-all(bf16[4,64,1024]{2,1,0:T(8,128)(2,1)} %shard_map.59), channel_id=1, replica_groups=mesh['z'=8,'y'=8,'core'=2,'blk'=4] {'blk'}, dimensions={0} | all-to-all | bytes 1048576 | tf_op jit(solution)/shard_map/all_to_all | solution.py:189
  61.8 0.1 reduce_sum.12
  61.9 3.1 %collective-permute-start.4 = (bf16[64,1024]{1,0:T(8,128)(2,1)S(1)}, bf16[64,1024]{1,0:T(8,128)(2,1)S(1)}, u32[]{:S(2)}, u32[]{:S(2)}) collective-permute-start(bf16[64,1024]{1,0:T(8,128)(2,1)S(1)} %reduce_sum.12), channel_id=1, source_target_pairs={{0,4},{4,0},{1,5},{5,1},{2,6},{6,2},{3,7},{7,3},{8,12},{12,8},{9,1... | collective-permute-start | bytes 393224 | tf_op jit(solution)/shard_map/ppermute | solution.py:140
  65.0 1.0 collective-permute-done.4
  66.0 0.0 copy-start.1
  66.0 7.0 %collective-permute-start.6 = (bf16[2,64,1024]{2,1,0:T(8,128)(2,1)S(1)}, bf16[2,64,1024]{2,1,0:T(8,128)(2,1)S(1)}, u32[]{:S(2)}, u32[]{:S(2)}) collective-permute-start(bf16[2,64,1024]{2,1,0:T(8,128)(2,1)S(1)} %maximum_select_fusion.refs_2_), channel_id=1, source_target_pairs={{504,0},{12,4},{0,8},{20,12},{8,16},{28,20},{16,24},{36,28},{24,32... | collective-permute-start | bytes 786440 | tf_op jit(solution)/shard_map/ppermute | solution.py:136
  73.0 2.8 %collective-permute-start.5 = (bf16[2,64,1024]{2,1,0:T(8,128)(2,1)S(1)}, bf16[2,64,1024]{2,1,0:T(8,128)(2,1)S(1)}, u32[]{:S(2)}, u32[]{:S(2)}) collective-permute-start(bf16[2,64,1024]{2,1,0:T(8,128)(2,1)S(1)} %maximum_select_fusion.refs_2_), channel_id=1, source_target_pairs={{496,0},{20,4},{504,8},{28,12},{0,16},{36,20},{8,24},{44,28},{16,3... | collective-permute-start | bytes 786440 | tf_op jit(solution)/shard_map/ppermute | solution.py:136
  75.8 0.4 collective-permute-done.6.refs_1_
  76.3 3.6 %collective-permute-start.7 = (bf16[2,64,1024]{2,1,0:T(8,128)(2,1)S(1)}, bf16[2,64,1024]{2,1,0:T(8,128)(2,1)S(1)}, u32[]{:S(2)}, u32[]{:S(2)}) collective-permute-start(bf16[2,64,1024]{2,1,0:T(8,128)(2,1)S(1)} %collective-permute-done.6.refs_1_), channel_id=1, source_target_pairs={{0,4},{4,0},{1,5},{5,1},{2,6},{6,2},{3,7},{7,3},{8,12},{12,8},{9,1... | collective-permute-start | bytes 786440 | tf_op jit(solution)/shard_map/ppermute | solution.py:140
  79.9 1.5 collective-permute-done.5.refs_0_
  81.4 5.6 %collective-permute-start.8 = (bf16[2,64,1024]{2,1,0:T(8,128)(2,1)S(1)}, bf16[2,64,1024]{2,1,0:T(8,128)(2,1)S(1)}, u32[]{:S(2)}, u32[]{:S(2)}) collective-permute-start(bf16[2,64,1024]{2,1,0:T(8,128)(2,1)S(1)} %collective-permute-done.5.refs_0_), channel_id=1, source_target_pairs={{0,4},{4,0},{1,5},{5,1},{2,6},{6,2},{3,7},{7,3},{8,12},{12,8},{9,1... | collective-permute-start | bytes 786440 | tf_op jit(solution)/shard_map/ppermute | solution.py:140
  87.0 0.0 collective-permute-done.7.refs_3_
  87.0 0.0 copy-start.8
  87.0 1.1 collective-permute-done.8.refs_4_
  88.1 0.0 copy-done.1
  88.1 0.0 copy-done.6
  88.1 0.0 copy-done.7
  88.1 0.0 copy-done.8
  88.1 0.7 copy-done.9
  88.8 7.2 %shard_map.60 = bf16[4,64,1024]{2,1,0:T(8,128)(2,1)} custom-call(s32[16,34]{1,0:T(8,128)} %fusion.4.index, bf16[2,64,1024]{2,1,0:T(8,128)(2,1)} %copy-done.7, bf16[2,64,1024]{2,1,0:T(8,128)(2,1)} %copy-done.6, bf16[2,64,1024]{2,1,0:T(8,128)(2,1)} %copy-done.1, bf16[2,64,1024]{2,1,0:T(8,128)(2,1)} %copy-done.8, bf16[2,64,1024]{2,1,0:T(8,128)(2,1)} %copy-done.9, ...), custom_call_target="tpu_custom_call" | custom-call | tf_op jit(solution)/shard_map/pallas_call | solution.py:180
  96.0 13.4 %all_to_all.27.parts = bf16[4,64,1024]{2,1,0:T(8,128)(2,1)} all-to-all(bf16[4,64,1024]{2,1,0:T(8,128)(2,1)} %shard_map.60), channel_id=1, replica_groups=mesh['z'=8,'y'=8,'core'=2,'blk'=4] {'blk'}, dimensions={0} | all-to-all | bytes 1048576 | tf_op jit(solution)/shard_map/all_to_all | solution.py:194
  109.4 2.1 %shard_map.61 = (bf16[64,1024]{1,0:T(8,128)(2,1)}, f32[8,32,128]{2,1,0:T(8,128)}) custom-call(s32[1]{0:T(128)} %bitcast.1.core, bf16[4,64,1024]{2,1,0:T(8,128)(2,1)} %all_to_all.27.parts, bf16[2,64,1024]{2,1,0:T(8,128)(2,1)} %bitcast.8), custom_call_target="tpu_custom_call" | custom-call | tf_op jit(solution)/shard_map/pallas_call | solution.py:195
  111.5 11.9 %all_to_all.28.parts = f32[8,32,128]{2,1,0:T(8,128)} all-to-all(f32[8,32,128]{2,1,0:T(8,128)} %get-tuple-element.4), channel_id=1, replica_groups=mesh['z'=8,'y'=8,'core'=2,'blk'=4] {'y'}, dimensions={0} | all-to-all | bytes 262144 | tf_op jit(solution)/shard_map/all_to_all | solution.py:200
  123.4 1.6 %shard_map.62 = f32[8,32,128]{2,1,0:T(8,128)} custom-call(f32[8,32,128]{2,1,0:T(8,128)} %all_to_all.28.parts), custom_call_target="tpu_custom_call" | custom-call | tf_op jit(solution)/shard_map/pallas_call | solution.py:201
  125.0 12.3 %all_to_all.29.parts = f32[8,32,128]{2,1,0:T(8,128)} all-to-all(f32[8,32,128]{2,1,0:T(8,128)} %shard_map.62), channel_id=1, replica_groups=mesh['z'=8,'y'=8,'core'=2,'blk'=4] {'z'}, dimensions={0} | all-to-all | bytes 262144 | tf_op jit(solution)/shard_map/all_to_all | solution.py:202
  137.3 1.5 shard_map.63.one
  138.8 5.6 %collective-permute-start.9 = (f32[1,32,128]{2,1,0:T(8,128)}, f32[1,32,128]{2,1,0:T(8,128)S(1)}, u32[]{:S(2)}, u32[]{:S(2)}) collective-permute-start(f32[1,32,128]{2,1,0:T(8,128)} %shard_map.63.one), channel_id=1, source_target_pairs={{0,4},{4,0},{1,5},{5,1},{2,6},{6,2},{3,7},{7,3},{8,12},{12,8},{9,1... | collective-permute-start | bytes 49160 | tf_op jit(solution)/shard_map/ppermute | solution.py:140
  144.5 1.0 collective-permute-done.9.two
  145.5 0.6 copy-done.10
  146.1 8.0 %shard_map.64 = (f32[16,1024]{1,0:T(8,128)}, f32[64,64]{1,0:T(8,128)}) custom-call(s32[1]{0:T(128)} %bitcast.blk, f32[1,32,128]{2,1,0:T(8,128)} %shard_map.63.one, f32[1,32,128]{2,1,0:T(8,128)} %copy-done.10, bf16[64,1024]{1,0:T(8,128)(2,1)} %get-tuple-element.5.filtered), custom_call_target="tpu_custom_call" | custom-call | tf_op jit(solution)/shard_map/pallas_call | solution.py:204
  (12 shorter events, 0.1 us)
Async XLA Ops:
  17.2 23.3 %copy-start = (bf16[8,16,1024]{2,1,0:T(8,128)(2,1)}, bf16[8,16,1024]{2,1,0:T(8,128)(2,1)S(1)}, u32[]{:S(2)}) copy-start(bf16[8,16,1024]{2,1,0:T(8,128)(2,1)S(1)} %all_to_all.25) | copy-start | bytes 786436
  17.2 13.7 %collective-permute-start.1 = (bf16[2,64,1024]{2,1,0:T(8,128)(2,1)S(1)}, bf16[2,64,1024]{2,1,0:T(8,128)(2,1)S(1)}, u32[]{:S(2)}, u32[]{:S(2)}) collective-permute-start(bf16[2,64,1024]{2,1,0:T(8,128)(2,1)S(1)} %bitcast.5), channel_id=1, source_target_pairs={{504,0},{12,4},{0,8},{20,12},{8,16},{28,20},{16,24},{36,28},{24,32... | collective-permute-start | bytes 786440 | tf_op jit(solution)/shard_map/ppermute | solution.py:136
  27.1 8.4 %collective-permute-start = (bf16[2,64,1024]{2,1,0:T(8,128)(2,1)S(1)}, bf16[2,64,1024]{2,1,0:T(8,128)(2,1)S(1)}, u32[]{:S(2)}, u32[]{:S(2)}) collective-permute-start(bf16[2,64,1024]{2,1,0:T(8,128)(2,1)S(1)} %bitcast.6), channel_id=1, source_target_pairs={{496,0},{20,4},{504,8},{28,12},{0,16},{36,20},{8,24},{44,28},{16,3... | collective-permute-start | bytes 786440 | tf_op jit(solution)/shard_map/ppermute | solution.py:136
  30.9 9.6 %copy-start.2 = (bf16[2,64,1024]{2,1,0:T(8,128)(2,1)}, bf16[2,64,1024]{2,1,0:T(8,128)(2,1)S(1)}, u32[]{:S(2)}) copy-start(bf16[2,64,1024]{2,1,0:T(8,128)(2,1)S(1)} %collective-permute-done.1.refs_1_) | copy-start | bytes 786436
  30.9 9.6 %collective-permute-start.2 = (bf16[2,64,1024]{2,1,0:T(8,128)(2,1)S(1)}, bf16[2,64,1024]{2,1,0:T(8,128)(2,1)S(1)}, u32[]{:S(2)}, u32[]{:S(2)}) collective-permute-start(bf16[2,64,1024]{2,1,0:T(8,128)(2,1)S(1)} %collective-permute-done.1.refs_1_), channel_id=1, source_target_pairs={{0,4},{4,0},{1,5},{5,1},{2,6},{6,2},{3,7},{7,3},{8,12},{12,8},{9,1... | collective-permute-start | bytes 786440 | tf_op jit(solution)/shard_map/ppermute | solution.py:140
  35.5 5.1 %copy-start.3 = (bf16[2,64,1024]{2,1,0:T(8,128)(2,1)}, bf16[2,64,1024]{2,1,0:T(8,128)(2,1)S(1)}, u32[]{:S(2)}) copy-start(bf16[2,64,1024]{2,1,0:T(8,128)(2,1)S(1)} %collective-permute-done.refs_0_) | copy-start | bytes 786436
  35.5 5.1 %collective-permute-start.3 = (bf16[2,64,1024]{2,1,0:T(8,128)(2,1)S(1)}, bf16[2,64,1024]{2,1,0:T(8,128)(2,1)S(1)}, u32[]{:S(2)}, u32[]{:S(2)}) collective-permute-start(bf16[2,64,1024]{2,1,0:T(8,128)(2,1)S(1)} %collective-permute-done.refs_0_), channel_id=1, source_target_pairs={{0,4},{4,0},{1,5},{5,1},{2,6},{6,2},{3,7},{7,3},{8,12},{12,8},{9,1... | collective-permute-start | bytes 786440 | tf_op jit(solution)/shard_map/ppermute | solution.py:140
  40.5 0.7 copy-start.4
  41.2 0.7 copy-start.5
  61.9 4.0 %collective-permute-start.4 = (bf16[64,1024]{1,0:T(8,128)(2,1)S(1)}, bf16[64,1024]{1,0:T(8,128)(2,1)S(1)}, u32[]{:S(2)}, u32[]{:S(2)}) collective-permute-start(bf16[64,1024]{1,0:T(8,128)(2,1)S(1)} %reduce_sum.12), channel_id=1, source_target_pairs={{0,4},{4,0},{1,5},{5,1},{2,6},{6,2},{3,7},{7,3},{8,12},{12,8},{9,1... | collective-permute-start | bytes 393224 | tf_op jit(solution)/shard_map/ppermute | solution.py:140
  66.0 22.1 %copy-start.1 = (bf16[2,64,1024]{2,1,0:T(8,128)(2,1)}, bf16[2,64,1024]{2,1,0:T(8,128)(2,1)S(1)}, u32[]{:S(2)}) copy-start(bf16[2,64,1024]{2,1,0:T(8,128)(2,1)S(1)} %maximum_select_fusion.refs_2_) | copy-start | bytes 786436
  66.0 10.3 %collective-permute-start.6 = (bf16[2,64,1024]{2,1,0:T(8,128)(2,1)S(1)}, bf16[2,64,1024]{2,1,0:T(8,128)(2,1)S(1)}, u32[]{:S(2)}, u32[]{:S(2)}) collective-permute-start(bf16[2,64,1024]{2,1,0:T(8,128)(2,1)S(1)} %maximum_select_fusion.refs_2_), channel_id=1, source_target_pairs={{504,0},{12,4},{0,8},{20,12},{8,16},{28,20},{16,24},{36,28},{24,32... | collective-permute-start | bytes 786440 | tf_op jit(solution)/shard_map/ppermute | solution.py:136
  73.0 8.4 %collective-permute-start.5 = (bf16[2,64,1024]{2,1,0:T(8,128)(2,1)S(1)}, bf16[2,64,1024]{2,1,0:T(8,128)(2,1)S(1)}, u32[]{:S(2)}, u32[]{:S(2)}) collective-permute-start(bf16[2,64,1024]{2,1,0:T(8,128)(2,1)S(1)} %maximum_select_fusion.refs_2_), channel_id=1, source_target_pairs={{496,0},{20,4},{504,8},{28,12},{0,16},{36,20},{8,24},{44,28},{16,3... | collective-permute-start | bytes 786440 | tf_op jit(solution)/shard_map/ppermute | solution.py:136
  76.3 11.8 %copy-start.6 = (bf16[2,64,1024]{2,1,0:T(8,128)(2,1)}, bf16[2,64,1024]{2,1,0:T(8,128)(2,1)S(1)}, u32[]{:S(2)}) copy-start(bf16[2,64,1024]{2,1,0:T(8,128)(2,1)S(1)} %collective-permute-done.6.refs_1_) | copy-start | bytes 786436
  76.3 10.7 %collective-permute-start.7 = (bf16[2,64,1024]{2,1,0:T(8,128)(2,1)S(1)}, bf16[2,64,1024]{2,1,0:T(8,128)(2,1)S(1)}, u32[]{:S(2)}, u32[]{:S(2)}) collective-permute-start(bf16[2,64,1024]{2,1,0:T(8,128)(2,1)S(1)} %collective-permute-done.6.refs_1_), channel_id=1, source_target_pairs={{0,4},{4,0},{1,5},{5,1},{2,6},{6,2},{3,7},{7,3},{8,12},{12,8},{9,1... | collective-permute-start | bytes 786440 | tf_op jit(solution)/shard_map/ppermute | solution.py:140
  81.4 6.7 %copy-start.7 = (bf16[2,64,1024]{2,1,0:T(8,128)(2,1)}, bf16[2,64,1024]{2,1,0:T(8,128)(2,1)S(1)}, u32[]{:S(2)}) copy-start(bf16[2,64,1024]{2,1,0:T(8,128)(2,1)S(1)} %collective-permute-done.5.refs_0_) | copy-start | bytes 786436
  81.4 6.7 %collective-permute-start.8 = (bf16[2,64,1024]{2,1,0:T(8,128)(2,1)S(1)}, bf16[2,64,1024]{2,1,0:T(8,128)(2,1)S(1)}, u32[]{:S(2)}, u32[]{:S(2)}) collective-permute-start(bf16[2,64,1024]{2,1,0:T(8,128)(2,1)S(1)} %collective-permute-done.5.refs_0_), channel_id=1, source_target_pairs={{0,4},{4,0},{1,5},{5,1},{2,6},{6,2},{3,7},{7,3},{8,12},{12,8},{9,1... | collective-permute-start | bytes 786440 | tf_op jit(solution)/shard_map/ppermute | solution.py:140
  87.0 1.1 copy-start.8
  88.1 0.7 copy-start.9
  138.8 6.6 %collective-permute-start.9 = (f32[1,32,128]{2,1,0:T(8,128)}, f32[1,32,128]{2,1,0:T(8,128)S(1)}, u32[]{:S(2)}, u32[]{:S(2)}) collective-permute-start(f32[1,32,128]{2,1,0:T(8,128)} %shard_map.63.one), channel_id=1, source_target_pairs={{0,4},{4,0},{1,5},{5,1},{2,6},{6,2},{3,7},{7,3},{8,12},{12,8},{9,1... | collective-permute-start | bytes 49160 | tf_op jit(solution)/shard_map/ppermute | solution.py:140
  145.5 0.6 copy-start.10

commit v2 on v1

--- a/solution.py
+++ b/solution.py
@@ -15,10 +15,15 @@
 SMEM_SPEC = pl.BlockSpec(memory_space=pltpu.SMEM)
 
 
-def call(kernel, out_shape, in_specs, scratch=()):
+def call(kernel, out_shape, in_specs, scratch=(), mib=4):
     outs = jax.tree.map(lambda _: VMEM_SPEC, out_shape)
     return pl.pallas_call(
-        kernel, out_shape=out_shape, in_specs=in_specs, out_specs=outs, scratch_shapes=scratch
+        kernel,
+        out_shape=out_shape,
+        in_specs=in_specs,
+        out_specs=outs,
+        scratch_shapes=scratch,
+        compiler_params=pltpu.CompilerParams(vmem_limit_bytes=mib << 20),
     )
 
 
@@ -75,20 +80,23 @@
     filtered[...] = value
     g = lax.dot_general(value, value, (((1,), (1,)), ((), ())), preferred_element_type=F32)
     packed = jnp.concatenate([g[:32], g[32:]], axis=1)
-    for c in range(8):
+    for c in range(gram.shape[0]):
         gram[c] = packed
 
 
 def sum_kernel(parts, out):
+    total = parts[0]
+    for c in range(1, parts.shape[0]):
+        total += parts[c]
+    for c in range(out.shape[0]):
+        out[c] = total
+
+
+def factor_kernel(scale, blk, parts, filtered, basis, factor, scratch):
     total = parts[0]
     for c in range(1, 8):
         total += parts[c]
-    for c in range(out.shape[0]):
-        out[c] = total
-
-
-def factor_kernel(scale, blk, one, two, filtered, basis, factor, scratch):
-    packed = (one[0] + two[0]) * scale
+    packed = total * scale
     lane = lax.broadcasted_iota(jnp.int32, (8, 128), 1)
     sub = lax.broadcasted_iota(jnp.int32, (8, 128), 0)
     chunks = []
@@ -98,22 +106,24 @@
             rows = jnp.concatenate([rows[:, 64:], rows[:, :64]], axis=1)
         eye = jnp.where(lane - 64 == sub + 8 * c, F32(1.0), F32(0.0))
         chunks.append(jnp.where(lane < 64, rows, eye))
-    for k in range(64):
+    for k in range(63):
         ck, r = divmod(k, 8)
-        row = chunks[ck][r : r + 1]
-        inv = 1.0 / jnp.sqrt(row[:, k : k + 1])
-        unit = row * inv
-        for c in range(ck, 8):
-            col = chunks[c][:, k : k + 1] * inv
-            if c == ck:
-                moved = jnp.where(sub > r, chunks[c] - col * unit, chunks[c])
-                chunks[c] = jnp.where(sub == r, jnp.broadcast_to(unit, (8, 128)), moved)
-            else:
-                chunks[c] = chunks[c] - col * unit
+        row = jnp.broadcast_to(chunks[ck][r : r + 1], (8, 128))
+        lead = jnp.broadcast_to(chunks[ck][:, k : k + 1], (8, 128))
+        inv = 1.0 / jnp.broadcast_to(lead[r : r + 1], (8, 128))
+        if r < 7:
+            times = jnp.where(sub > r, lead * inv, F32(0.0))
+            chunks[ck] = chunks[ck] - times * row
+        for c in range(ck + 1, 8):
+            lead = jnp.broadcast_to(chunks[c][:, k : k + 1], (8, 128))
+            chunks[c] = chunks[c] - (lead * inv) * row
     for c in range(8):
-        keep = jnp.where(lane >= sub + 8 * c, chunks[c], F32(0.0))
+        pivot = jnp.where(lane == sub + 8 * c, chunks[c], F32(0.0))
+        root = 1.0 / jnp.sqrt(jnp.sum(pivot, axis=1, keepdims=True))
+        scaled = chunks[c] * root
+        keep = jnp.where(lane >= sub + 8 * c, scaled, F32(0.0))
         factor[8 * c : 8 * c + 8, :] = keep[:, :64]
-        scratch[8 * c : 8 * c + 8, :] = chunks[c][:, 64:]
+        scratch[8 * c : 8 * c + 8, :] = scaled[:, 64:]
     mine = scratch[pl.ds(pl.multiple_of(blk[0] * 16, 16), 16), :]
     total = jnp.zeros(basis.shape, F32)
     rest = mine
@@ -182,6 +192,7 @@
             shape((copies, vecs, block_rows * width), BF16),
             [SMEM_SPEC] + [VMEM_SPEC] * 6,
             [pltpu.VMEM((161, vecs, 128), BF16)],
+            12,
         )(index, *pieces, hamiltonian)
 
     pair = to_all(vectors, ("core", "blk"), 8).reshape(2, vecs, block_rows * width)
@@ -194,19 +205,18 @@
     parts = lax.all_to_all(parts, "blk", 0, 0, tiled=True)
     filtered, gram = call(
         gram_kernel,
-        (shape((vecs, block_rows * width), BF16), shape((8, 32, 128), F32)),
+        (shape((vecs, block_rows * width), BF16), shape((16, 32, 128), F32)),
         [SMEM_SPEC, VMEM_SPEC, VMEM_SPEC],
     )(core_id, parts, pair)
-    gram = lax.all_to_all(gram, "y", 0, 0, tiled=True)
+    gram = lax.all_to_all(gram, ("y", "core"), 0, 0, tiled=True)
     gram = call(sum_kernel, shape((8, 32, 128), F32), [VMEM_SPEC])(gram)
     gram = lax.all_to_all(gram, "z", 0, 0, tiled=True)
-    gram = call(sum_kernel, shape((1, 32, 128), F32), [VMEM_SPEC])(gram)
     basis, factor = call(
         functools.partial(factor_kernel, 1.0 / (total_blocks * width)),
         (shape(vectors.shape, F32), shape((vecs, vecs), F32)),
-        [SMEM_SPEC] + [VMEM_SPEC] * 3,
+        [SMEM_SPEC] + [VMEM_SPEC] * 2,
         [pltpu.VMEM((vecs, vecs), F32)],
-    )(blk_id, gram, flip(gram), filtered)
+    )(blk_id, gram, filtered)
     return basis, factor
 
 

time: 155 us -> 143 us (0.923)
  Pallas kernels: 27.6 us -> 18.4 us
  starting transfers between devices: 48 us -> 43.1 us
  local copies, waits for them, and re-layouts: 3.47 us -> 5.3 us
    pallas_call x2, Pallas kernels: 14.3 us -> 8.96 us  [products(): call(functools.partial(product_kernel, copies), shape((copies, vecs, bloc...]
    ppermute x6 -> x5, starting transfers between devices: 24.5 us -> 19.6 us  [flip(): return lax.ppermute(value, 'core', [(0, 1), (1, 0)])]
    all_to_all x1, blocking collectives: 11.9 us -> 15.4 us  [body(): gram = lax.all_to_all(gram, ('y', 'core'), 0, 0, tiled=True)]
    all_to_all x2, blocking collectives: 26.1 us -> 22.8 us  [body(): parts = lax.all_to_all(parts, 'blk', 0, 0, tiled=True)]
    pallas_call x2 -> x1, Pallas kernels: 3.6 us -> 0.32 us  [body(): call(gram_kernel, (shape((vecs, block_rows * width), BF16), shape((16, 32...]
    unnamed x22 -> x4, local copies, waits for them, and re-layouts: 2.69 us -> 4.52 us
    pallas_call x1, Pallas kernels: 1.59 us -> 0.03 us  [body(): gram = call(sum_kernel, shape((8, 32, 128), F32), [VMEM_SPEC])(gram)]
    ppermute x6 -> x5, waiting for transfers between devices: 3.12 us -> 2.44 us  [flip(): return lax.ppermute(value, 'core', [(0, 1), (1, 0)])]
  transfers between devices with their start and end apart: 10 -> 9, of which waited for: 6 -> 6; matrix products, arithmetic and copies ran while one was open for 1% -> 1% of each run, Pallas kernels for 0% -> 0%
where the time goes in v2:
time: 143 us; the launch traced here: 142 us
  blocking collectives  67.5 us (47%)
  starting transfers between devices  43.1 us (30%)
  Pallas kernels  18.4 us (13%)
  waiting for transfers between devices  6.02 us (4%)
  local copies, waits for them, and re-layouts  5.3 us (4%)
    ppermute x4, starting transfers between devices, from_chip(): return lax.ppermute(value, ROWS, pairs)  23.5 us
    all_to_all x2, blocking collectives, body(): parts = lax.all_to_all(parts, 'blk', 0, 0, tiled=True)  22.8 us
    ppermute x5, starting transfers between devices, flip(): return lax.ppermute(value, 'core', [(0, 1), (1, 0)])  19.6 us
    all_to_all x1, blocking collectives, to_all(): lax.all_to_all(jnp.broadcast_to(value[None], (count,) + value.shape), axe...  15.8 us
    all_to_all x1, blocking collectives, body(): gram = lax.all_to_all(gram, ('y', 'core'), 0, 0, tiled=True)  15.4 us
    all_to_all x1, blocking collectives, body(): gram = lax.all_to_all(gram, 'z', 0, 0, tiled=True)  13.5 us
    pallas_call x1, Pallas kernels, body(): call(functools.partial(factor_kernel, 1.0 / (total_blocks * width)), (sha...  9.14 us
    pallas_call x2, Pallas kernels, products(): call(functools.partial(product_kernel, copies), shape((copies, vecs, bloc...  8.96 us
  transfers between devices with their start and end apart: 9, of which 6 were waited for; matrix products, arithmetic and copies ran while one was open for 1% of the time, Pallas kernels for 0%

profile of v2, /device:TPU:1, one launch (start us, length us, event | category | flops | bytes accessed | tf_op | source)
XLA Modules:
  0.0 142.1 jit_solution(6268892768489930265)
XLA Ops:
  0.6 0.8 broadcast_in_dim.12
  1.4 15.8 %all_to_all.25 = bf16[8,16,1024]{2,1,0:T(8,128)(2,1)S(1)} all-to-all(bf16[8,16,1024]{2,1,0:T(8,128)(2,1)S(1)} %broadcast_in_dim.12), channel_id=1, replica_groups=mesh['z'=8,'y'=8,'core'=2,'blk'=4] {'core','blk'}, dimensions={0} | all-to-all | bytes 524288 | tf_op jit(solution)/shard_map/all_to_all | solution.py:162
  17.2 9.9 %collective-permute-start.1 = (bf16[2,64,1024]{2,1,0:T(8,128)(2,1)S(1)}, bf16[2,64,1024]{2,1,0:T(8,128)(2,1)S(1)}, u32[]{:S(2)}, u32[]{:S(2)}) collective-permute-start(bf16[2,64,1024]{2,1,0:T(8,128)(2,1)S(1)} %bitcast.5), channel_id=1, source_target_pairs={{504,0},{12,4},{0,8},{20,12},{8,16},{28,20},{16,24},{36,28},{24,32... | collective-permute-start | bytes 786440 | tf_op jit(solution)/shard_map/ppermute | solution.py:146
  27.1 3.8 %collective-permute-start = (bf16[2,64,1024]{2,1,0:T(8,128)(2,1)S(1)}, bf16[2,64,1024]{2,1,0:T(8,128)(2,1)S(1)}, u32[]{:S(2)}, u32[]{:S(2)}) collective-permute-start(bf16[2,64,1024]{2,1,0:T(8,128)(2,1)S(1)} %bitcast.6), channel_id=1, source_target_pairs={{496,0},{20,4},{504,8},{28,12},{0,16},{36,20},{8,24},{44,28},{16,3... | collective-permute-start | bytes 786440 | tf_op jit(solution)/shard_map/ppermute | solution.py:146
  30.9 0.0 collective-permute-done.1.refs_1_
  30.9 3.0 %collective-permute-start.2 = (bf16[2,64,1024]{2,1,0:T(8,128)(2,1)S(1)}, bf16[2,64,1024]{2,1,0:T(8,128)(2,1)S(1)}, u32[]{:S(2)}, u32[]{:S(2)}) collective-permute-start(bf16[2,64,1024]{2,1,0:T(8,128)(2,1)S(1)} %collective-permute-done.1.refs_1_), channel_id=1, source_target_pairs={{0,4},{4,0},{1,5},{5,1},{2,6},{6,2},{3,7},{7,3},{8,12},{12,8},{9,1... | collective-permute-start | bytes 786440 | tf_op jit(solution)/shard_map/ppermute | solution.py:150
  34.0 1.5 %collective-permute-done.refs_0_ = bf16[2,64,1024]{2,1,0:T(8,128)(2,1)S(1)} collective-permute-done((bf16[2,64,1024]{2,1,0:T(8,128)(2,1)S(1)}, bf16[2,64,1024]{2,1,0:T(8,128)(2,1)S(1)}, u32[]{:S(2)}, u32[]{:S(2)}) %collective-permute-start) | collective-permute-done | bytes 262176 | tf_op jit(solution)/shard_map/ppermute | solution.py:146
  35.5 3.6 %collective-permute-start.3 = (bf16[2,64,1024]{2,1,0:T(8,128)(2,1)S(1)}, bf16[2,64,1024]{2,1,0:T(8,128)(2,1)S(1)}, u32[]{:S(2)}, u32[]{:S(2)}) collective-permute-start(bf16[2,64,1024]{2,1,0:T(8,128)(2,1)S(1)} %collective-permute-done.refs_0_), channel_id=1, source_target_pairs={{0,4},{4,0},{1,5},{5,1},{2,6},{6,2},{3,7},{7,3},{8,12},{12,8},{9,1... | collective-permute-start | bytes 786440 | tf_op jit(solution)/shard_map/ppermute | solution.py:150
  39.1 0.8 fusion.4.index
  39.9 0.0 collective-permute-done.2.refs_3_
  39.9 0.3 collective-permute-done.3.refs_4_
  40.2 0.0 copy-start
  40.3 2.3 %copy-done = bf16[16,64,2176]{2,1,0:T(8,128)(2,1)S(1)} copy-done((bf16[16,64,2176]{2,1,0:T(8,128)(2,1)S(1)}, bf16[16,64,2176]{2,1,0:T(8,128)(2,1)}, u32[]{:S(2)}) %copy-start) | copy-done | bytes 4456472
  42.5 4.5 %shard_map.59 = bf16[4,64,1024]{2,1,0:T(8,128)(2,1)S(1)} custom-call(s32[16,34]{1,0:T(8,128)S(1)} %fusion.4.index, bf16[2,64,1024]{2,1,0:T(8,128)(2,1)S(1)} %collective-permute-done.refs_0_, bf16[2,64,1024]{2,1,0:T(8,128)(2,1)S(1)} %collective-permute-done.1.refs_1_, bf16[2,64,1024]{2,1,0:T(8,128)(2,1)S(1)} %bitcast.7, ...), custom_call_target="tpu_custom_call" | custom-call | tf_op jit(solution)/shard_map/pallas_call | solution.py:190
  47.0 11.2 %all_to_all.26 = bf16[4,64,1024]{2,1,0:T(8,128)(2,1)S(1)} all-to-all(bf16[4,64,1024]{2,1,0:T(8,128)(2,1)S(1)} %shard_map.59), channel_id=1, replica_groups=mesh['z'=8,'y'=8,'core'=2,'blk'=4] {'blk'}, dimensions={0} | all-to-all | bytes 1048576 | tf_op jit(solution)/shard_map/all_to_all | solution.py:200
  58.2 0.1 reduce_sum.12
  58.3 3.7 %collective-permute-start.4 = (bf16[64,1024]{1,0:T(8,128)(2,1)S(1)}, bf16[64,1024]{1,0:T(8,128)(2,1)S(1)}, u32[]{:S(2)}, u32[]{:S(2)}) collective-permute-start(bf16[64,1024]{1,0:T(8,128)(2,1)S(1)} %reduce_sum.12), channel_id=1, source_target_pairs={{0,4},{4,0},{1,5},{5,1},{2,6},{6,2},{3,7},{7,3},{8,12},{12,8},{9,1... | collective-permute-start | bytes 393224 | tf_op jit(solution)/shard_map/ppermute | solution.py:150
  62.0 1.0 collective-permute-done.4
  63.0 7.2 %collective-permute-start.6 = (bf16[2,64,1024]{2,1,0:T(8,128)(2,1)S(1)}, bf16[2,64,1024]{2,1,0:T(8,128)(2,1)S(1)}, u32[]{:S(2)}, u32[]{:S(2)}) collective-permute-start(bf16[2,64,1024]{2,1,0:T(8,128)(2,1)S(1)} %maximum_select_fusion.refs_2_), channel_id=1, source_target_pairs={{504,0},{12,4},{0,8},{20,12},{8,16},{28,20},{16,24},{36,28},{24,32... | collective-permute-start | bytes 786440 | tf_op jit(solution)/shard_map/ppermute | solution.py:146
  70.2 2.7 %collective-permute-start.5 = (bf16[2,64,1024]{2,1,0:T(8,128)(2,1)S(1)}, bf16[2,64,1024]{2,1,0:T(8,128)(2,1)S(1)}, u32[]{:S(2)}, u32[]{:S(2)}) collective-permute-start(bf16[2,64,1024]{2,1,0:T(8,128)(2,1)S(1)} %maximum_select_fusion.refs_2_), channel_id=1, source_target_pairs={{496,0},{20,4},{504,8},{28,12},{0,16},{36,20},{8,24},{44,28},{16,3... | collective-permute-start | bytes 786440 | tf_op jit(solution)/shard_map/ppermute | solution.py:146
  72.9 0.6 collective-permute-done.6.refs_1_
  73.5 3.6 %collective-permute-start.7 = (bf16[2,64,1024]{2,1,0:T(8,128)(2,1)S(1)}, bf16[2,64,1024]{2,1,0:T(8,128)(2,1)S(1)}, u32[]{:S(2)}, u32[]{:S(2)}) collective-permute-start(bf16[2,64,1024]{2,1,0:T(8,128)(2,1)S(1)} %collective-permute-done.6.refs_1_), channel_id=1, source_target_pairs={{0,4},{4,0},{1,5},{5,1},{2,6},{6,2},{3,7},{7,3},{8,12},{12,8},{9,1... | collective-permute-start | bytes 786440 | tf_op jit(solution)/shard_map/ppermute | solution.py:150
  77.1 1.5 %collective-permute-done.5.refs_0_ = bf16[2,64,1024]{2,1,0:T(8,128)(2,1)S(1)} collective-permute-done((bf16[2,64,1024]{2,1,0:T(8,128)(2,1)S(1)}, bf16[2,64,1024]{2,1,0:T(8,128)(2,1)S(1)}, u32[]{:S(2)}, u32[]{:S(2)}) %collective-permute-start.5) | collective-permute-done | bytes 262176 | tf_op jit(solution)/shard_map/ppermute | solution.py:146
  78.6 5.6 %collective-permute-start.8 = (bf16[2,64,1024]{2,1,0:T(8,128)(2,1)S(1)}, bf16[2,64,1024]{2,1,0:T(8,128)(2,1)S(1)}, u32[]{:S(2)}, u32[]{:S(2)}) collective-permute-start(bf16[2,64,1024]{2,1,0:T(8,128)(2,1)S(1)} %collective-permute-done.5.refs_0_), channel_id=1, source_target_pairs={{0,4},{4,0},{1,5},{5,1},{2,6},{6,2},{3,7},{7,3},{8,12},{12,8},{9,1... | collective-permute-start | bytes 786440 | tf_op jit(solution)/shard_map/ppermute | solution.py:150
  84.2 0.0 collective-permute-done.7.refs_3_
  84.2 1.1 collective-permute-done.8.refs_4_
  85.3 0.0 copy-start.1
  85.3 2.3 %copy-done.1 = bf16[16,64,2176]{2,1,0:T(8,128)(2,1)S(1)} copy-done((bf16[16,64,2176]{2,1,0:T(8,128)(2,1)S(1)}, bf16[16,64,2176]{2,1,0:T(8,128)(2,1)}, u32[]{:S(2)}) %copy-start.1) | copy-done | bytes 4456472
  87.6 4.5 %shard_map.60 = bf16[4,64,1024]{2,1,0:T(8,128)(2,1)S(1)} custom-call(s32[16,34]{1,0:T(8,128)S(1)} %fusion.4.index, bf16[2,64,1024]{2,1,0:T(8,128)(2,1)S(1)} %collective-permute-done.5.refs_0_, bf16[2,64,1024]{2,1,0:T(8,128)(2,1)S(1)} %collective-permute-done.6.refs_1_, bf16[2,64,1024]{2,1,0:T(8,128)(2,1)S(1)} %maximum_select_fusion.refs_2_, ...), custom_call_target="tpu_custom_call" | custom-call | tf_op jit(solution)/shard_map/pallas_call | solution.py:190
  92.1 11.6 %all_to_all.27.parts = bf16[4,64,1024]{2,1,0:T(8,128)(2,1)S(1)} all-to-all(bf16[4,64,1024]{2,1,0:T(8,128)(2,1)S(1)} %shard_map.60), channel_id=1, replica_groups=mesh['z'=8,'y'=8,'core'=2,'blk'=4] {'blk'}, dimensions={0} | all-to-all | bytes 1048576 | tf_op jit(solution)/shard_map/all_to_all | solution.py:205
  103.7 0.3 shard_map.61
  104.0 15.4 %all_to_all.28.parts = f32[16,32,128]{2,1,0:T(8,128)S(1)} all-to-all(f32[16,32,128]{2,1,0:T(8,128)S(1)} %get-tuple-element.4), channel_id=1, replica_groups=mesh['z'=8,'y'=8,'core'=2,'blk'=4] {'y','core'}, dimensions={0} | all-to-all | bytes 524288 | tf_op jit(solution)/shard_map/all_to_all | solution.py:211
  119.4 13.5 %all_to_all.29.parts = f32[8,32,128]{2,1,0:T(8,128)S(1)} all-to-all(f32[8,32,128]{2,1,0:T(8,128)S(1)} %shard_map.62), channel_id=1, replica_groups=mesh['z'=8,'y'=8,'core'=2,'blk'=4] {'z'}, dimensions={0} | all-to-all | bytes 262144 | tf_op jit(solution)/shard_map/all_to_all | solution.py:213
  132.9 9.1 %shard_map.63 = (f32[16,1024]{1,0:T(8,128)}, f32[64,64]{1,0:T(8,128)}) custom-call(s32[1]{0:T(128)} %bitcast.blk, f32[8,32,128]{2,1,0:T(8,128)S(1)} %all_to_all.29.parts, bf16[64,1024]{1,0:T(8,128)(2,1)S(1)} %get-tuple-element.5.filtered), custom_call_target="tpu_custom_call" | custom-call | tf_op jit(solution)/shard_map/pallas_call | solution.py:214
  (5 shorter events, 0.1 us)
Async XLA Ops:
  17.2 13.7 %collective-permute-start.1 = (bf16[2,64,1024]{2,1,0:T(8,128)(2,1)S(1)}, bf16[2,64,1024]{2,1,0:T(8,128)(2,1)S(1)}, u32[]{:S(2)}, u32[]{:S(2)}) collective-permute-start(bf16[2,64,1024]{2,1,0:T(8,128)(2,1)S(1)} %bitcast.5), channel_id=1, source_target_pairs={{504,0},{12,4},{0,8},{20,12},{8,16},{28,20},{16,24},{36,28},{24,32... | collective-permute-start | bytes 786440 | tf_op jit(solution)/shard_map/ppermute | solution.py:146
  27.1 8.4 %collective-permute-start = (bf16[2,64,1024]{2,1,0:T(8,128)(2,1)S(1)}, bf16[2,64,1024]{2,1,0:T(8,128)(2,1)S(1)}, u32[]{:S(2)}, u32[]{:S(2)}) collective-permute-start(bf16[2,64,1024]{2,1,0:T(8,128)(2,1)S(1)} %bitcast.6), channel_id=1, source_target_pairs={{496,0},{20,4},{504,8},{28,12},{0,16},{36,20},{8,24},{44,28},{16,3... | collective-permute-start | bytes 786440 | tf_op jit(solution)/shard_map/ppermute | solution.py:146
  30.9 9.0 %collective-permute-start.2 = (bf16[2,64,1024]{2,1,0:T(8,128)(2,1)S(1)}, bf16[2,64,1024]{2,1,0:T(8,128)(2,1)S(1)}, u32[]{:S(2)}, u32[]{:S(2)}) collective-permute-start(bf16[2,64,1024]{2,1,0:T(8,128)(2,1)S(1)} %collective-permute-done.1.refs_1_), channel_id=1, source_target_pairs={{0,4},{4,0},{1,5},{5,1},{2,6},{6,2},{3,7},{7,3},{8,12},{12,8},{9,1... | collective-permute-start | bytes 786440 | tf_op jit(solution)/shard_map/ppermute | solution.py:150
  35.5 4.8 %collective-permute-start.3 = (bf16[2,64,1024]{2,1,0:T(8,128)(2,1)S(1)}, bf16[2,64,1024]{2,1,0:T(8,128)(2,1)S(1)}, u32[]{:S(2)}, u32[]{:S(2)}) collective-permute-start(bf16[2,64,1024]{2,1,0:T(8,128)(2,1)S(1)} %collective-permute-done.refs_0_), channel_id=1, source_target_pairs={{0,4},{4,0},{1,5},{5,1},{2,6},{6,2},{3,7},{7,3},{8,12},{12,8},{9,1... | collective-permute-start | bytes 786440 | tf_op jit(solution)/shard_map/ppermute | solution.py:150
  40.2 2.3 %copy-start = (bf16[16,64,2176]{2,1,0:T(8,128)(2,1)S(1)}, bf16[16,64,2176]{2,1,0:T(8,128)(2,1)}, u32[]{:S(2)}) copy-start(bf16[16,64,2176]{2,1,0:T(8,128)(2,1)} %refs_5_.3) | copy-start | bytes 13369348
  58.3 4.7 %collective-permute-start.4 = (bf16[64,1024]{1,0:T(8,128)(2,1)S(1)}, bf16[64,1024]{1,0:T(8,128)(2,1)S(1)}, u32[]{:S(2)}, u32[]{:S(2)}) collective-permute-start(bf16[64,1024]{1,0:T(8,128)(2,1)S(1)} %reduce_sum.12), channel_id=1, source_target_pairs={{0,4},{4,0},{1,5},{5,1},{2,6},{6,2},{3,7},{7,3},{8,12},{12,8},{9,1... | collective-permute-start | bytes 393224 | tf_op jit(solution)/shard_map/ppermute | solution.py:150
  63.0 10.5 %collective-permute-start.6 = (bf16[2,64,1024]{2,1,0:T(8,128)(2,1)S(1)}, bf16[2,64,1024]{2,1,0:T(8,128)(2,1)S(1)}, u32[]{:S(2)}, u32[]{:S(2)}) collective-permute-start(bf16[2,64,1024]{2,1,0:T(8,128)(2,1)S(1)} %maximum_select_fusion.refs_2_), channel_id=1, source_target_pairs={{504,0},{12,4},{0,8},{20,12},{8,16},{28,20},{16,24},{36,28},{24,32... | collective-permute-start | bytes 786440 | tf_op jit(solution)/shard_map/ppermute | solution.py:146
  70.2 8.4 %collective-permute-start.5 = (bf16[2,64,1024]{2,1,0:T(8,128)(2,1)S(1)}, bf16[2,64,1024]{2,1,0:T(8,128)(2,1)S(1)}, u32[]{:S(2)}, u32[]{:S(2)}) collective-permute-start(bf16[2,64,1024]{2,1,0:T(8,128)(2,1)S(1)} %maximum_select_fusion.refs_2_), channel_id=1, source_target_pairs={{496,0},{20,4},{504,8},{28,12},{0,16},{36,20},{8,24},{44,28},{16,3... | collective-permute-start | bytes 786440 | tf_op jit(solution)/shard_map/ppermute | solution.py:146
  73.5 10.7 %collective-permute-start.7 = (bf16[2,64,1024]{2,1,0:T(8,128)(2,1)S(1)}, bf16[2,64,1024]{2,1,0:T(8,128)(2,1)S(1)}, u32[]{:S(2)}, u32[]{:S(2)}) collective-permute-start(bf16[2,64,1024]{2,1,0:T(8,128)(2,1)S(1)} %collective-permute-done.6.refs_1_), channel_id=1, source_target_pairs={{0,4},{4,0},{1,5},{5,1},{2,6},{6,2},{3,7},{7,3},{8,12},{12,8},{9,1... | collective-permute-start | bytes 786440 | tf_op jit(solution)/shard_map/ppermute | solution.py:150
  78.6 6.8 %collective-permute-start.8 = (bf16[2,64,1024]{2,1,0:T(8,128)(2,1)S(1)}, bf16[2,64,1024]{2,1,0:T(8,128)(2,1)S(1)}, u32[]{:S(2)}, u32[]{:S(2)}) collective-permute-start(bf16[2,64,1024]{2,1,0:T(8,128)(2,1)S(1)} %collective-permute-done.5.refs_0_), channel_id=1, source_target_pairs={{0,4},{4,0},{1,5},{5,1},{2,6},{6,2},{3,7},{7,3},{8,12},{12,8},{9,1... | collective-permute-start | bytes 786440 | tf_op jit(solution)/shard_map/ppermute | solution.py:150
  85.3 2.3 %copy-start.1 = (bf16[16,64,2176]{2,1,0:T(8,128)(2,1)S(1)}, bf16[16,64,2176]{2,1,0:T(8,128)(2,1)}, u32[]{:S(2)}) copy-start(bf16[16,64,2176]{2,1,0:T(8,128)(2,1)} %refs_5_.3) | copy-start | bytes 13369348

commit v3 on v2

v3 whole, which is shorter than its diff:
```python
import functools

import jax
import jax.numpy as jnp
from jax import lax
from jax.experimental import pallas as pl
from jax.experimental.pallas import tpu as pltpu
from jax.sharding import Mesh, PartitionSpec as P

HW = 64
ROWS = ("z", "y", "core")
F32 = jnp.float32
BF16 = jnp.bfloat16
VMEM_SPEC = pl.BlockSpec(memory_space=pltpu.VMEM)
ANY_SPEC = pl.BlockSpec(memory_space=pl.ANY)
SMEM_SPEC = pl.BlockSpec(memory_space=pltpu.SMEM)


def call(kernel, out_shape, in_specs, scratch=(), mib=4):
    outs = jax.tree.map(lambda _: VMEM_SPEC, out_shape)
    return pl.pallas_call(
        kernel,
        out_shape=out_shape,
        in_specs=in_specs,
        out_specs=outs,
        scratch_shapes=scratch,
        compiler_params=pltpu.CompilerParams(vmem_limit_bytes=mib << 20),
    )


def shape(dims, dtype):
    return jax.ShapeDtypeStruct(dims, dtype)


def product_kernel(copies, index, *refs):
    pieces, (ham, out, tiles) = refs[:5], refs[5:]
    vecs = ham.shape[1]
    half = lax.broadcasted_iota(jnp.int16, (vecs, 128), 1) < jnp.int16(64)
    for p, piece in enumerate(pieces):
        for u in range(2):
            base = 32 * p + 16 * u
            start = here = piece[u, :, :128]
            for t in range(8):
                after = start if t == 7 else piece[u, :, 128 * (t + 1) : 128 * (t + 2)]
                tiles[base + 2 * t] = here
                tiles[base + 2 * t + 1] = pltpu.roll(jnp.where(half, after, here), 64, 1)
                here = after
    tiles[160] = jnp.zeros((vecs, 128), BF16)
    pairs = ham.shape[2] // 128

    def picked(row):
        return jnp.concatenate(
            [
                jnp.where(half, tiles[index[row, 2 * s]], tiles[index[row, 2 * s + 1]])
                for s in range(pairs)
            ],
            axis=1,
        )

    def two_rows(m, carry):
        sums = []
        for k in range(2):
            row = 2 * m + k
            sums.append(
                lax.dot_general(
                    picked(row), ham[row], (((1,), (1,)), ((), ())), preferred_element_type=F32
                )
            )
        both = jnp.concatenate(sums, axis=1).astype(BF16)
        lanes = pl.ds(pl.multiple_of(m * 128, 128), 128)
        for c in range(copies):
            out[c, :, lanes] = both
        return carry

    lax.fori_loop(0, ham.shape[0] // 2, two_rows, 0, unroll=4)


def index_kernel(total_blocks, block_rows, columns, counts, ham, out):
    core, blk = lax.axis_index("core"), lax.axis_index("blk")
    chip = lax.axis_index("z") * lax.axis_size("y") + lax.axis_index("y")
    slot = lax.broadcasted_iota(jnp.int32, columns.shape, 1)
    live = slot + blk * columns.shape[1] < counts[...]
    offset = (columns[...] - (chip - 2) * 2 * block_rows) & (total_blocks - 1)
    away, block = offset >> 5, offset & 15
    place = jnp.where(core == 0, away, 4 - away) * 32 + (offset & 16)
    tile = place + jnp.where((slot & 1) == 0, block, (block + 15) & 15)
    out[...] = jnp.where(live, tile, 160)


def first_kernel(parts, out):
    total = parts[0].astype(F32)
    for b in range(1, 4):
        total += parts[b].astype(F32)
    out[...] = total.astype(BF16)


def pair_kernel(mine, other, out):
    core = lax.axis_index("core")
    out[core] = mine[...]
    out[1 - core] = other[...]


STRIPS = ((7, 6, 0), (5, 4, 3), (2, 1))


def pack(g):
    lane = lax.broadcasted_iota(jnp.int32, (8, 128), 1)
    rows = []
    for group in STRIPS:
        at, line = 0, jnp.zeros((8, 128), F32)
        for i in group:
            wide = jnp.concatenate([g[8 * i : 8 * i + 8], jnp.zeros((8, 64), F32)], axis=1)
            moved = pltpu.roll(wide, at, 1) if at else wide
            line = jnp.where((lane >= at) & (lane < at + 8 * i + 8), moved, line)
            at += 8 * i + 8
        rows.append(line)
    return jnp.concatenate(rows, axis=0)


def unpack(packed):
    strips = [None] * 8
    for q, group in enumerate(STRIPS):
        at, line = 0, packed[8 * q : 8 * q + 8]
        for i in group:
            strips[i] = (pltpu.roll(line, 128 - at, 1) if at else line)[:, :64]
            at += 8 * i + 8
    low = jnp.concatenate(strips, axis=0)
    row = lax.broadcasted_iota(jnp.int32, (64, 64), 0) // 8
    col = lax.broadcasted_iota(jnp.int32, (64, 64), 1) // 8
    return jnp.where(col <= row, low, low.T)


def gram_kernel(parts, own, filtered, gram):
    total = parts[0].astype(F32)
    for b in range(1, 4):
        total += parts[b].astype(F32)
    value = (2.0 * total - own[lax.axis_index("core")].astype(F32)).astype(BF16)
    filtered[...] = value
    g = lax.dot_general(value, value, (((1,), (1,)), ((), ())), preferred_element_type=F32)
    packed = pack(g)
    for c in range(gram.shape[0]):
        gram[c] = packed


def sum_kernel(parts, out):
    total = parts[0]
    for c in range(1, parts.shape[0]):
        total += parts[c]
    for c in range(out.shape[0]):
        out[c] = total


def factor_kernel(scale, parts, filtered, basis, factor, scratch):
    total = parts[0]
    for c in range(1, 8):
        total += parts[c]
    whole = unpack(total * scale)
    lane = lax.broadcasted_iota(jnp.int32, (8, 128), 1)
    sub = lax.broadcasted_iota(jnp.int32, (8, 128), 0)
    zero = jnp.zeros((8, 64), F32)
    chunks = []
    for c in range(8):
        eye = jnp.where(lane - 64 == sub + 8 * c, F32(1.0), F32(0.0))
        wide = jnp.concatenate([whole[8 * c : 8 * c + 8], zero], axis=1)
        chunks.append(jnp.where(lane < 64, wide, eye))

    def spread(chunk, k):
        value = jnp.sum(jnp.where(lane == k, chunk, F32(0.0)), axis=1, keepdims=True)
        return jnp.broadcast_to(value, (8, 128))

    def down(value, r):
        return jnp.broadcast_to(value[r : r + 1], (8, 128))

    for b in range(8):
        cols = {c: [spread(chunks[c], 8 * b + j) for j in range(8)] for c in range(b, 8)}
        for r in range(8):
            row = down(chunks[b], r)
            heads = [down(cols[b][j], r) for j in range(r, 8)]
            inv = 1.0 / heads[0]
            for c in range(b if r < 7 else b + 1, 8):
                times = cols[c][r] * inv
                if c == b:
                    times = jnp.where(sub > r, times, F32(0.0))
                chunks[c] = chunks[c] - times * row
                for j in range(r + 1, 8):
                    cols[c][j] = cols[c][j] - times * heads[j - r]
    for c in range(8):
        pivot = jnp.where(lane == sub + 8 * c, chunks[c], F32(0.0))
        root = 1.0 / jnp.sqrt(jnp.sum(pivot, axis=1, keepdims=True))
        scaled = chunks[c] * root
        keep = jnp.where(lane >= sub + 8 * c, scaled, F32(0.0))
        factor[8 * c : 8 * c + 8, :] = keep[:, :64]
        scratch[8 * c : 8 * c + 8, :] = scaled[:, 64:]
    mine = scratch[pl.ds(pl.multiple_of(lax.axis_index("blk") * 16, 16), 16), :]
    total = jnp.zeros(basis.shape, F32)
    rest = mine
    parts = []
    for _ in range(3):
        top = rest.astype(BF16)
        parts.append(top)
        rest = rest - top.astype(F32)
    for top in reversed(parts):
        total += jnp.dot(top, filtered[...], preferred_element_type=F32)
    basis[...] = total


def from_chip(value, distance):
    chips = lax.axis_size("z") * lax.axis_size("y")
    pairs = []
    for c in range(chips):
        pairs.append((2 * ((c - distance) % chips), 2 * c))
        pairs.append((2 * ((c + distance) % chips) + 1, 2 * c + 1))
    return lax.ppermute(value, ROWS, pairs)


def flip(value):
    return lax.ppermute(value, "core", [(0, 1), (1, 0)])


def window(pair, beside=None):
    near = from_chip(pair, 1)
    far = from_chip(pair, 2)
    if beside is not None:
        near, beside = lax.optimization_barrier((near, beside))
    far_other = flip(far)
    near_other = flip(near)
    return (far, near, pair, near_other, far_other), beside


def to_all(value, axes, count):
    return lax.all_to_all(
        jnp.broadcast_to(value[None], (count,) + value.shape), axes, 0, 0, tiled=True
    )


def body(vectors, hamiltonian, column_index, counts):
    block_rows = counts.shape[0]
    width = hamiltonian.shape[1]
    vecs = width
    total_blocks = block_rows * lax.axis_size(ROWS)
    index = call(
        functools.partial(index_kernel, total_blocks, block_rows),
        shape(column_index.shape, jnp.int32),
        [VMEM_SPEC] * 2 + [ANY_SPEC],
    )(column_index, counts.reshape(block_rows, 1), hamiltonian)

    def products(pieces, index, copies):
        return call(
            functools.partial(product_kernel, copies),
            shape((copies, vecs, block_rows * width), BF16),
            [SMEM_SPEC] + [VMEM_SPEC] * 6,
            [pltpu.VMEM((161, vecs, 128), BF16)],
            12,
        )(index, *pieces, hamiltonian)

    pair = to_all(vectors, ("core", "blk"), 8).reshape(2, vecs, block_rows * width)
    pieces, index = window(pair, index)
    parts = products(pieces, index, 4)
    parts = lax.all_to_all(parts, "blk", 0, 0, tiled=True)
    unit = shape((vecs, block_rows * width), BF16)
    first = call(first_kernel, unit, [VMEM_SPEC])(parts)
    pair_two = call(pair_kernel, shape(pair.shape, BF16), [VMEM_SPEC] * 2)(first, flip(first))
    parts = products(window(pair_two)[0], index, 4)
    parts = lax.all_to_all(parts, "blk", 0, 0, tiled=True)
    filtered, gram = call(
        gram_kernel,
        (unit, shape((16, 24, 128), F32)),
        [VMEM_SPEC] * 2,
    )(parts, pair)
    gram = lax.all_to_all(gram, ("y", "core"), 0, 0, tiled=True)
    gram = call(sum_kernel, shape((8, 24, 128), F32), [VMEM_SPEC])(gram)
    gram = lax.all_to_all(gram, "z", 0, 0, tiled=True)
    basis, factor = call(
        functools.partial(factor_kernel, 1.0 / (total_blocks * width)),
        (shape(vectors.shape, F32), shape((vecs, vecs), F32)),
        [VMEM_SPEC] * 2,
        [pltpu.VMEM((vecs, vecs), F32)],
    )(gram, filtered)
    return basis, factor


def solution(mesh):
    chips = mesh.shape["rows"] // 2
    y = 8
    fine = Mesh(
        mesh.devices.reshape(chips // y, y, 2, mesh.shape["blk"]), ("z", "y", "core", "blk")
    )
    in_specs = (P("blk", ROWS), P(ROWS, None, "blk"), P(ROWS, "blk"), P(ROWS))
    out_specs = (P("blk", ROWS), P())
    return jax.shard_map(body, mesh=fine, in_specs=in_specs, out_specs=out_specs, check_vma=False)
```

time: 143 us -> 128 us (0.90)
  Pallas kernels: 18.4 us -> 9.36 us
  blocking collectives: 67.5 us -> 65.3 us
  starting transfers between devices: 43.1 us -> 41.5 us
    pallas_call x1, Pallas kernels: 9.14 us -> 2.63 us  [body(): call(functools.partial(factor_kernel, 1.0 / (total_blocks * width)), (sha...]
    pallas_call x2, Pallas kernels: 8.96 us -> 6.23 us  [products(): call(functools.partial(product_kernel, copies), shape((copies, vecs, bloc...]
    ppermute x5, starting transfers between devices: 19.6 us -> 18 us  [flip(): return lax.ppermute(value, 'core', [(0, 1), (1, 0)])]
    unnamed x4 -> x6, local copies, waits for them, and re-layouts: 4.52 us -> 2.96 us
    all_to_all x1, blocking collectives: 15.4 us -> 13.9 us  [body(): gram = lax.all_to_all(gram, ('y', 'core'), 0, 0, tiled=True)]
where the time goes in v3:
time: 128 us
  blocking collectives  65.3 us (51%)
  starting transfers between devices  41.5 us (32%)
  Pallas kernels  9.36 us (7%)
  waiting for transfers between devices  6.24 us (5%)
  local copies, waits for them, and re-layouts  4.47 us (3%)
    ppermute x4, starting transfers between devices, from_chip(): return lax.ppermute(value, ROWS, pairs)  23.5 us
    all_to_all x2, blocking collectives, body(): parts = lax.all_to_all(parts, 'blk', 0, 0, tiled=True)  23.4 us
    ppermute x5, starting transfers between devices, flip(): return lax.ppermute(value, 'core', [(0, 1), (1, 0)])  18 us
    all_to_all x1, blocking collectives, to_all(): lax.all_to_all(jnp.broadcast_to(value[None], (count,) + value.shape), axe...  15.8 us
    all_to_all x1, blocking collectives, body(): gram = lax.all_to_all(gram, ('y', 'core'), 0, 0, tiled=True)  13.9 us
    all_to_all x1, blocking collectives, body(): gram = lax.all_to_all(gram, 'z', 0, 0, tiled=True)  12.2 us
    pallas_call x2, Pallas kernels, products(): call(functools.partial(product_kernel, copies), shape((copies, vecs, bloc...  6.23 us
    ppermute x5, waiting for transfers between devices, flip(): return lax.ppermute(value, 'core', [(0, 1), (1, 0)])  3.59 us
  transfers between devices with their start and end apart: 9, of which 6 were waited for; matrix products, arithmetic and copies ran while one was open for 1% of the time, Pallas kernels for 0%

profile of v3, /device:TPU:1, one launch (start us, length us, event | category | flops | bytes accessed | tf_op | source)
XLA Modules:
  0.0 127.6 jit_solution(8162155355581526246)
XLA Ops:
  0.6 0.8 broadcast_in_dim.2
  1.4 15.8 %all_to_all.25 = bf16[8,16,1024]{2,1,0:T(8,128)(2,1)S(1)} all-to-all(bf16[8,16,1024]{2,1,0:T(8,128)(2,1)S(1)} %broadcast_in_dim.2), channel_id=1, replica_groups=mesh['z'=8,'y'=8,'core'=2,'blk'=4] {'core','blk'}, dimensions={0} | all-to-all | bytes 524288 | tf_op jit(solution)/shard_map/all_to_all | solution.py:231
  17.2 9.9 %collective-permute-start = (bf16[2,64,1024]{2,1,0:T(8,128)(2,1)S(1)}, bf16[2,64,1024]{2,1,0:T(8,128)(2,1)S(1)}, u32[]{:S(2)}, u32[]{:S(2)}) collective-permute-start(bf16[2,64,1024]{2,1,0:T(8,128)(2,1)S(1)} %bitcast.2), channel_id=1, source_target_pairs={{504,0},{12,4},{0,8},{20,12},{8,16},{28,20},{16,24},{36,28},{24,32... | collective-permute-start | bytes 786440 | tf_op jit(solution)/shard_map/ppermute | solution.py:213
  27.1 3.8 %collective-permute-start.1 = (bf16[2,64,1024]{2,1,0:T(8,128)(2,1)S(1)}, bf16[2,64,1024]{2,1,0:T(8,128)(2,1)S(1)}, u32[]{:S(2)}, u32[]{:S(2)}) collective-permute-start(bf16[2,64,1024]{2,1,0:T(8,128)(2,1)S(1)} %bitcast.3), channel_id=1, source_target_pairs={{496,0},{20,4},{504,8},{28,12},{0,16},{36,20},{8,24},{44,28},{16,3... | collective-permute-start | bytes 786440 | tf_op jit(solution)/shard_map/ppermute | solution.py:213
  30.9 0.7 copy.6.counts
  31.6 0.0 copy-start
  31.6 2.3 %copy-done = bf16[16,64,2176]{2,1,0:T(8,128)(2,1)S(1)} copy-done((bf16[16,64,2176]{2,1,0:T(8,128)(2,1)S(1)}, bf16[16,64,2176]{2,1,0:T(8,128)(2,1)}, u32[]{:S(2)}) %copy-start) | copy-done | bytes 4456472
  33.9 0.0 copy-start.2
  33.9 0.7 copy-done.2
  34.6 0.0 copy-start.1
  34.6 0.1 shard_map.59.index
  34.6 0.0 collective-permute-done.refs_1_
  34.6 0.8 collective-permute-done.1.refs_0_
  35.5 3.6 %collective-permute-start.3 = (bf16[2,64,1024]{2,1,0:T(8,128)(2,1)S(1)}, bf16[2,64,1024]{2,1,0:T(8,128)(2,1)S(1)}, u32[]{:S(2)}, u32[]{:S(2)}) collective-permute-start(bf16[2,64,1024]{2,1,0:T(8,128)(2,1)S(1)} %collective-permute-done.1.refs_0_), channel_id=1, source_target_pairs={{0,4},{4,0},{1,5},{5,1},{2,6},{6,2},{3,7},{7,3},{8,12},{12,8},{9,1... | collective-permute-start | bytes 786440 | tf_op jit(solution)/shard_map/ppermute | solution.py:217
  39.1 1.9 %collective-permute-start.2 = (bf16[2,64,1024]{2,1,0:T(8,128)(2,1)S(1)}, bf16[2,64,1024]{2,1,0:T(8,128)(2,1)S(1)}, u32[]{:S(2)}, u32[]{:S(2)}) collective-permute-start(bf16[2,64,1024]{2,1,0:T(8,128)(2,1)S(1)} %collective-permute-done.refs_1_), channel_id=1, source_target_pairs={{0,4},{4,0},{1,5},{5,1},{2,6},{6,2},{3,7},{7,3},{8,12},{12,8},{9,1... | collective-permute-start | bytes 786440 | tf_op jit(solution)/shard_map/ppermute | solution.py:217
  41.0 0.0 collective-permute-done.3.refs_4_
  41.0 1.5 %collective-permute-done.2.refs_3_ = bf16[2,64,1024]{2,1,0:T(8,128)(2,1)S(1)} collective-permute-done((bf16[2,64,1024]{2,1,0:T(8,128)(2,1)S(1)}, bf16[2,64,1024]{2,1,0:T(8,128)(2,1)S(1)}, u32[]{:S(2)}, u32[]{:S(2)}) %collective-permute-start.2) | collective-permute-done | bytes 262176 | tf_op jit(solution)/shard_map/ppermute | solution.py:217
  42.5 0.0 copy-done.1
  42.5 3.1 %shard_map.60 = bf16[4,64,1024]{2,1,0:T(8,128)(2,1)S(1)} custom-call(s32[16,34]{1,0:T(8,128)S(1)} %shard_map.59.index, bf16[2,64,1024]{2,1,0:T(8,128)(2,1)S(1)} %collective-permute-done.1.refs_0_, bf16[2,64,1024]{2,1,0:T(8,128)(2,1)S(1)} %collective-permute-done.refs_1_, bf16[2,64,1024]{2,1,0:T(8,128)(2,1)S(1)} %bitcast.4, ...), custom_call_target="tpu_custom_call" | custom-call | tf_op jit(solution)/shard_map/pallas_call | solution.py:248
  45.7 11.8 %all_to_all.26.parts = bf16[4,64,1024]{2,1,0:T(8,128)(2,1)S(1)} all-to-all(bf16[4,64,1024]{2,1,0:T(8,128)(2,1)S(1)} %shard_map.60), channel_id=1, replica_groups=mesh['z'=8,'y'=8,'core'=2,'blk'=4] {'blk'}, dimensions={0} | all-to-all | bytes 1048576 | tf_op jit(solution)/shard_map/all_to_all | solution.py:259
  57.4 0.1 shard_map.61.mine
  57.5 3.2 %collective-permute-start.4 = (bf16[64,1024]{1,0:T(8,128)(2,1)S(1)}, bf16[64,1024]{1,0:T(8,128)(2,1)S(1)}, u32[]{:S(2)}, u32[]{:S(2)}) collective-permute-start(bf16[64,1024]{1,0:T(8,128)(2,1)S(1)} %shard_map.61.mine), channel_id=1, source_target_pairs={{0,4},{4,0},{1,5},{5,1},{2,6},{6,2},{3,7},{7,3},{8,12},{12,8},{9,1... | collective-permute-start | bytes 393224 | tf_op jit(solution)/shard_map/ppermute | solution.py:217
  60.7 1.0 collective-permute-done.4.other
  61.7 7.0 %collective-permute-start.6 = (bf16[2,64,1024]{2,1,0:T(8,128)(2,1)S(1)}, bf16[2,64,1024]{2,1,0:T(8,128)(2,1)S(1)}, u32[]{:S(2)}, u32[]{:S(2)}) collective-permute-start(bf16[2,64,1024]{2,1,0:T(8,128)(2,1)S(1)} %shard_map.62.refs_2_), channel_id=1, source_target_pairs={{504,0},{12,4},{0,8},{20,12},{8,16},{28,20},{16,24},{36,28},{24,32... | collective-permute-start | bytes 786440 | tf_op jit(solution)/shard_map/ppermute | solution.py:213
  68.6 2.9 %collective-permute-start.5 = (bf16[2,64,1024]{2,1,0:T(8,128)(2,1)S(1)}, bf16[2,64,1024]{2,1,0:T(8,128)(2,1)S(1)}, u32[]{:S(2)}, u32[]{:S(2)}) collective-permute-start(bf16[2,64,1024]{2,1,0:T(8,128)(2,1)S(1)} %shard_map.62.refs_2_), channel_id=1, source_target_pairs={{496,0},{20,4},{504,8},{28,12},{0,16},{36,20},{8,24},{44,28},{16,3... | collective-permute-start | bytes 786440 | tf_op jit(solution)/shard_map/ppermute | solution.py:213
  71.6 0.4 collective-permute-done.6.refs_1_
  71.9 3.6 %collective-permute-start.7 = (bf16[2,64,1024]{2,1,0:T(8,128)(2,1)S(1)}, bf16[2,64,1024]{2,1,0:T(8,128)(2,1)S(1)}, u32[]{:S(2)}, u32[]{:S(2)}) collective-permute-start(bf16[2,64,1024]{2,1,0:T(8,128)(2,1)S(1)} %collective-permute-done.6.refs_1_), channel_id=1, source_target_pairs={{0,4},{4,0},{1,5},{5,1},{2,6},{6,2},{3,7},{7,3},{8,12},{12,8},{9,1... | collective-permute-start | bytes 786440 | tf_op jit(solution)/shard_map/ppermute | solution.py:217
  75.5 1.5 %collective-permute-done.5.refs_0_ = bf16[2,64,1024]{2,1,0:T(8,128)(2,1)S(1)} collective-permute-done((bf16[2,64,1024]{2,1,0:T(8,128)(2,1)S(1)}, bf16[2,64,1024]{2,1,0:T(8,128)(2,1)S(1)}, u32[]{:S(2)}, u32[]{:S(2)}) %collective-permute-start.5) | collective-permute-done | bytes 262176 | tf_op jit(solution)/shard_map/ppermute | solution.py:213
  77.0 5.6 %collective-permute-start.8 = (bf16[2,64,1024]{2,1,0:T(8,128)(2,1)S(1)}, bf16[2,64,1024]{2,1,0:T(8,128)(2,1)S(1)}, u32[]{:S(2)}, u32[]{:S(2)}) collective-permute-start(bf16[2,64,1024]{2,1,0:T(8,128)(2,1)S(1)} %collective-permute-done.5.refs_0_), channel_id=1, source_target_pairs={{0,4},{4,0},{1,5},{5,1},{2,6},{6,2},{3,7},{7,3},{8,12},{12,8},{9,1... | collective-permute-start | bytes 786440 | tf_op jit(solution)/shard_map/ppermute | solution.py:217
  82.6 0.0 collective-permute-done.7.refs_3_
  82.6 1.1 collective-permute-done.8.refs_4_
  83.8 3.1 %shard_map.63 = bf16[4,64,1024]{2,1,0:T(8,128)(2,1)S(1)} custom-call(s32[16,34]{1,0:T(8,128)S(1)} %shard_map.59.index, bf16[2,64,1024]{2,1,0:T(8,128)(2,1)S(1)} %collective-permute-done.5.refs_0_, bf16[2,64,1024]{2,1,0:T(8,128)(2,1)S(1)} %collective-permute-done.6.refs_1_, bf16[2,64,1024]{2,1,0:T(8,128)(2,1)S(1)} %shard_map.62.refs_2_, ...), custom_call_target="tpu_custom_call" | custom-call | tf_op jit(solution)/shard_map/pallas_call | solution.py:248
  86.9 11.6 %all_to_all.27.parts = bf16[4,64,1024]{2,1,0:T(8,128)(2,1)S(1)} all-to-all(bf16[4,64,1024]{2,1,0:T(8,128)(2,1)S(1)} %shard_map.63), channel_id=1, replica_groups=mesh['z'=8,'y'=8,'core'=2,'blk'=4] {'blk'}, dimensions={0} | all-to-all | bytes 1048576 | tf_op jit(solution)/shard_map/all_to_all | solution.py:264
  98.5 0.3 shard_map.64
  98.8 13.9 %all_to_all.28.parts = f32[16,24,128]{2,1,0:T(8,128)S(1)} all-to-all(f32[16,24,128]{2,1,0:T(8,128)S(1)} %get-tuple-element.8), channel_id=1, replica_groups=mesh['z'=8,'y'=8,'core'=2,'blk'=4] {'y','core'}, dimensions={0} | all-to-all | bytes 393216 | tf_op jit(solution)/shard_map/all_to_all | solution.py:270
  112.7 12.2 %all_to_all.29.parts = f32[8,24,128]{2,1,0:T(8,128)S(1)} all-to-all(f32[8,24,128]{2,1,0:T(8,128)S(1)} %shard_map.65), channel_id=1, replica_groups=mesh['z'=8,'y'=8,'core'=2,'blk'=4] {'z'}, dimensions={0} | all-to-all | bytes 196608 | tf_op jit(solution)/shard_map/all_to_all | solution.py:272
  125.0 2.6 %shard_map.66 = (f32[16,1024]{1,0:T(8,128)}, f32[64,64]{1,0:T(8,128)}) custom-call(f32[8,24,128]{2,1,0:T(8,128)S(1)} %all_to_all.29.parts, bf16[64,1024]{1,0:T(8,128)(2,1)S(1)} %get-tuple-element.9.filtered), custom_call_target="tpu_custom_call" | custom-call | tf_op jit(solution)/shard_map/pallas_call | solution.py:273
  (2 shorter events, 0.1 us)
Async XLA Ops:
  17.2 17.5 %collective-permute-start = (bf16[2,64,1024]{2,1,0:T(8,128)(2,1)S(1)}, bf16[2,64,1024]{2,1,0:T(8,128)(2,1)S(1)}, u32[]{:S(2)}, u32[]{:S(2)}) collective-permute-start(bf16[2,64,1024]{2,1,0:T(8,128)(2,1)S(1)} %bitcast.2), channel_id=1, source_target_pairs={{504,0},{12,4},{0,8},{20,12},{8,16},{28,20},{16,24},{36,28},{24,32... | collective-permute-start | bytes 786440 | tf_op jit(solution)/shard_map/ppermute | solution.py:213
  27.1 8.4 %collective-permute-start.1 = (bf16[2,64,1024]{2,1,0:T(8,128)(2,1)S(1)}, bf16[2,64,1024]{2,1,0:T(8,128)(2,1)S(1)}, u32[]{:S(2)}, u32[]{:S(2)}) collective-permute-start(bf16[2,64,1024]{2,1,0:T(8,128)(2,1)S(1)} %bitcast.3), channel_id=1, source_target_pairs={{496,0},{20,4},{504,8},{28,12},{0,16},{36,20},{8,24},{44,28},{16,3... | collective-permute-start | bytes 786440 | tf_op jit(solution)/shard_map/ppermute | solution.py:213
  31.6 2.3 %copy-start = (bf16[16,64,2176]{2,1,0:T(8,128)(2,1)S(1)}, bf16[16,64,2176]{2,1,0:T(8,128)(2,1)}, u32[]{:S(2)}) copy-start(bf16[16,64,2176]{2,1,0:T(8,128)(2,1)} %refs_5_.3) | copy-start | bytes 13369348
  33.9 0.7 copy-start.2
  34.6 8.0 %copy-start.1 = (bf16[16,64,2176]{2,1,0:T(8,128)(2,1)S(1)}, bf16[16,64,2176]{2,1,0:T(8,128)(2,1)}, u32[]{:S(2)}) copy-start(bf16[16,64,2176]{2,1,0:T(8,128)(2,1)} %refs_5_.3) | copy-start | bytes 13369348
  35.5 5.6 %collective-permute-start.3 = (bf16[2,64,1024]{2,1,0:T(8,128)(2,1)S(1)}, bf16[2,64,1024]{2,1,0:T(8,128)(2,1)S(1)}, u32[]{:S(2)}, u32[]{:S(2)}) collective-permute-start(bf16[2,64,1024]{2,1,0:T(8,128)(2,1)S(1)} %collective-permute-done.1.refs_0_), channel_id=1, source_target_pairs={{0,4},{4,0},{1,5},{5,1},{2,6},{6,2},{3,7},{7,3},{8,12},{12,8},{9,1... | collective-permute-start | bytes 786440 | tf_op jit(solution)/shard_map/ppermute | solution.py:217
  39.1 3.4 %collective-permute-start.2 = (bf16[2,64,1024]{2,1,0:T(8,128)(2,1)S(1)}, bf16[2,64,1024]{2,1,0:T(8,128)(2,1)S(1)}, u32[]{:S(2)}, u32[]{:S(2)}) collective-permute-start(bf16[2,64,1024]{2,1,0:T(8,128)(2,1)S(1)} %collective-permute-done.refs_1_), channel_id=1, source_target_pairs={{0,4},{4,0},{1,5},{5,1},{2,6},{6,2},{3,7},{7,3},{8,12},{12,8},{9,1... | collective-permute-start | bytes 786440 | tf_op jit(solution)/shard_map/ppermute | solution.py:217
  57.5 4.2 %collective-permute-start.4 = (bf16[64,1024]{1,0:T(8,128)(2,1)S(1)}, bf16[64,1024]{1,0:T(8,128)(2,1)S(1)}, u32[]{:S(2)}, u32[]{:S(2)}) collective-permute-start(bf16[64,1024]{1,0:T(8,128)(2,1)S(1)} %shard_map.61.mine), channel_id=1, source_target_pairs={{0,4},{4,0},{1,5},{5,1},{2,6},{6,2},{3,7},{7,3},{8,12},{12,8},{9,1... | collective-permute-start | bytes 393224 | tf_op jit(solution)/shard_map/ppermute | solution.py:217
  61.7 10.3 %collective-permute-start.6 = (bf16[2,64,1024]{2,1,0:T(8,128)(2,1)S(1)}, bf16[2,64,1024]{2,1,0:T(8,128)(2,1)S(1)}, u32[]{:S(2)}, u32[]{:S(2)}) collective-permute-start(bf16[2,64,1024]{2,1,0:T(8,128)(2,1)S(1)} %shard_map.62.refs_2_), channel_id=1, source_target_pairs={{504,0},{12,4},{0,8},{20,12},{8,16},{28,20},{16,24},{36,28},{24,32... | collective-permute-start | bytes 786440 | tf_op jit(solution)/shard_map/ppermute | solution.py:213
  68.6 8.4 %collective-permute-start.5 = (bf16[2,64,1024]{2,1,0:T(8,128)(2,1)S(1)}, bf16[2,64,1024]{2,1,0:T(8,128)(2,1)S(1)}, u32[]{:S(2)}, u32[]{:S(2)}) collective-permute-start(bf16[2,64,1024]{2,1,0:T(8,128)(2,1)S(1)} %shard_map.62.refs_2_), channel_id=1, source_target_pairs={{496,0},{20,4},{504,8},{28,12},{0,16},{36,20},{8,24},{44,28},{16,3... | collective-permute-start | bytes 786440 | tf_op jit(solution)/shard_map/ppermute | solution.py:213
  71.9 10.7 %collective-permute-start.7 = (bf16[2,64,1024]{2,1,0:T(8,128)(2,1)S(1)}, bf16[2,64,1024]{2,1,0:T(8,128)(2,1)S(1)}, u32[]{:S(2)}, u32[]{:S(2)}) collective-permute-start(bf16[2,64,1024]{2,1,0:T(8,128)(2,1)S(1)} %collective-permute-done.6.refs_1_), channel_id=1, source_target_pairs={{0,4},{4,0},{1,5},{5,1},{2,6},{6,2},{3,7},{7,3},{8,12},{12,8},{9,1... | collective-permute-start | bytes 786440 | tf_op jit(solution)/shard_map/ppermute | solution.py:217
  77.0 6.8 %collective-permute-start.8 = (bf16[2,64,1024]{2,1,0:T(8,128)(2,1)S(1)}, bf16[2,64,1024]{2,1,0:T(8,128)(2,1)S(1)}, u32[]{:S(2)}, u32[]{:S(2)}) collective-permute-start(bf16[2,64,1024]{2,1,0:T(8,128)(2,1)S(1)} %collective-permute-done.5.refs_0_), channel_id=1, source_target_pairs={{0,4},{4,0},{1,5},{5,1},{2,6},{6,2},{3,7},{7,3},{8,12},{12,8},{9,1... | collective-permute-start | bytes 786440 | tf_op jit(solution)/shard_map/ppermute | solution.py:217

commit v4 on v3

--- a/solution.py
+++ b/solution.py
@@ -7,7 +7,6 @@
 from jax.experimental.pallas import tpu as pltpu
 from jax.sharding import Mesh, PartitionSpec as P
 
-HW = 64
 ROWS = ("z", "y", "core")
 F32 = jnp.float32
 BF16 = jnp.bfloat16
@@ -217,14 +216,12 @@
     return lax.ppermute(value, "core", [(0, 1), (1, 0)])
 
 
-def window(pair, beside=None):
+def window(pair):
     near = from_chip(pair, 1)
-    far = from_chip(pair, 2)
-    if beside is not None:
-        near, beside = lax.optimization_barrier((near, beside))
+    far = from_chip(pair, -2)
+    near_other = flip(near)
     far_other = flip(far)
-    near_other = flip(near)
-    return (far, near, pair, near_other, far_other), beside
+    return far_other, near, pair, near_other, far
 
 
 def to_all(value, axes, count):
@@ -233,7 +230,7 @@
     )
 
 
-def body(vectors, hamiltonian, column_index, counts):
+def program(vectors, hamiltonian, column_index, counts):
     block_rows = counts.shape[0]
     width = hamiltonian.shape[1]
     vecs = width
@@ -244,7 +241,7 @@
         [VMEM_SPEC] * 2 + [ANY_SPEC],
     )(column_index, counts.reshape(block_rows, 1), hamiltonian)
 
-    def products(pieces, index, copies):
+    def products(pieces, copies):
         return call(
             functools.partial(product_kernel, copies),
             shape((copies, vecs, block_rows * width), BF16),
@@ -254,13 +251,12 @@
         )(index, *pieces, hamiltonian)
 
     pair = to_all(vectors, ("core", "blk"), 8).reshape(2, vecs, block_rows * width)
-    pieces, index = window(pair, index)
-    parts = products(pieces, index, 4)
+    parts = products(window(pair), 4)
     parts = lax.all_to_all(parts, "blk", 0, 0, tiled=True)
     unit = shape((vecs, block_rows * width), BF16)
     first = call(first_kernel, unit, [VMEM_SPEC])(parts)
     pair_two = call(pair_kernel, shape(pair.shape, BF16), [VMEM_SPEC] * 2)(first, flip(first))
-    parts = products(window(pair_two)[0], index, 4)
+    parts = products(window(pair_two), 4)
     parts = lax.all_to_all(parts, "blk", 0, 0, tiled=True)
     filtered, gram = call(
         gram_kernel,
@@ -287,4 +283,4 @@
     )
     in_specs = (P("blk", ROWS), P(ROWS, None, "blk"), P(ROWS, "blk"), P(ROWS))
     out_specs = (P("blk", ROWS), P())
-    return jax.shard_map(body, mesh=fine, in_specs=in_specs, out_specs=out_specs, check_vma=False)
+    return jax.shard_map(program, mesh=fine, in_specs=in_specs, out_specs=out_specs, check_vma=False)

time: 128 us -> 132 us (1.031)
  waiting for transfers between devices: 6.24 us -> 13.1 us
  starting transfers between devices: 41.5 us -> 36.1 us
  local copies, waits for them, and re-layouts: 4.47 us -> 6.65 us
    ppermute x4, waiting for transfers between devices: 2.65 us -> 10.7 us  [from_chip(): return lax.ppermute(value, ROWS, pairs)]
    ppermute x4, starting transfers between devices: 23.5 us -> 15.7 us  [from_chip(): return lax.ppermute(value, ROWS, pairs)]
    ppermute x5, starting transfers between devices: 18 us -> 20.5 us  [flip(): return lax.ppermute(value, 'core', [(0, 1), (1, 0)])]
    unnamed x6, local copies, waits for them, and re-layouts: 2.96 us -> 5.14 us
  transfers between devices with their start and end apart: 9 -> 9, of which waited for: 6 -> 5; matrix products, arithmetic and copies ran while one was open for 1% -> 1% of each run, Pallas kernels for 0% -> 0%
where the time goes in v4:
time: 132 us; the launch traced here: 131 us
  blocking collectives  65.1 us (49%)
  starting transfers between devices  36.1 us (27%)
  waiting for transfers between devices  13.1 us (10%)
  Pallas kernels  9.36 us (7%)
  local copies, waits for them, and re-layouts  6.65 us (5%)
    all_to_all x2, blocking collectives, program(): parts = lax.all_to_all(parts, 'blk', 0, 0, tiled=True)  23.1 us
    ppermute x5, starting transfers between devices, flip(): return lax.ppermute(value, 'core', [(0, 1), (1, 0)])  20.5 us
    all_to_all x1, blocking collectives, to_all(): lax.all_to_all(jnp.broadcast_to(value[None], (count,) + value.shape), axe...  15.8 us
    ppermute x4, starting transfers between devices, from_chip(): return lax.ppermute(value, ROWS, pairs)  15.7 us
    all_to_all x1, blocking collectives, program(): gram = lax.all_to_all(gram, ('y', 'core'), 0, 0, tiled=True)  14.2 us
    all_to_all x1, blocking collectives, program(): gram = lax.all_to_all(gram, 'z', 0, 0, tiled=True)  12 us
    ppermute x4, waiting for transfers between devices, from_chip(): return lax.ppermute(value, ROWS, pairs)  10.7 us
    pallas_call x2, Pallas kernels, products(): call(functools.partial(product_kernel, copies), shape((copies, vecs, bloc...  6.23 us
  transfers between devices with their start and end apart: 9, of which 5 were waited for; matrix products, arithmetic and copies ran while one was open for 1% of the time, Pallas kernels for 0%

profile of v4, /device:TPU:1, one launch (start us, length us, event | category | flops | bytes accessed | tf_op | source)
XLA Modules:
  0.0 131.1 jit_solution(10678145704567185099)
XLA Ops:
  0.6 0.8 broadcast_in_dim.2
  1.4 15.8 %all_to_all.25 = bf16[8,16,1024]{2,1,0:T(8,128)(2,1)S(1)} all-to-all(bf16[8,16,1024]{2,1,0:T(8,128)(2,1)S(1)} %broadcast_in_dim.2), channel_id=1, replica_groups=mesh['z'=8,'y'=8,'core'=2,'blk'=4] {'core','blk'}, dimensions={0} | all-to-all | bytes 524288 | tf_op jit(solution)/shard_map/all_to_all | solution.py:228
  17.2 9.9 %collective-permute-start.2 = (bf16[2,64,1024]{2,1,0:T(8,128)(2,1)S(1)}, bf16[2,64,1024]{2,1,0:T(8,128)(2,1)S(1)}, u32[]{:S(2)}, u32[]{:S(2)}) collective-permute-start(bf16[2,64,1024]{2,1,0:T(8,128)(2,1)S(1)} %bitcast.2), channel_id=1, source_target_pairs={{504,0},{12,4},{0,8},{20,12},{8,16},{28,20},{16,24},{36,28},{24,32... | collective-permute-start | bytes 786440 | tf_op jit(solution)/shard_map/ppermute | solution.py:212
  27.1 1.9 %collective-permute-start = (bf16[2,64,1024]{2,1,0:T(8,128)(2,1)S(1)}, bf16[2,64,1024]{2,1,0:T(8,128)(2,1)S(1)}, u32[]{:S(2)}, u32[]{:S(2)}) collective-permute-start(bf16[2,64,1024]{2,1,0:T(8,128)(2,1)S(1)} %bitcast.3), channel_id=1, source_target_pairs={{16,0},{500,4},{24,8},{508,12},{32,16},{4,20},{40,24},{12,28},{48,... | collective-permute-start | bytes 786440 | tf_op jit(solution)/shard_map/ppermute | solution.py:212
  29.0 1.4 %collective-permute-done.2.refs_1_ = bf16[2,64,1024]{2,1,0:T(8,128)(2,1)S(1)} collective-permute-done((bf16[2,64,1024]{2,1,0:T(8,128)(2,1)S(1)}, bf16[2,64,1024]{2,1,0:T(8,128)(2,1)S(1)}, u32[]{:S(2)}, u32[]{:S(2)}) %collective-permute-start.2) | collective-permute-done | bytes 262176 | tf_op jit(solution)/shard_map/ppermute | solution.py:212
  30.4 3.9 %collective-permute-start.3 = (bf16[2,64,1024]{2,1,0:T(8,128)(2,1)S(1)}, bf16[2,64,1024]{2,1,0:T(8,128)(2,1)S(1)}, u32[]{:S(2)}, u32[]{:S(2)}) collective-permute-start(bf16[2,64,1024]{2,1,0:T(8,128)(2,1)S(1)} %collective-permute-done.2.refs_1_), channel_id=1, source_target_pairs={{0,4},{4,0},{1,5},{5,1},{2,6},{6,2},{3,7},{7,3},{8,12},{12,8},{9,1... | collective-permute-start | bytes 786440 | tf_op jit(solution)/shard_map/ppermute | solution.py:216
  34.3 6.1 %collective-permute-done.refs_4_ = bf16[2,64,1024]{2,1,0:T(8,128)(2,1)S(1)} collective-permute-done((bf16[2,64,1024]{2,1,0:T(8,128)(2,1)S(1)}, bf16[2,64,1024]{2,1,0:T(8,128)(2,1)S(1)}, u32[]{:S(2)}, u32[]{:S(2)}) %collective-permute-start) | collective-permute-done | bytes 262176 | tf_op jit(solution)/shard_map/ppermute | solution.py:212
  40.4 1.9 %collective-permute-start.1 = (bf16[2,64,1024]{2,1,0:T(8,128)(2,1)S(1)}, bf16[2,64,1024]{2,1,0:T(8,128)(2,1)S(1)}, u32[]{:S(2)}, u32[]{:S(2)}) collective-permute-start(bf16[2,64,1024]{2,1,0:T(8,128)(2,1)S(1)} %collective-permute-done.refs_4_), channel_id=1, source_target_pairs={{0,4},{4,0},{1,5},{5,1},{2,6},{6,2},{3,7},{7,3},{8,12},{12,8},{9,1... | collective-permute-start | bytes 786440 | tf_op jit(solution)/shard_map/ppermute | solution.py:216
  42.3 0.7 copy.6.counts
  43.0 0.0 copy-start
  43.0 2.3 %copy-done = bf16[16,64,2176]{2,1,0:T(8,128)(2,1)S(1)} copy-done((bf16[16,64,2176]{2,1,0:T(8,128)(2,1)S(1)}, bf16[16,64,2176]{2,1,0:T(8,128)(2,1)}, u32[]{:S(2)}) %copy-start) | copy-done | bytes 4456472
  45.3 0.0 copy-start.2
  45.3 0.7 copy-done.2
  46.0 0.0 copy-start.1
  46.0 0.1 shard_map.59.index
  46.0 0.0 collective-permute-done.3.refs_3_
  46.0 0.0 collective-permute-done.1.refs_0_
  46.1 2.2 %copy-done.1 = bf16[16,64,2176]{2,1,0:T(8,128)(2,1)S(1)} copy-done((bf16[16,64,2176]{2,1,0:T(8,128)(2,1)S(1)}, bf16[16,64,2176]{2,1,0:T(8,128)(2,1)}, u32[]{:S(2)}) %copy-start.1) | copy-done | bytes 4456472
  48.2 3.1 %shard_map.60 = bf16[4,64,1024]{2,1,0:T(8,128)(2,1)S(1)} custom-call(s32[16,34]{1,0:T(8,128)S(1)} %shard_map.59.index, bf16[2,64,1024]{2,1,0:T(8,128)(2,1)S(1)} %collective-permute-done.1.refs_0_, bf16[2,64,1024]{2,1,0:T(8,128)(2,1)S(1)} %collective-permute-done.2.refs_1_, bf16[2,64,1024]{2,1,0:T(8,128)(2,1)S(1)} %bitcast.4, ...), custom_call_target="tpu_custom_call" | custom-call | tf_op jit(solution)/shard_map/pallas_call | solution.py:245
  51.3 11.5 %all_to_all.26.parts = bf16[4,64,1024]{2,1,0:T(8,128)(2,1)S(1)} all-to-all(bf16[4,64,1024]{2,1,0:T(8,128)(2,1)S(1)} %shard_map.60), channel_id=1, replica_groups=mesh['z'=8,'y'=8,'core'=2,'blk'=4] {'blk'}, dimensions={0} | all-to-all | bytes 1048576 | tf_op jit(solution)/shard_map/all_to_all | solution.py:255
  62.8 0.1 shard_map.61.mine
  62.9 3.3 %collective-permute-start.4 = (bf16[64,1024]{1,0:T(8,128)(2,1)S(1)}, bf16[64,1024]{1,0:T(8,128)(2,1)S(1)}, u32[]{:S(2)}, u32[]{:S(2)}) collective-permute-start(bf16[64,1024]{1,0:T(8,128)(2,1)S(1)} %shard_map.61.mine), channel_id=1, source_target_pairs={{0,4},{4,0},{1,5},{5,1},{2,6},{6,2},{3,7},{7,3},{8,12},{12,8},{9,1... | collective-permute-start | bytes 393224 | tf_op jit(solution)/shard_map/ppermute | solution.py:216
  66.2 1.0 collective-permute-done.4.other
  67.2 1.9 %collective-permute-start.7 = (bf16[2,64,1024]{2,1,0:T(8,128)(2,1)S(1)}, bf16[2,64,1024]{2,1,0:T(8,128)(2,1)S(1)}, u32[]{:S(2)}, u32[]{:S(2)}) collective-permute-start(bf16[2,64,1024]{2,1,0:T(8,128)(2,1)S(1)} %shard_map.62.refs_2_), channel_id=1, source_target_pairs={{504,0},{12,4},{0,8},{20,12},{8,16},{28,20},{16,24},{36,28},{24,32... | collective-permute-start | bytes 786440 | tf_op jit(solution)/shard_map/ppermute | solution.py:212
  69.1 1.9 %collective-permute-start.5 = (bf16[2,64,1024]{2,1,0:T(8,128)(2,1)S(1)}, bf16[2,64,1024]{2,1,0:T(8,128)(2,1)S(1)}, u32[]{:S(2)}, u32[]{:S(2)}) collective-permute-start(bf16[2,64,1024]{2,1,0:T(8,128)(2,1)S(1)} %shard_map.62.refs_2_), channel_id=1, source_target_pairs={{16,0},{500,4},{24,8},{508,12},{32,16},{4,20},{40,24},{12,28},{48,... | collective-permute-start | bytes 786440 | tf_op jit(solution)/shard_map/ppermute | solution.py:212
  71.0 3.3 %collective-permute-done.7.refs_1_ = bf16[2,64,1024]{2,1,0:T(8,128)(2,1)S(1)} collective-permute-done((bf16[2,64,1024]{2,1,0:T(8,128)(2,1)S(1)}, bf16[2,64,1024]{2,1,0:T(8,128)(2,1)S(1)}, u32[]{:S(2)}, u32[]{:S(2)}) %collective-permute-start.7) | collective-permute-done | bytes 262176 | tf_op jit(solution)/shard_map/ppermute | solution.py:212
  74.3 9.5 %collective-permute-start.8 = (bf16[2,64,1024]{2,1,0:T(8,128)(2,1)S(1)}, bf16[2,64,1024]{2,1,0:T(8,128)(2,1)S(1)}, u32[]{:S(2)}, u32[]{:S(2)}) collective-permute-start(bf16[2,64,1024]{2,1,0:T(8,128)(2,1)S(1)} %collective-permute-done.7.refs_1_), channel_id=1, source_target_pairs={{0,4},{4,0},{1,5},{5,1},{2,6},{6,2},{3,7},{7,3},{8,12},{12,8},{9,1... | collective-permute-start | bytes 786440 | tf_op jit(solution)/shard_map/ppermute | solution.py:216
  83.7 0.0 collective-permute-done.5.refs_4_
  83.8 1.9 %collective-permute-start.6 = (bf16[2,64,1024]{2,1,0:T(8,128)(2,1)S(1)}, bf16[2,64,1024]{2,1,0:T(8,128)(2,1)S(1)}, u32[]{:S(2)}, u32[]{:S(2)}) collective-permute-start(bf16[2,64,1024]{2,1,0:T(8,128)(2,1)S(1)} %collective-permute-done.5.refs_4_), channel_id=1, source_target_pairs={{0,4},{4,0},{1,5},{5,1},{2,6},{6,2},{3,7},{7,3},{8,12},{12,8},{9,1... | collective-permute-start | bytes 786440 | tf_op jit(solution)/shard_map/ppermute | solution.py:216
  85.7 0.0 collective-permute-done.8.refs_3_
  85.7 1.5 %collective-permute-done.6.refs_0_ = bf16[2,64,1024]{2,1,0:T(8,128)(2,1)S(1)} collective-permute-done((bf16[2,64,1024]{2,1,0:T(8,128)(2,1)S(1)}, bf16[2,64,1024]{2,1,0:T(8,128)(2,1)S(1)}, u32[]{:S(2)}, u32[]{:S(2)}) %collective-permute-start.6) | collective-permute-done | bytes 262176 | tf_op jit(solution)/shard_map/ppermute | solution.py:216
  87.2 3.1 %shard_map.63 = bf16[4,64,1024]{2,1,0:T(8,128)(2,1)S(1)} custom-call(s32[16,34]{1,0:T(8,128)S(1)} %shard_map.59.index, bf16[2,64,1024]{2,1,0:T(8,128)(2,1)S(1)} %collective-permute-done.6.refs_0_, bf16[2,64,1024]{2,1,0:T(8,128)(2,1)S(1)} %collective-permute-done.7.refs_1_, bf16[2,64,1024]{2,1,0:T(8,128)(2,1)S(1)} %shard_map.62.refs_2_, ...), custom_call_target="tpu_custom_call" | custom-call | tf_op jit(solution)/shard_map/pallas_call | solution.py:245
  90.3 11.6 %all_to_all.27.parts = bf16[4,64,1024]{2,1,0:T(8,128)(2,1)S(1)} all-to-all(bf16[4,64,1024]{2,1,0:T(8,128)(2,1)S(1)} %shard_map.63), channel_id=1, replica_groups=mesh['z'=8,'y'=8,'core'=2,'blk'=4] {'blk'}, dimensions={0} | all-to-all | bytes 1048576 | tf_op jit(solution)/shard_map/all_to_all | solution.py:260
  101.9 0.3 shard_map.64
  102.3 14.2 %all_to_all.28.parts = f32[16,24,128]{2,1,0:T(8,128)S(1)} all-to-all(f32[16,24,128]{2,1,0:T(8,128)S(1)} %get-tuple-element.4), channel_id=1, replica_groups=mesh['z'=8,'y'=8,'core'=2,'blk'=4] {'y','core'}, dimensions={0} | all-to-all | bytes 393216 | tf_op jit(solution)/shard_map/all_to_all | solution.py:266
  116.5 12.0 %all_to_all.29.parts = f32[8,24,128]{2,1,0:T(8,128)S(1)} all-to-all(f32[8,24,128]{2,1,0:T(8,128)S(1)} %shard_map.65), channel_id=1, replica_groups=mesh['z'=8,'y'=8,'core'=2,'blk'=4] {'z'}, dimensions={0} | all-to-all | bytes 196608 | tf_op jit(solution)/shard_map/all_to_all | solution.py:268
  128.5 2.6 %shard_map.66 = (f32[16,1024]{1,0:T(8,128)}, f32[64,64]{1,0:T(8,128)}) custom-call(f32[8,24,128]{2,1,0:T(8,128)S(1)} %all_to_all.29.parts, bf16[64,1024]{1,0:T(8,128)(2,1)S(1)} %get-tuple-element.5.filtered), custom_call_target="tpu_custom_call" | custom-call | tf_op jit(solution)/shard_map/pallas_call | solution.py:269
  (2 shorter events, 0.1 us)
Async XLA Ops:
  17.2 13.2 %collective-permute-start.2 = (bf16[2,64,1024]{2,1,0:T(8,128)(2,1)S(1)}, bf16[2,64,1024]{2,1,0:T(8,128)(2,1)S(1)}, u32[]{:S(2)}, u32[]{:S(2)}) collective-permute-start(bf16[2,64,1024]{2,1,0:T(8,128)(2,1)S(1)} %bitcast.2), channel_id=1, source_target_pairs={{504,0},{12,4},{0,8},{20,12},{8,16},{28,20},{16,24},{36,28},{24,32... | collective-permute-start | bytes 786440 | tf_op jit(solution)/shard_map/ppermute | solution.py:212
  27.1 13.3 %collective-permute-start = (bf16[2,64,1024]{2,1,0:T(8,128)(2,1)S(1)}, bf16[2,64,1024]{2,1,0:T(8,128)(2,1)S(1)}, u32[]{:S(2)}, u32[]{:S(2)}) collective-permute-start(bf16[2,64,1024]{2,1,0:T(8,128)(2,1)S(1)} %bitcast.3), channel_id=1, source_target_pairs={{16,0},{500,4},{24,8},{508,12},{32,16},{4,20},{40,24},{12,28},{48,... | collective-permute-start | bytes 786440 | tf_op jit(solution)/shard_map/ppermute | solution.py:212
  30.4 15.7 %collective-permute-start.3 = (bf16[2,64,1024]{2,1,0:T(8,128)(2,1)S(1)}, bf16[2,64,1024]{2,1,0:T(8,128)(2,1)S(1)}, u32[]{:S(2)}, u32[]{:S(2)}) collective-permute-start(bf16[2,64,1024]{2,1,0:T(8,128)(2,1)S(1)} %collective-permute-done.2.refs_1_), channel_id=1, source_target_pairs={{0,4},{4,0},{1,5},{5,1},{2,6},{6,2},{3,7},{7,3},{8,12},{12,8},{9,1... | collective-permute-start | bytes 786440 | tf_op jit(solution)/shard_map/ppermute | solution.py:216
  40.4 5.7 %collective-permute-start.1 = (bf16[2,64,1024]{2,1,0:T(8,128)(2,1)S(1)}, bf16[2,64,1024]{2,1,0:T(8,128)(2,1)S(1)}, u32[]{:S(2)}, u32[]{:S(2)}) collective-permute-start(bf16[2,64,1024]{2,1,0:T(8,128)(2,1)S(1)} %collective-permute-done.refs_4_), channel_id=1, source_target_pairs={{0,4},{4,0},{1,5},{5,1},{2,6},{6,2},{3,7},{7,3},{8,12},{12,8},{9,1... | collective-permute-start | bytes 786440 | tf_op jit(solution)/shard_map/ppermute | solution.py:216
  43.0 2.3 %copy-start = (bf16[16,64,2176]{2,1,0:T(8,128)(2,1)S(1)}, bf16[16,64,2176]{2,1,0:T(8,128)(2,1)}, u32[]{:S(2)}) copy-start(bf16[16,64,2176]{2,1,0:T(8,128)(2,1)} %refs_5_.3) | copy-start | bytes 13369348
  45.3 0.7 copy-start.2
  46.0 2.3 %copy-start.1 = (bf16[16,64,2176]{2,1,0:T(8,128)(2,1)S(1)}, bf16[16,64,2176]{2,1,0:T(8,128)(2,1)}, u32[]{:S(2)}) copy-start(bf16[16,64,2176]{2,1,0:T(8,128)(2,1)} %refs_5_.3) | copy-start | bytes 13369348
  62.9 4.2 %collective-permute-start.4 = (bf16[64,1024]{1,0:T(8,128)(2,1)S(1)}, bf16[64,1024]{1,0:T(8,128)(2,1)S(1)}, u32[]{:S(2)}, u32[]{:S(2)}) collective-permute-start(bf16[64,1024]{1,0:T(8,128)(2,1)S(1)} %shard_map.61.mine), channel_id=1, source_target_pairs={{0,4},{4,0},{1,5},{5,1},{2,6},{6,2},{3,7},{7,3},{8,12},{12,8},{9,1... | collective-permute-start | bytes 393224 | tf_op jit(solution)/shard_map/ppermute | solution.py:216
  67.2 7.1 %collective-permute-start.7 = (bf16[2,64,1024]{2,1,0:T(8,128)(2,1)S(1)}, bf16[2,64,1024]{2,1,0:T(8,128)(2,1)S(1)}, u32[]{:S(2)}, u32[]{:S(2)}) collective-permute-start(bf16[2,64,1024]{2,1,0:T(8,128)(2,1)S(1)} %shard_map.62.refs_2_), channel_id=1, source_target_pairs={{504,0},{12,4},{0,8},{20,12},{8,16},{28,20},{16,24},{36,28},{24,32... | collective-permute-start | bytes 786440 | tf_op jit(solution)/shard_map/ppermute | solution.py:212
  69.1 14.7 %collective-permute-start.5 = (bf16[2,64,1024]{2,1,0:T(8,128)(2,1)S(1)}, bf16[2,64,1024]{2,1,0:T(8,128)(2,1)S(1)}, u32[]{:S(2)}, u32[]{:S(2)}) collective-permute-start(bf16[2,64,1024]{2,1,0:T(8,128)(2,1)S(1)} %shard_map.62.refs_2_), channel_id=1, source_target_pairs={{16,0},{500,4},{24,8},{508,12},{32,16},{4,20},{40,24},{12,28},{48,... | collective-permute-start | bytes 786440 | tf_op jit(solution)/shard_map/ppermute | solution.py:212
  74.3 11.4 %collective-permute-start.8 = (bf16[2,64,1024]{2,1,0:T(8,128)(2,1)S(1)}, bf16[2,64,1024]{2,1,0:T(8,128)(2,1)S(1)}, u32[]{:S(2)}, u32[]{:S(2)}) collective-permute-start(bf16[2,64,1024]{2,1,0:T(8,128)(2,1)S(1)} %collective-permute-done.7.refs_1_), channel_id=1, source_target_pairs={{0,4},{4,0},{1,5},{5,1},{2,6},{6,2},{3,7},{7,3},{8,12},{12,8},{9,1... | collective-permute-start | bytes 786440 | tf_op jit(solution)/shard_map/ppermute | solution.py:216
  83.8 3.4 %collective-permute-start.6 = (bf16[2,64,1024]{2,1,0:T(8,128)(2,1)S(1)}, bf16[2,64,1024]{2,1,0:T(8,128)(2,1)S(1)}, u32[]{:S(2)}, u32[]{:S(2)}) collective-permute-start(bf16[2,64,1024]{2,1,0:T(8,128)(2,1)S(1)} %collective-permute-done.5.refs_4_), channel_id=1, source_target_pairs={{0,4},{4,0},{1,5},{5,1},{2,6},{6,2},{3,7},{7,3},{8,12},{12,8},{9,1... | collective-permute-start | bytes 786440 | tf_op jit(solution)/shard_map/ppermute | solution.py:216

commit v5 on v4

--- a/solution.py
+++ b/solution.py
@@ -99,31 +99,54 @@
     out[1 - core] = other[...]
 
 
-STRIPS = ((7, 6, 0), (5, 4, 3), (2, 1))
+LINES = (((7, 0, 64), (6, 0, 56), (0, 0, 8)), ((5, 0, 48), (4, 0, 40), (3, 0, 32), (1, 0, 8)))
+REST = ((2, 0, 24), (1, 8, 8))
+PACKED = 18 * 128
+
+
+def turn(value, by):
+    return pltpu.roll(value, by % 128, 1) if by % 128 else value
 
 
 def pack(g):
     lane = lax.broadcasted_iota(jnp.int32, (8, 128), 1)
-    rows = []
-    for group in STRIPS:
+    row_lane = lax.broadcasted_iota(jnp.int32, (1, 128), 1)
+
+    def side_by_side(group):
         at, line = 0, jnp.zeros((8, 128), F32)
-        for i in group:
-            wide = jnp.concatenate([g[8 * i : 8 * i + 8], jnp.zeros((8, 64), F32)], axis=1)
-            moved = pltpu.roll(wide, at, 1) if at else wide
-            line = jnp.where((lane >= at) & (lane < at + 8 * i + 8), moved, line)
-            at += 8 * i + 8
-        rows.append(line)
-    return jnp.concatenate(rows, axis=0)
+        for strip, first, count in group:
+            wide = jnp.concatenate(
+                [g[8 * strip : 8 * strip + 8], jnp.zeros((8, 64), F32)], axis=1
+            )
+            line = jnp.where((lane >= at) & (lane < at + count), turn(wide, at - first), line)
+            at += count
+        return line
+
+    rows = [line[r : r + 1] for line in map(side_by_side, LINES) for r in range(8)]
+    rest = side_by_side(REST)
+    for q in range(2):
+        row = jnp.zeros((1, 128), F32)
+        for p in range(4):
+            here = (row_lane >= 32 * p) & (row_lane < 32 * p + 32)
+            row = jnp.where(here, turn(rest[2 * p + q : 2 * p + q + 1], 32 * p), row)
+        rows.append(row)
+    return rows
 
 
 def unpack(packed):
-    strips = [None] * 8
-    for q, group in enumerate(STRIPS):
-        at, line = 0, packed[8 * q : 8 * q + 8]
-        for i in group:
-            strips[i] = (pltpu.roll(line, 128 - at, 1) if at else line)[:, :64]
-            at += 8 * i + 8
-    low = jnp.concatenate(strips, axis=0)
+    lane = lax.broadcasted_iota(jnp.int32, (8, 128), 1)
+    rows = [packed[:, 128 * r : 128 * r + 128] for r in range(18)]
+    lines = [jnp.concatenate(rows[8 * q : 8 * q + 8], axis=0) for q in range(2)]
+    rest = [turn(rows[16 + r % 2], -32 * (r // 2)) for r in range(8)]
+    lines.append(jnp.concatenate(rest, axis=0))
+    strips = [jnp.zeros((8, 128), F32) for _ in range(8)]
+    for line, group in zip(lines, LINES + (REST,)):
+        at = 0
+        for strip, first, count in group:
+            here = (lane >= first) & (lane < first + count)
+            strips[strip] = jnp.where(here, turn(line, first - at), strips[strip])
+            at += count
+    low = jnp.concatenate([strip[:, :64] for strip in strips], axis=0)
     row = lax.broadcasted_iota(jnp.int32, (64, 64), 0) // 8
     col = lax.broadcasted_iota(jnp.int32, (64, 64), 1) // 8
     return jnp.where(col <= row, low, low.T)
@@ -136,9 +159,9 @@
     value = (2.0 * total - own[lax.axis_index("core")].astype(F32)).astype(BF16)
     filtered[...] = value
     g = lax.dot_general(value, value, (((1,), (1,)), ((), ())), preferred_element_type=F32)
-    packed = pack(g)
-    for c in range(gram.shape[0]):
-        gram[c] = packed
+    for r, row in enumerate(pack(g)):
+        for c in range(gram.shape[0]):
+            gram[c, :, 128 * r : 128 * r + 128] = row
 
 
 def sum_kernel(parts, out):
@@ -218,10 +241,10 @@
 
 def window(pair):
     near = from_chip(pair, 1)
-    far = from_chip(pair, -2)
+    far = from_chip(pair, 2)
     near_other = flip(near)
     far_other = flip(far)
-    return far_other, near, pair, near_other, far
+    return far, near, pair, near_other, far_other
 
 
 def to_all(value, axes, count):
@@ -260,11 +283,11 @@
     parts = lax.all_to_all(parts, "blk", 0, 0, tiled=True)
     filtered, gram = call(
         gram_kernel,
-        (unit, shape((16, 24, 128), F32)),
+        (unit, shape((16, 1, PACKED), F32)),
         [VMEM_SPEC] * 2,
     )(parts, pair)
     gram = lax.all_to_all(gram, ("y", "core"), 0, 0, tiled=True)
-    gram = call(sum_kernel, shape((8, 24, 128), F32), [VMEM_SPEC])(gram)
+    gram = call(sum_kernel, shape((8, 1, PACKED), F32), [VMEM_SPEC])(gram)
     gram = lax.all_to_all(gram, "z", 0, 0, tiled=True)
     basis, factor = call(
         functools.partial(factor_kernel, 1.0 / (total_blocks * width)),

time: 132 us -> 130 us (0.985)
  waiting for transfers between devices: 13.1 us -> 5.44 us
  starting transfers between devices: 36.1 us -> 42.5 us
    ppermute x4, starting transfers between devices: 15.7 us -> 23.5 us  [from_chip(): return lax.ppermute(value, ROWS, pairs)]
    ppermute x4, waiting for transfers between devices: 10.7 us -> 3.34 us  [from_chip(): return lax.ppermute(value, ROWS, pairs)]
    ppermute x5, starting transfers between devices: 20.5 us -> 19 us  [flip(): return lax.ppermute(value, 'core', [(0, 1), (1, 0)])]
where the time goes in v5:
time: 130 us; the launch traced here: 129 us
  blocking collectives  64.2 us (49%)
  starting transfers between devices  42.5 us (33%)
  Pallas kernels  9.5 us (7%)
  local copies, waits for them, and re-layouts  6.65 us (5%)
  waiting for transfers between devices  5.44 us (4%)
    ppermute x4, starting transfers between devices, from_chip(): return lax.ppermute(value, ROWS, pairs)  23.5 us
    all_to_all x2, blocking collectives, program(): parts = lax.all_to_all(parts, 'blk', 0, 0, tiled=True)  23.5 us
    ppermute x5, starting transfers between devices, flip(): return lax.ppermute(value, 'core', [(0, 1), (1, 0)])  19 us
    all_to_all x1, blocking collectives, to_all(): lax.all_to_all(jnp.broadcast_to(value[None], (count,) + value.shape), axe...  15.8 us
    all_to_all x1, blocking collectives, program(): gram = lax.all_to_all(gram, ('y', 'core'), 0, 0, tiled=True)  13.2 us
    all_to_all x1, blocking collectives, program(): gram = lax.all_to_all(gram, 'z', 0, 0, tiled=True)  11.8 us
    pallas_call x2, Pallas kernels, products(): call(functools.partial(product_kernel, copies), shape((copies, vecs, bloc...  6.22 us
    unnamed x6, local copies, waits for them, and re-layouts  5.14 us
  transfers between devices with their start and end apart: 9, of which 5 were waited for; matrix products, arithmetic and copies ran while one was open for 1% of the time, Pallas kernels for 0%

profile of v5, /device:TPU:1, one launch (start us, length us, event | category | flops | bytes accessed | tf_op | source)
XLA Modules:
  0.0 129.1 jit_solution(775211009001225756)
XLA Ops:
  0.6 0.8 broadcast_in_dim.2
  1.4 15.8 %all_to_all.25 = bf16[8,16,1024]{2,1,0:T(8,128)(2,1)S(1)} all-to-all(bf16[8,16,1024]{2,1,0:T(8,128)(2,1)S(1)} %broadcast_in_dim.2), channel_id=1, replica_groups=mesh['z'=8,'y'=8,'core'=2,'blk'=4] {'core','blk'}, dimensions={0} | all-to-all | bytes 524288 | tf_op jit(solution)/shard_map/all_to_all | solution.py:251
  17.2 9.9 %collective-permute-start.1 = (bf16[2,64,1024]{2,1,0:T(8,128)(2,1)S(1)}, bf16[2,64,1024]{2,1,0:T(8,128)(2,1)S(1)}, u32[]{:S(2)}, u32[]{:S(2)}) collective-permute-start(bf16[2,64,1024]{2,1,0:T(8,128)(2,1)S(1)} %bitcast.2), channel_id=1, source_target_pairs={{504,0},{12,4},{0,8},{20,12},{8,16},{28,20},{16,24},{36,28},{24,32... | collective-permute-start | bytes 786440 | tf_op jit(solution)/shard_map/ppermute | solution.py:235
  27.1 3.8 %collective-permute-start = (bf16[2,64,1024]{2,1,0:T(8,128)(2,1)S(1)}, bf16[2,64,1024]{2,1,0:T(8,128)(2,1)S(1)}, u32[]{:S(2)}, u32[]{:S(2)}) collective-permute-start(bf16[2,64,1024]{2,1,0:T(8,128)(2,1)S(1)} %bitcast.3), channel_id=1, source_target_pairs={{496,0},{20,4},{504,8},{28,12},{0,16},{36,20},{8,24},{44,28},{16,3... | collective-permute-start | bytes 786440 | tf_op jit(solution)/shard_map/ppermute | solution.py:235
  30.9 0.0 collective-permute-done.1.refs_1_
  30.9 3.1 %collective-permute-start.2 = (bf16[2,64,1024]{2,1,0:T(8,128)(2,1)S(1)}, bf16[2,64,1024]{2,1,0:T(8,128)(2,1)S(1)}, u32[]{:S(2)}, u32[]{:S(2)}) collective-permute-start(bf16[2,64,1024]{2,1,0:T(8,128)(2,1)S(1)} %collective-permute-done.1.refs_1_), channel_id=1, source_target_pairs={{0,4},{4,0},{1,5},{5,1},{2,6},{6,2},{3,7},{7,3},{8,12},{12,8},{9,1... | collective-permute-start | bytes 786440 | tf_op jit(solution)/shard_map/ppermute | solution.py:239
  34.0 1.5 %collective-permute-done.refs_0_ = bf16[2,64,1024]{2,1,0:T(8,128)(2,1)S(1)} collective-permute-done((bf16[2,64,1024]{2,1,0:T(8,128)(2,1)S(1)}, bf16[2,64,1024]{2,1,0:T(8,128)(2,1)S(1)}, u32[]{:S(2)}, u32[]{:S(2)}) %collective-permute-start) | collective-permute-done | bytes 262176 | tf_op jit(solution)/shard_map/ppermute | solution.py:235
  35.5 3.6 %collective-permute-start.3 = (bf16[2,64,1024]{2,1,0:T(8,128)(2,1)S(1)}, bf16[2,64,1024]{2,1,0:T(8,128)(2,1)S(1)}, u32[]{:S(2)}, u32[]{:S(2)}) collective-permute-start(bf16[2,64,1024]{2,1,0:T(8,128)(2,1)S(1)} %collective-permute-done.refs_0_), channel_id=1, source_target_pairs={{0,4},{4,0},{1,5},{5,1},{2,6},{6,2},{3,7},{7,3},{8,12},{12,8},{9,1... | collective-permute-start | bytes 786440 | tf_op jit(solution)/shard_map/ppermute | solution.py:239
  39.1 0.7 copy.6.counts
  39.8 0.0 copy-start
  39.8 2.3 %copy-done = bf16[16,64,2176]{2,1,0:T(8,128)(2,1)S(1)} copy-done((bf16[16,64,2176]{2,1,0:T(8,128)(2,1)S(1)}, bf16[16,64,2176]{2,1,0:T(8,128)(2,1)}, u32[]{:S(2)}) %copy-start) | copy-done | bytes 4456472
  42.1 0.0 copy-start.2
  42.1 0.7 copy-done.2
  42.8 0.0 copy-start.1
  42.8 0.1 shard_map.59.index
  42.9 0.0 collective-permute-done.2.refs_3_
  42.9 0.0 collective-permute-done.3.refs_4_
  42.9 2.2 %copy-done.1 = bf16[16,64,2176]{2,1,0:T(8,128)(2,1)S(1)} copy-done((bf16[16,64,2176]{2,1,0:T(8,128)(2,1)S(1)}, bf16[16,64,2176]{2,1,0:T(8,128)(2,1)}, u32[]{:S(2)}) %copy-start.1) | copy-done | bytes 4456472
  45.1 3.1 %shard_map.60 = bf16[4,64,1024]{2,1,0:T(8,128)(2,1)S(1)} custom-call(s32[16,34]{1,0:T(8,128)S(1)} %shard_map.59.index, bf16[2,64,1024]{2,1,0:T(8,128)(2,1)S(1)} %collective-permute-done.refs_0_, bf16[2,64,1024]{2,1,0:T(8,128)(2,1)S(1)} %collective-permute-done.1.refs_1_, bf16[2,64,1024]{2,1,0:T(8,128)(2,1)S(1)} %bitcast.4, ...), custom_call_target="tpu_custom_call" | custom-call | tf_op jit(solution)/shard_map/pallas_call | solution.py:268
  48.2 11.9 %all_to_all.26.parts = bf16[4,64,1024]{2,1,0:T(8,128)(2,1)S(1)} all-to-all(bf16[4,64,1024]{2,1,0:T(8,128)(2,1)S(1)} %shard_map.60), channel_id=1, replica_groups=mesh['z'=8,'y'=8,'core'=2,'blk'=4] {'blk'}, dimensions={0} | all-to-all | bytes 1048576 | tf_op jit(solution)/shard_map/all_to_all | solution.py:278
  60.1 0.1 shard_map.61.mine
  60.1 3.1 %collective-permute-start.4 = (bf16[64,1024]{1,0:T(8,128)(2,1)S(1)}, bf16[64,1024]{1,0:T(8,128)(2,1)S(1)}, u32[]{:S(2)}, u32[]{:S(2)}) collective-permute-start(bf16[64,1024]{1,0:T(8,128)(2,1)S(1)} %shard_map.61.mine), channel_id=1, source_target_pairs={{0,4},{4,0},{1,5},{5,1},{2,6},{6,2},{3,7},{7,3},{8,12},{12,8},{9,1... | collective-permute-start | bytes 393224 | tf_op jit(solution)/shard_map/ppermute | solution.py:239
  63.2 1.0 collective-permute-done.4.other
  64.2 6.8 %collective-permute-start.6 = (bf16[2,64,1024]{2,1,0:T(8,128)(2,1)S(1)}, bf16[2,64,1024]{2,1,0:T(8,128)(2,1)S(1)}, u32[]{:S(2)}, u32[]{:S(2)}) collective-permute-start(bf16[2,64,1024]{2,1,0:T(8,128)(2,1)S(1)} %shard_map.62.refs_2_), channel_id=1, source_target_pairs={{504,0},{12,4},{0,8},{20,12},{8,16},{28,20},{16,24},{36,28},{24,32... | collective-permute-start | bytes 786440 | tf_op jit(solution)/shard_map/ppermute | solution.py:235
  71.0 3.0 %collective-permute-start.5 = (bf16[2,64,1024]{2,1,0:T(8,128)(2,1)S(1)}, bf16[2,64,1024]{2,1,0:T(8,128)(2,1)S(1)}, u32[]{:S(2)}, u32[]{:S(2)}) collective-permute-start(bf16[2,64,1024]{2,1,0:T(8,128)(2,1)S(1)} %shard_map.62.refs_2_), channel_id=1, source_target_pairs={{496,0},{20,4},{504,8},{28,12},{0,16},{36,20},{8,24},{44,28},{16,3... | collective-permute-start | bytes 786440 | tf_op jit(solution)/shard_map/ppermute | solution.py:235
  74.1 0.2 collective-permute-done.6.refs_1_
  74.3 3.7 %collective-permute-start.7 = (bf16[2,64,1024]{2,1,0:T(8,128)(2,1)S(1)}, bf16[2,64,1024]{2,1,0:T(8,128)(2,1)S(1)}, u32[]{:S(2)}, u32[]{:S(2)}) collective-permute-start(bf16[2,64,1024]{2,1,0:T(8,128)(2,1)S(1)} %collective-permute-done.6.refs_1_), channel_id=1, source_target_pairs={{0,4},{4,0},{1,5},{5,1},{2,6},{6,2},{3,7},{7,3},{8,12},{12,8},{9,1... | collective-permute-start | bytes 786440 | tf_op jit(solution)/shard_map/ppermute | solution.py:239
  78.1 1.6 %collective-permute-done.5.refs_0_ = bf16[2,64,1024]{2,1,0:T(8,128)(2,1)S(1)} collective-permute-done((bf16[2,64,1024]{2,1,0:T(8,128)(2,1)S(1)}, bf16[2,64,1024]{2,1,0:T(8,128)(2,1)S(1)}, u32[]{:S(2)}, u32[]{:S(2)}) %collective-permute-start.5) | collective-permute-done | bytes 262176 | tf_op jit(solution)/shard_map/ppermute | solution.py:235
  79.6 5.5 %collective-permute-start.8 = (bf16[2,64,1024]{2,1,0:T(8,128)(2,1)S(1)}, bf16[2,64,1024]{2,1,0:T(8,128)(2,1)S(1)}, u32[]{:S(2)}, u32[]{:S(2)}) collective-permute-start(bf16[2,64,1024]{2,1,0:T(8,128)(2,1)S(1)} %collective-permute-done.5.refs_0_), channel_id=1, source_target_pairs={{0,4},{4,0},{1,5},{5,1},{2,6},{6,2},{3,7},{7,3},{8,12},{12,8},{9,1... | collective-permute-start | bytes 786440 | tf_op jit(solution)/shard_map/ppermute | solution.py:239
  85.1 0.0 collective-permute-done.7.refs_3_
  85.2 1.1 collective-permute-done.8.refs_4_
  86.3 3.1 %shard_map.63 = bf16[4,64,1024]{2,1,0:T(8,128)(2,1)S(1)} custom-call(s32[16,34]{1,0:T(8,128)S(1)} %shard_map.59.index, bf16[2,64,1024]{2,1,0:T(8,128)(2,1)S(1)} %collective-permute-done.5.refs_0_, bf16[2,64,1024]{2,1,0:T(8,128)(2,1)S(1)} %collective-permute-done.6.refs_1_, bf16[2,64,1024]{2,1,0:T(8,128)(2,1)S(1)} %shard_map.62.refs_2_, ...), custom_call_target="tpu_custom_call" | custom-call | tf_op jit(solution)/shard_map/pallas_call | solution.py:268
  89.4 11.6 %all_to_all.27.parts = bf16[4,64,1024]{2,1,0:T(8,128)(2,1)S(1)} all-to-all(bf16[4,64,1024]{2,1,0:T(8,128)(2,1)S(1)} %shard_map.63), channel_id=1, replica_groups=mesh['z'=8,'y'=8,'core'=2,'blk'=4] {'blk'}, dimensions={0} | all-to-all | bytes 1048576 | tf_op jit(solution)/shard_map/all_to_all | solution.py:283
  101.0 0.4 shard_map.64
  101.4 13.2 %all_to_all.28.parts = f32[16,1,2304]{2,1,0:T(1,128)S(1)} all-to-all(f32[16,1,2304]{2,1,0:T(1,128)S(1)} %get-tuple-element.4), channel_id=1, replica_groups=mesh['z'=8,'y'=8,'core'=2,'blk'=4] {'y','core'}, dimensions={0} | all-to-all | bytes 294912 | tf_op jit(solution)/shard_map/all_to_all | solution.py:289
  114.6 11.8 %all_to_all.29.parts = f32[8,1,2304]{2,1,0:T(1,128)S(1)} all-to-all(f32[8,1,2304]{2,1,0:T(1,128)S(1)} %shard_map.65), channel_id=1, replica_groups=mesh['z'=8,'y'=8,'core'=2,'blk'=4] {'z'}, dimensions={0} | all-to-all | bytes 147456 | tf_op jit(solution)/shard_map/all_to_all | solution.py:291
  126.4 2.7 %shard_map.66 = (f32[16,1024]{1,0:T(8,128)}, f32[64,64]{1,0:T(8,128)}) custom-call(f32[8,1,2304]{2,1,0:T(1,128)S(1)} %all_to_all.29.parts, bf16[64,1024]{1,0:T(8,128)(2,1)S(1)} %get-tuple-element.5.filtered), custom_call_target="tpu_custom_call" | custom-call | tf_op jit(solution)/shard_map/pallas_call | solution.py:292
  (2 shorter events, 0.1 us)
Async XLA Ops:
  17.2 13.7 %collective-permute-start.1 = (bf16[2,64,1024]{2,1,0:T(8,128)(2,1)S(1)}, bf16[2,64,1024]{2,1,0:T(8,128)(2,1)S(1)}, u32[]{:S(2)}, u32[]{:S(2)}) collective-permute-start(bf16[2,64,1024]{2,1,0:T(8,128)(2,1)S(1)} %bitcast.2), channel_id=1, source_target_pairs={{504,0},{12,4},{0,8},{20,12},{8,16},{28,20},{16,24},{36,28},{24,32... | collective-permute-start | bytes 786440 | tf_op jit(solution)/shard_map/ppermute | solution.py:235
  27.1 8.4 %collective-permute-start = (bf16[2,64,1024]{2,1,0:T(8,128)(2,1)S(1)}, bf16[2,64,1024]{2,1,0:T(8,128)(2,1)S(1)}, u32[]{:S(2)}, u32[]{:S(2)}) collective-permute-start(bf16[2,64,1024]{2,1,0:T(8,128)(2,1)S(1)} %bitcast.3), channel_id=1, source_target_pairs={{496,0},{20,4},{504,8},{28,12},{0,16},{36,20},{8,24},{44,28},{16,3... | collective-permute-start | bytes 786440 | tf_op jit(solution)/shard_map/ppermute | solution.py:235
  30.9 12.0 %collective-permute-start.2 = (bf16[2,64,1024]{2,1,0:T(8,128)(2,1)S(1)}, bf16[2,64,1024]{2,1,0:T(8,128)(2,1)S(1)}, u32[]{:S(2)}, u32[]{:S(2)}) collective-permute-start(bf16[2,64,1024]{2,1,0:T(8,128)(2,1)S(1)} %collective-permute-done.1.refs_1_), channel_id=1, source_target_pairs={{0,4},{4,0},{1,5},{5,1},{2,6},{6,2},{3,7},{7,3},{8,12},{12,8},{9,1... | collective-permute-start | bytes 786440 | tf_op jit(solution)/shard_map/ppermute | solution.py:239
  35.5 7.4 %collective-permute-start.3 = (bf16[2,64,1024]{2,1,0:T(8,128)(2,1)S(1)}, bf16[2,64,1024]{2,1,0:T(8,128)(2,1)S(1)}, u32[]{:S(2)}, u32[]{:S(2)}) collective-permute-start(bf16[2,64,1024]{2,1,0:T(8,128)(2,1)S(1)} %collective-permute-done.refs_0_), channel_id=1, source_target_pairs={{0,4},{4,0},{1,5},{5,1},{2,6},{6,2},{3,7},{7,3},{8,12},{12,8},{9,1... | collective-permute-start | bytes 786440 | tf_op jit(solution)/shard_map/ppermute | solution.py:239
  39.8 2.3 %copy-start = (bf16[16,64,2176]{2,1,0:T(8,128)(2,1)S(1)}, bf16[16,64,2176]{2,1,0:T(8,128)(2,1)}, u32[]{:S(2)}) copy-start(bf16[16,64,2176]{2,1,0:T(8,128)(2,1)} %refs_5_.3) | copy-start | bytes 13369348
  42.1 0.7 copy-start.2
  42.8 2.3 %copy-start.1 = (bf16[16,64,2176]{2,1,0:T(8,128)(2,1)S(1)}, bf16[16,64,2176]{2,1,0:T(8,128)(2,1)}, u32[]{:S(2)}) copy-start(bf16[16,64,2176]{2,1,0:T(8,128)(2,1)} %refs_5_.3) | copy-start | bytes 13369348
  60.1 4.0 %collective-permute-start.4 = (bf16[64,1024]{1,0:T(8,128)(2,1)S(1)}, bf16[64,1024]{1,0:T(8,128)(2,1)S(1)}, u32[]{:S(2)}, u32[]{:S(2)}) collective-permute-start(bf16[64,1024]{1,0:T(8,128)(2,1)S(1)} %shard_map.61.mine), channel_id=1, source_target_pairs={{0,4},{4,0},{1,5},{5,1},{2,6},{6,2},{3,7},{7,3},{8,12},{12,8},{9,1... | collective-permute-start | bytes 393224 | tf_op jit(solution)/shard_map/ppermute | solution.py:239
  64.2 10.1 %collective-permute-start.6 = (bf16[2,64,1024]{2,1,0:T(8,128)(2,1)S(1)}, bf16[2,64,1024]{2,1,0:T(8,128)(2,1)S(1)}, u32[]{:S(2)}, u32[]{:S(2)}) collective-permute-start(bf16[2,64,1024]{2,1,0:T(8,128)(2,1)S(1)} %shard_map.62.refs_2_), channel_id=1, source_target_pairs={{504,0},{12,4},{0,8},{20,12},{8,16},{28,20},{16,24},{36,28},{24,32... | collective-permute-start | bytes 786440 | tf_op jit(solution)/shard_map/ppermute | solution.py:235
  71.0 8.6 %collective-permute-start.5 = (bf16[2,64,1024]{2,1,0:T(8,128)(2,1)S(1)}, bf16[2,64,1024]{2,1,0:T(8,128)(2,1)S(1)}, u32[]{:S(2)}, u32[]{:S(2)}) collective-permute-start(bf16[2,64,1024]{2,1,0:T(8,128)(2,1)S(1)} %shard_map.62.refs_2_), channel_id=1, source_target_pairs={{496,0},{20,4},{504,8},{28,12},{0,16},{36,20},{8,24},{44,28},{16,3... | collective-permute-start | bytes 786440 | tf_op jit(solution)/shard_map/ppermute | solution.py:235
  74.3 10.8 %collective-permute-start.7 = (bf16[2,64,1024]{2,1,0:T(8,128)(2,1)S(1)}, bf16[2,64,1024]{2,1,0:T(8,128)(2,1)S(1)}, u32[]{:S(2)}, u32[]{:S(2)}) collective-permute-start(bf16[2,64,1024]{2,1,0:T(8,128)(2,1)S(1)} %collective-permute-done.6.refs_1_), channel_id=1, source_target_pairs={{0,4},{4,0},{1,5},{5,1},{2,6},{6,2},{3,7},{7,3},{8,12},{12,8},{9,1... | collective-permute-start | bytes 786440 | tf_op jit(solution)/shard_map/ppermute | solution.py:239
  79.6 6.6 %collective-permute-start.8 = (bf16[2,64,1024]{2,1,0:T(8,128)(2,1)S(1)}, bf16[2,64,1024]{2,1,0:T(8,128)(2,1)S(1)}, u32[]{:S(2)}, u32[]{:S(2)}) collective-permute-start(bf16[2,64,1024]{2,1,0:T(8,128)(2,1)S(1)} %collective-permute-done.5.refs_0_), channel_id=1, source_target_pairs={{0,4},{4,0},{1,5},{5,1},{2,6},{6,2},{3,7},{7,3},{8,12},{12,8},{9,1... | collective-permute-start | bytes 786440 | tf_op jit(solution)/shard_map/ppermute | solution.py:239

commit v6 on v5

--- a/solution.py
+++ b/solution.py
@@ -31,16 +31,24 @@
     return jax.ShapeDtypeStruct(dims, dtype)
 
 
-def product_kernel(copies, index, *refs):
-    pieces, (ham, out, tiles) = refs[:5], refs[5:]
+PAIRS = tuple((slot, None) for slot in range(5))
+UNITS = ((0, True), (0, False), (1, None), (2, None), (3, None), (4, True))
+
+
+def product_kernel(copies, plan, index, *refs):
+    pieces, (ham, out, tiles) = refs[: len(plan)], refs[len(plan) :]
+    core = lax.axis_index("core")
     vecs = ham.shape[1]
     half = lax.broadcasted_iota(jnp.int16, (vecs, 128), 1) < jnp.int16(64)
-    for p, piece in enumerate(pieces):
-        for u in range(2):
-            base = 32 * p + 16 * u
-            start = here = piece[u, :, :128]
+    for piece, (slot, own) in zip(pieces, plan):
+        if own is None:
+            units = [(piece.at[u], 32 * slot + 16 * u) for u in range(2)]
+        else:
+            units = [(piece, 32 * slot + 16 * (core if own else 1 - core))]
+        for unit, base in units:
+            start = here = unit[:, :128]
             for t in range(8):
-                after = start if t == 7 else piece[u, :, 128 * (t + 1) : 128 * (t + 2)]
+                after = start if t == 7 else unit[:, 128 * (t + 1) : 128 * (t + 2)]
                 tiles[base + 2 * t] = here
                 tiles[base + 2 * t + 1] = pltpu.roll(jnp.where(half, after, here), 64, 1)
                 here = after
@@ -247,6 +255,17 @@
     return far, near, pair, near_other, far_other
 
 
+def unit_window(unit):
+    ahead = from_chip(unit, -2)
+    behind = from_chip(unit, 2)
+    other = flip(unit)
+    pair = call(pair_kernel, shape((2,) + unit.shape, BF16), [VMEM_SPEC] * 2)(unit, other)
+    near = from_chip(pair, 1)
+    crossed = flip(ahead)
+    near_other = flip(near)
+    return behind, crossed, near, pair, near_other, ahead
+
+
 def to_all(value, axes, count):
     return lax.all_to_all(
         jnp.broadcast_to(value[None], (count,) + value.shape), axes, 0, 0, tiled=True
@@ -264,22 +283,21 @@
         [VMEM_SPEC] * 2 + [ANY_SPEC],
     )(column_index, counts.reshape(block_rows, 1), hamiltonian)
 
-    def products(pieces, copies):
+    def products(pieces, plan, copies):
         return call(
-            functools.partial(product_kernel, copies),
+            functools.partial(product_kernel, copies, plan),
             shape((copies, vecs, block_rows * width), BF16),
-            [SMEM_SPEC] + [VMEM_SPEC] * 6,
+            [SMEM_SPEC] + [VMEM_SPEC] * (len(plan) + 1),
             [pltpu.VMEM((161, vecs, 128), BF16)],
             12,
         )(index, *pieces, hamiltonian)
 
     pair = to_all(vectors, ("core", "blk"), 8).reshape(2, vecs, block_rows * width)
-    parts = products(window(pair), 4)
+    parts = products(window(pair), PAIRS, 4)
     parts = lax.all_to_all(parts, "blk", 0, 0, tiled=True)
     unit = shape((vecs, block_rows * width), BF16)
     first = call(first_kernel, unit, [VMEM_SPEC])(parts)
-    pair_two = call(pair_kernel, shape(pair.shape, BF16), [VMEM_SPEC] * 2)(first, flip(first))
-    parts = products(window(pair_two), 4)
+    parts = products(unit_window(first), UNITS, 4)
     parts = lax.all_to_all(parts, "blk", 0, 0, tiled=True)
     filtered, gram = call(
         gram_kernel,

time: 130 us -> 133 us (1.023)
  blocking collectives: 64.2 us -> 68.4 us
    all_to_all x1, blocking collectives: 13.2 us -> 18.2 us  [program(): gram = lax.all_to_all(gram, ('y', 'core'), 0, 0, tiled=True)]
    ppermute x5, starting transfers between devices: 19 us -> 15.7 us  [flip(): return lax.ppermute(value, 'core', [(0, 1), (1, 0)])]
    ppermute x4 -> x5, starting transfers between devices: 23.5 us -> 26.5 us  [from_chip(): return lax.ppermute(value, ROWS, pairs)]
    all_to_all x2, blocking collectives: 23.5 us -> 21.2 us  [program(): parts = lax.all_to_all(parts, 'blk', 0, 0, tiled=True)]
    all_to_all x1, blocking collectives: 11.8 us -> 13.2 us  [program(): gram = lax.all_to_all(gram, 'z', 0, 0, tiled=True)]
    ppermute x4 -> x5, waiting for transfers between devices: 3.34 us -> 3.4 us  [from_chip(): return lax.ppermute(value, ROWS, pairs)]
  transfers between devices with their start and end apart: 9 -> 10, of which waited for: 5 -> 5; matrix products, arithmetic and copies ran while one was open for 1% -> 1% of each run, Pallas kernels for 0% -> 0%
where the time goes in v6:
time: 133 us
  blocking collectives  68.4 us (51%)
  starting transfers between devices  42.3 us (32%)
  Pallas kernels  9.49 us (7%)
  local copies, waits for them, and re-layouts  6.65 us (5%)
  waiting for transfers between devices  5.15 us (4%)
    ppermute x5, starting transfers between devices, from_chip(): return lax.ppermute(value, ROWS, pairs)  26.5 us
    all_to_all x2, blocking collectives, program(): parts = lax.all_to_all(parts, 'blk', 0, 0, tiled=True)  21.2 us
    all_to_all x1, blocking collectives, program(): gram = lax.all_to_all(gram, ('y', 'core'), 0, 0, tiled=True)  18.2 us
    all_to_all x1, blocking collectives, to_all(): lax.all_to_all(jnp.broadcast_to(value[None], (count,) + value.shape), axe...  15.8 us
    ppermute x5, starting transfers between devices, flip(): return lax.ppermute(value, 'core', [(0, 1), (1, 0)])  15.7 us
    all_to_all x1, blocking collectives, program(): gram = lax.all_to_all(gram, 'z', 0, 0, tiled=True)  13.2 us
    pallas_call x2, Pallas kernels, products(): call(functools.partial(product_kernel, copies, plan), shape((copies, vecs...  6.21 us
    unnamed x6, local copies, waits for them, and re-layouts  5.14 us
  transfers between devices with their start and end apart: 10, of which 5 were waited for; matrix products, arithmetic and copies ran while one was open for 1% of the time, Pallas kernels for 0%

profile of v6, /device:TPU:1, one launch (start us, length us, event | category | flops | bytes accessed | tf_op | source)
XLA Modules:
  0.0 132.7 jit_solution(1931316533507393102)
XLA Ops:
  0.6 0.8 broadcast_in_dim.2
  1.4 15.8 %all_to_all.25 = bf16[8,16,1024]{2,1,0:T(8,128)(2,1)S(1)} all-to-all(bf16[8,16,1024]{2,1,0:T(8,128)(2,1)S(1)} %broadcast_in_dim.2), channel_id=1, replica_groups=mesh['z'=8,'y'=8,'core'=2,'blk'=4] {'core','blk'}, dimensions={0} | all-to-all | bytes 524288 | tf_op jit(solution)/shard_map/all_to_all | solution.py:270
  17.2 9.9 %collective-permute-start.1 = (bf16[2,64,1024]{2,1,0:T(8,128)(2,1)S(1)}, bf16[2,64,1024]{2,1,0:T(8,128)(2,1)S(1)}, u32[]{:S(2)}, u32[]{:S(2)}) collective-permute-start(bf16[2,64,1024]{2,1,0:T(8,128)(2,1)S(1)} %bitcast.2), channel_id=1, source_target_pairs={{504,0},{12,4},{0,8},{20,12},{8,16},{28,20},{16,24},{36,28},{24,32... | collective-permute-start | bytes 786440 | tf_op jit(solution)/shard_map/ppermute | solution.py:243
  27.1 3.8 %collective-permute-start = (bf16[2,64,1024]{2,1,0:T(8,128)(2,1)S(1)}, bf16[2,64,1024]{2,1,0:T(8,128)(2,1)S(1)}, u32[]{:S(2)}, u32[]{:S(2)}) collective-permute-start(bf16[2,64,1024]{2,1,0:T(8,128)(2,1)S(1)} %bitcast.3), channel_id=1, source_target_pairs={{496,0},{20,4},{504,8},{28,12},{0,16},{36,20},{8,24},{44,28},{16,3... | collective-permute-start | bytes 786440 | tf_op jit(solution)/shard_map/ppermute | solution.py:243
  30.9 0.0 collective-permute-done.1.refs_1_
  30.9 3.1 %collective-permute-start.2 = (bf16[2,64,1024]{2,1,0:T(8,128)(2,1)S(1)}, bf16[2,64,1024]{2,1,0:T(8,128)(2,1)S(1)}, u32[]{:S(2)}, u32[]{:S(2)}) collective-permute-start(bf16[2,64,1024]{2,1,0:T(8,128)(2,1)S(1)} %collective-permute-done.1.refs_1_), channel_id=1, source_target_pairs={{0,4},{4,0},{1,5},{5,1},{2,6},{6,2},{3,7},{7,3},{8,12},{12,8},{9,1... | collective-permute-start | bytes 786440 | tf_op jit(solution)/shard_map/ppermute | solution.py:247
  34.0 1.5 %collective-permute-done.refs_0_ = bf16[2,64,1024]{2,1,0:T(8,128)(2,1)S(1)} collective-permute-done((bf16[2,64,1024]{2,1,0:T(8,128)(2,1)S(1)}, bf16[2,64,1024]{2,1,0:T(8,128)(2,1)S(1)}, u32[]{:S(2)}, u32[]{:S(2)}) %collective-permute-start) | collective-permute-done | bytes 262176 | tf_op jit(solution)/shard_map/ppermute | solution.py:243
  35.5 3.6 %collective-permute-start.3 = (bf16[2,64,1024]{2,1,0:T(8,128)(2,1)S(1)}, bf16[2,64,1024]{2,1,0:T(8,128)(2,1)S(1)}, u32[]{:S(2)}, u32[]{:S(2)}) collective-permute-start(bf16[2,64,1024]{2,1,0:T(8,128)(2,1)S(1)} %collective-permute-done.refs_0_), channel_id=1, source_target_pairs={{0,4},{4,0},{1,5},{5,1},{2,6},{6,2},{3,7},{7,3},{8,12},{12,8},{9,1... | collective-permute-start | bytes 786440 | tf_op jit(solution)/shard_map/ppermute | solution.py:247
  39.1 0.7 copy.6.counts
  39.8 0.0 copy-start
  39.8 2.3 %copy-done = bf16[16,64,2176]{2,1,0:T(8,128)(2,1)S(1)} copy-done((bf16[16,64,2176]{2,1,0:T(8,128)(2,1)S(1)}, bf16[16,64,2176]{2,1,0:T(8,128)(2,1)}, u32[]{:S(2)}) %copy-start) | copy-done | bytes 4456472
  42.1 0.0 copy-start.2
  42.1 0.7 copy-done.2
  42.8 0.0 copy-start.1
  42.8 0.1 shard_map.59.index
  42.9 0.0 collective-permute-done.2.refs_3_
  42.9 0.0 collective-permute-done.3.refs_4_
  42.9 2.2 %copy-done.1 = bf16[16,64,2176]{2,1,0:T(8,128)(2,1)S(1)} copy-done((bf16[16,64,2176]{2,1,0:T(8,128)(2,1)S(1)}, bf16[16,64,2176]{2,1,0:T(8,128)(2,1)}, u32[]{:S(2)}) %copy-start.1) | copy-done | bytes 4456472
  45.1 3.1 %shard_map.60 = bf16[4,64,1024]{2,1,0:T(8,128)(2,1)S(1)} custom-call(s32[16,34]{1,0:T(8,128)S(1)} %shard_map.59.index, bf16[2,64,1024]{2,1,0:T(8,128)(2,1)S(1)} %collective-permute-done.refs_0_, bf16[2,64,1024]{2,1,0:T(8,128)(2,1)S(1)} %collective-permute-done.1.refs_1_, bf16[2,64,1024]{2,1,0:T(8,128)(2,1)S(1)} %bitcast.4, ...), custom_call_target="tpu_custom_call" | custom-call | tf_op jit(solution)/shard_map/pallas_call | solution.py:287
  48.2 11.9 %all_to_all.26.parts = bf16[4,64,1024]{2,1,0:T(8,128)(2,1)S(1)} all-to-all(bf16[4,64,1024]{2,1,0:T(8,128)(2,1)S(1)} %shard_map.60), channel_id=1, replica_groups=mesh['z'=8,'y'=8,'core'=2,'blk'=4] {'blk'}, dimensions={0} | all-to-all | bytes 1048576 | tf_op jit(solution)/shard_map/all_to_all | solution.py:297
  60.1 0.1 shard_map.61.mine
  60.1 3.1 %collective-permute-start.7 = (bf16[64,1024]{1,0:T(8,128)(2,1)S(1)}, bf16[64,1024]{1,0:T(8,128)(2,1)S(1)}, u32[]{:S(2)}, u32[]{:S(2)}) collective-permute-start(bf16[64,1024]{1,0:T(8,128)(2,1)S(1)} %shard_map.61.mine), channel_id=1, source_target_pairs={{0,4},{4,0},{1,5},{5,1},{2,6},{6,2},{3,7},{7,3},{8,12},{12,8},{9,1... | collective-permute-start | bytes 393224 | tf_op jit(solution)/shard_map/ppermute | solution.py:247
  63.2 1.0 collective-permute-done.7.other
  64.2 6.8 %collective-permute-start.8 = (bf16[2,64,1024]{2,1,0:T(8,128)(2,1)S(1)}, bf16[2,64,1024]{2,1,0:T(8,128)(2,1)S(1)}, u32[]{:S(2)}, u32[]{:S(2)}) collective-permute-start(bf16[2,64,1024]{2,1,0:T(8,128)(2,1)S(1)} %shard_map.62.refs_3_), channel_id=1, source_target_pairs={{504,0},{12,4},{0,8},{20,12},{8,16},{28,20},{16,24},{36,28},{24,32... | collective-permute-start | bytes 786440 | tf_op jit(solution)/shard_map/ppermute | solution.py:243
  71.0 1.9 %collective-permute-start.5 = (bf16[64,1024]{1,0:T(8,128)(2,1)S(1)}, bf16[64,1024]{1,0:T(8,128)(2,1)S(1)}, u32[]{:S(2)}, u32[]{:S(2)}) collective-permute-start(bf16[64,1024]{1,0:T(8,128)(2,1)S(1)} %shard_map.61.mine), channel_id=1, source_target_pairs={{16,0},{500,4},{24,8},{508,12},{32,16},{4,20},{40,24},{12,28},{48,... | collective-permute-start | bytes 393224 | tf_op jit(solution)/shard_map/ppermute | solution.py:243
  73.0 1.4 %collective-permute-done.8.refs_2_ = bf16[2,64,1024]{2,1,0:T(8,128)(2,1)S(1)} collective-permute-done((bf16[2,64,1024]{2,1,0:T(8,128)(2,1)S(1)}, bf16[2,64,1024]{2,1,0:T(8,128)(2,1)S(1)}, u32[]{:S(2)}, u32[]{:S(2)}) %collective-permute-start.8) | collective-permute-done | bytes 262176 | tf_op jit(solution)/shard_map/ppermute | solution.py:243
  74.3 4.0 %collective-permute-start.9 = (bf16[2,64,1024]{2,1,0:T(8,128)(2,1)S(1)}, bf16[2,64,1024]{2,1,0:T(8,128)(2,1)S(1)}, u32[]{:S(2)}, u32[]{:S(2)}) collective-permute-start(bf16[2,64,1024]{2,1,0:T(8,128)(2,1)S(1)} %collective-permute-done.8.refs_2_), channel_id=1, source_target_pairs={{0,4},{4,0},{1,5},{5,1},{2,6},{6,2},{3,7},{7,3},{8,12},{12,8},{9,1... | collective-permute-start | bytes 786440 | tf_op jit(solution)/shard_map/ppermute | solution.py:247
  78.3 4.1 %collective-permute-start.4 = (bf16[64,1024]{1,0:T(8,128)(2,1)S(1)}, bf16[64,1024]{1,0:T(8,128)(2,1)S(1)}, u32[]{:S(2)}, u32[]{:S(2)}) collective-permute-start(bf16[64,1024]{1,0:T(8,128)(2,1)S(1)} %shard_map.61.mine), channel_id=1, source_target_pairs={{496,0},{20,4},{504,8},{28,12},{0,16},{36,20},{8,24},{44,28},{16,3... | collective-permute-start | bytes 393224 | tf_op jit(solution)/shard_map/ppermute | solution.py:243
  82.5 0.0 collective-permute-done.5.refs_5_
  82.5 1.9 %collective-permute-start.6 = (bf16[64,1024]{1,0:T(8,128)(2,1)S(1)}, bf16[64,1024]{1,0:T(8,128)(2,1)S(1)}, u32[]{:S(2)}, u32[]{:S(2)}) collective-permute-start(bf16[64,1024]{1,0:T(8,128)(2,1)S(1)} %collective-permute-done.5.refs_5_), channel_id=1, source_target_pairs={{0,4},{4,0},{1,5},{5,1},{2,6},{6,2},{3,7},{7,3},{8,12},{12,8},{9,1... | collective-permute-start | bytes 393224 | tf_op jit(solution)/shard_map/ppermute | solution.py:247
  84.4 0.5 collective-permute-done.4.refs_0_
  85.0 0.8 collective-permute-done.6.refs_1_
  85.7 0.0 collective-permute-done.9.refs_4_
  85.7 3.1 %shard_map.63 = bf16[4,64,1024]{2,1,0:T(8,128)(2,1)S(1)} custom-call(s32[16,34]{1,0:T(8,128)S(1)} %shard_map.59.index, bf16[64,1024]{1,0:T(8,128)(2,1)S(1)} %collective-permute-done.4.refs_0_, bf16[64,1024]{1,0:T(8,128)(2,1)S(1)} %collective-permute-done.6.refs_1_, bf16[2,64,1024]{2,1,0:T(8,128)(2,1)S(1)} %collective-permute-done.8.refs_2_, ...), custom_call_target="tpu_custom_call" | custom-call | tf_op jit(solution)/shard_map/pallas_call | solution.py:287
  88.9 9.3 %all_to_all.27.parts = bf16[4,64,1024]{2,1,0:T(8,128)(2,1)S(1)} all-to-all(bf16[4,64,1024]{2,1,0:T(8,128)(2,1)S(1)} %shard_map.63), channel_id=1, replica_groups=mesh['z'=8,'y'=8,'core'=2,'blk'=4] {'blk'}, dimensions={0} | all-to-all | bytes 1048576 | tf_op jit(solution)/shard_map/all_to_all | solution.py:301
  98.2 0.4 shard_map.64
  98.6 18.2 %all_to_all.28.parts = f32[16,1,2304]{2,1,0:T(1,128)S(1)} all-to-all(f32[16,1,2304]{2,1,0:T(1,128)S(1)} %get-tuple-element.4), channel_id=1, replica_groups=mesh['z'=8,'y'=8,'core'=2,'blk'=4] {'y','core'}, dimensions={0} | all-to-all | bytes 294912 | tf_op jit(solution)/shard_map/all_to_all | solution.py:307
  116.8 13.2 %all_to_all.29.parts = f32[8,1,2304]{2,1,0:T(1,128)S(1)} all-to-all(f32[8,1,2304]{2,1,0:T(1,128)S(1)} %shard_map.65), channel_id=1, replica_groups=mesh['z'=8,'y'=8,'core'=2,'blk'=4] {'z'}, dimensions={0} | all-to-all | bytes 147456 | tf_op jit(solution)/shard_map/all_to_all | solution.py:309
  130.0 2.7 %shard_map.66 = (f32[16,1024]{1,0:T(8,128)}, f32[64,64]{1,0:T(8,128)}) custom-call(f32[8,1,2304]{2,1,0:T(1,128)S(1)} %all_to_all.29.parts, bf16[64,1024]{1,0:T(8,128)(2,1)S(1)} %get-tuple-element.5.filtered), custom_call_target="tpu_custom_call" | custom-call | tf_op jit(solution)/shard_map/pallas_call | solution.py:310
  (2 shorter events, 0.1 us)
Async XLA Ops:
  17.2 13.7 %collective-permute-start.1 = (bf16[2,64,1024]{2,1,0:T(8,128)(2,1)S(1)}, bf16[2,64,1024]{2,1,0:T(8,128)(2,1)S(1)}, u32[]{:S(2)}, u32[]{:S(2)}) collective-permute-start(bf16[2,64,1024]{2,1,0:T(8,128)(2,1)S(1)} %bitcast.2), channel_id=1, source_target_pairs={{504,0},{12,4},{0,8},{20,12},{8,16},{28,20},{16,24},{36,28},{24,32... | collective-permute-start | bytes 786440 | tf_op jit(solution)/shard_map/ppermute | solution.py:243
  27.1 8.4 %collective-permute-start = (bf16[2,64,1024]{2,1,0:T(8,128)(2,1)S(1)}, bf16[2,64,1024]{2,1,0:T(8,128)(2,1)S(1)}, u32[]{:S(2)}, u32[]{:S(2)}) collective-permute-start(bf16[2,64,1024]{2,1,0:T(8,128)(2,1)S(1)} %bitcast.3), channel_id=1, source_target_pairs={{496,0},{20,4},{504,8},{28,12},{0,16},{36,20},{8,24},{44,28},{16,3... | collective-permute-start | bytes 786440 | tf_op jit(solution)/shard_map/ppermute | solution.py:243
  30.9 12.0 %collective-permute-start.2 = (bf16[2,64,1024]{2,1,0:T(8,128)(2,1)S(1)}, bf16[2,64,1024]{2,1,0:T(8,128)(2,1)S(1)}, u32[]{:S(2)}, u32[]{:S(2)}) collective-permute-start(bf16[2,64,1024]{2,1,0:T(8,128)(2,1)S(1)} %collective-permute-done.1.refs_1_), channel_id=1, source_target_pairs={{0,4},{4,0},{1,5},{5,1},{2,6},{6,2},{3,7},{7,3},{8,12},{12,8},{9,1... | collective-permute-start | bytes 786440 | tf_op jit(solution)/shard_map/ppermute | solution.py:247
  35.5 7.4 %collective-permute-start.3 = (bf16[2,64,1024]{2,1,0:T(8,128)(2,1)S(1)}, bf16[2,64,1024]{2,1,0:T(8,128)(2,1)S(1)}, u32[]{:S(2)}, u32[]{:S(2)}) collective-permute-start(bf16[2,64,1024]{2,1,0:T(8,128)(2,1)S(1)} %collective-permute-done.refs_0_), channel_id=1, source_target_pairs={{0,4},{4,0},{1,5},{5,1},{2,6},{6,2},{3,7},{7,3},{8,12},{12,8},{9,1... | collective-permute-start | bytes 786440 | tf_op jit(solution)/shard_map/ppermute | solution.py:247
  39.8 2.3 %copy-start = (bf16[16,64,2176]{2,1,0:T(8,128)(2,1)S(1)}, bf16[16,64,2176]{2,1,0:T(8,128)(2,1)}, u32[]{:S(2)}) copy-start(bf16[16,64,2176]{2,1,0:T(8,128)(2,1)} %refs_6_.1) | copy-start | bytes 13369348
  42.1 0.7 copy-start.2
  42.8 2.3 %copy-start.1 = (bf16[16,64,2176]{2,1,0:T(8,128)(2,1)S(1)}, bf16[16,64,2176]{2,1,0:T(8,128)(2,1)}, u32[]{:S(2)}) copy-start(bf16[16,64,2176]{2,1,0:T(8,128)(2,1)} %refs_6_.1) | copy-start | bytes 13369348
  60.1 4.0 %collective-permute-start.7 = (bf16[64,1024]{1,0:T(8,128)(2,1)S(1)}, bf16[64,1024]{1,0:T(8,128)(2,1)S(1)}, u32[]{:S(2)}, u32[]{:S(2)}) collective-permute-start(bf16[64,1024]{1,0:T(8,128)(2,1)S(1)} %shard_map.61.mine), channel_id=1, source_target_pairs={{0,4},{4,0},{1,5},{5,1},{2,6},{6,2},{3,7},{7,3},{8,12},{12,8},{9,1... | collective-permute-start | bytes 393224 | tf_op jit(solution)/shard_map/ppermute | solution.py:247
  64.2 10.1 %collective-permute-start.8 = (bf16[2,64,1024]{2,1,0:T(8,128)(2,1)S(1)}, bf16[2,64,1024]{2,1,0:T(8,128)(2,1)S(1)}, u32[]{:S(2)}, u32[]{:S(2)}) collective-permute-start(bf16[2,64,1024]{2,1,0:T(8,128)(2,1)S(1)} %shard_map.62.refs_3_), channel_id=1, source_target_pairs={{504,0},{12,4},{0,8},{20,12},{8,16},{28,20},{16,24},{36,28},{24,32... | collective-permute-start | bytes 786440 | tf_op jit(solution)/shard_map/ppermute | solution.py:243
  71.0 11.5 %collective-permute-start.5 = (bf16[64,1024]{1,0:T(8,128)(2,1)S(1)}, bf16[64,1024]{1,0:T(8,128)(2,1)S(1)}, u32[]{:S(2)}, u32[]{:S(2)}) collective-permute-start(bf16[64,1024]{1,0:T(8,128)(2,1)S(1)} %shard_map.61.mine), channel_id=1, source_target_pairs={{16,0},{500,4},{24,8},{508,12},{32,16},{4,20},{40,24},{12,28},{48,... | collective-permute-start | bytes 393224 | tf_op jit(solution)/shard_map/ppermute | solution.py:243
  74.3 11.4 %collective-permute-start.9 = (bf16[2,64,1024]{2,1,0:T(8,128)(2,1)S(1)}, bf16[2,64,1024]{2,1,0:T(8,128)(2,1)S(1)}, u32[]{:S(2)}, u32[]{:S(2)}) collective-permute-start(bf16[2,64,1024]{2,1,0:T(8,128)(2,1)S(1)} %collective-permute-done.8.refs_2_), channel_id=1, source_target_pairs={{0,4},{4,0},{1,5},{5,1},{2,6},{6,2},{3,7},{7,3},{8,12},{12,8},{9,1... | collective-permute-start | bytes 786440 | tf_op jit(solution)/shard_map/ppermute | solution.py:247
  78.3 6.6 %collective-permute-start.4 = (bf16[64,1024]{1,0:T(8,128)(2,1)S(1)}, bf16[64,1024]{1,0:T(8,128)(2,1)S(1)}, u32[]{:S(2)}, u32[]{:S(2)}) collective-permute-start(bf16[64,1024]{1,0:T(8,128)(2,1)S(1)} %shard_map.61.mine), channel_id=1, source_target_pairs={{496,0},{20,4},{504,8},{28,12},{0,16},{36,20},{8,24},{44,28},{16,3... | collective-permute-start | bytes 393224 | tf_op jit(solution)/shard_map/ppermute | solution.py:243
  82.5 3.2 %collective-permute-start.6 = (bf16[64,1024]{1,0:T(8,128)(2,1)S(1)}, bf16[64,1024]{1,0:T(8,128)(2,1)S(1)}, u32[]{:S(2)}, u32[]{:S(2)}) collective-permute-start(bf16[64,1024]{1,0:T(8,128)(2,1)S(1)} %collective-permute-done.5.refs_5_), channel_id=1, source_target_pairs={{0,4},{4,0},{1,5},{5,1},{2,6},{6,2},{3,7},{7,3},{8,12},{12,8},{9,1... | collective-permute-start | bytes 393224 | tf_op jit(solution)/shard_map/ppermute | solution.py:247
